TPU v7x, 512 devices: a whole 4x4x16 slice. The times are simulated.
512 devices in a mesh: ctx: 32 (over x, z_lo, core), tp: 16 (over y, z_hi).
Axes of the slice: x: 4, y: 4, z: 16 (z_hi: 4, z_lo: 4; z = z_hi * 4 + z_lo), core: 2. Of those that a mesh axis runs over, the one named last changes fastest.
Arguments:
- attention_out: bfloat16 [512, 8192], P('ctx', 'tp'), may hold values from -6 to 6
- w_out: bfloat16 [8192, 8192], P('tp', 'ctx'), may hold values from -0.0625 to 0.0625
- residual: bfloat16 [512, 8192], P(('ctx', 'tp')), may hold values from -6 to 6
- norm_gain: float32 [8192], replicated, may hold values from 0.1 to 1.9
- w_gate: bfloat16 [28672, 8192], P(('ctx', 'tp')), may hold values from -0.0625 to 0.0625
- w_up: bfloat16 [28672, 8192], P(('ctx', 'tp')), may hold values from -0.0625 to 0.0625
- w_down: bfloat16 [32, 896, 8192], P(None, 'tp', 'ctx'), may hold values from -0.03125 to 0.03125
Outputs:
- mixed: bfloat16 [512, 8192], P(('ctx', 'tp'))
All inputs are finite; a program needn't handle non-finite values.
Results may differ from a plain program's by a relative error of at most 0.02.
Values may be sent and summed in bfloat16 or wider, within the bound.
No kernel may reach another device: no remote copies, remote signals or barrier semaphores. Data moves between devices by JAX's collectives and lax.ppermute only.
A program may use at most 64 MiB of HBM per device.

v0:
```python
import jax
import jax.numpy as jnp
from jax import lax
from jax.sharding import PartitionSpec as P


def owner_order(partial_value, ctx_count, tp_count, row_count):
    col_count = partial_value.shape[1]
    grouped = partial_value.reshape(ctx_count, tp_count, row_count, col_count)
    return jnp.transpose(grouped, (1, 0, 2, 3)).reshape(tp_count * ctx_count * row_count, col_count)


def shards(attention_out, w_out, residual, norm_gain, w_gate, w_up, w_down):
    row_count = residual.shape[0]
    ctx_count = lax.axis_size("ctx")
    tp_count = lax.axis_size("tp")
    unit_count = w_gate.shape[0]
    col_count = w_down.shape[2]
    partial_value = jnp.dot(
        lax.all_gather(attention_out, "ctx", axis=0, tiled=True),
        w_out,
        preferred_element_type=jnp.float32,
    )
    summed = lax.psum_scatter(
        owner_order(partial_value, ctx_count, tp_count, row_count).astype(jnp.bfloat16),
        "tp",
        scatter_dimension=0,
        tiled=True,
    ).astype(jnp.float32)
    proj = lax.all_to_all(
        summed.astype(jnp.bfloat16), "ctx", split_axis=0, concat_axis=1, tiled=True
    ).astype(summed.dtype)
    carried = residual.astype(jnp.float32) + proj
    mean_square = jnp.mean(carried * carried, axis=-1, keepdims=True)
    normed = (carried * lax.rsqrt(mean_square + 1e-05) * norm_gain).astype(jnp.bfloat16)
    paired = jnp.concatenate([w_gate, w_up], axis=0)
    group = lax.all_gather(normed, "tp", axis=0, tiled=True)
    gate_up = lax.dot_general(
        lax.all_gather(group, "ctx", axis=0, tiled=True),
        paired,
        (((1,), (1,)), ((), ())),
        preferred_element_type=jnp.float32,
    )
    gate_part = gate_up[:, :unit_count]
    up_part = gate_up[:, unit_count:]
    hidden = (jax.nn.silu(gate_part) * up_part).astype(jnp.bfloat16)
    flat_down = w_down.reshape(ctx_count * unit_count, col_count)
    partial_down = jnp.dot(
        lax.all_gather(hidden, "ctx", axis=1, tiled=True),
        flat_down,
        preferred_element_type=jnp.float32,
    )
    reduced = lax.psum_scatter(
        owner_order(partial_down, ctx_count, tp_count, row_count).astype(jnp.bfloat16),
        "tp",
        scatter_dimension=0,
        tiled=True,
    ).astype(jnp.float32)
    down = lax.all_to_all(
        reduced.astype(jnp.bfloat16), "ctx", split_axis=0, concat_axis=1, tiled=True
    ).astype(reduced.dtype)
    return (carried + down).astype(jnp.bfloat16)


def solution(mesh):
    in_specs = (
        P("ctx", "tp"),
        P("tp", "ctx"),
        P(("ctx", "tp"), None),
        P(),
        P(("ctx", "tp"), None),
        P(("ctx", "tp"), None),
        P(None, "tp", "ctx"),
    )
    out_specs = P(("ctx", "tp"), None)
    return jax.shard_map(shards, mesh=mesh, in_specs=in_specs, out_specs=out_specs, check_vma=False)
```

profile of v0, /device:TPU:1, one launch (start us, length us, event | category | flops | bytes accessed | tf_op | source)
XLA Modules:
  0.0 513.3 jit_solution(6987445112993718375)
XLA Ops:
  6.5 0.0 copy-start
  6.5 0.0 copy-start.1
  6.5 0.0 copy-start.2
  6.5 0.0 reduce-scatter.3.cloned.1.call-start
  6.5 48.2 %all_gather.12 = bf16[512,512]{1,0:T(8,128)(2,1)S(1)} all-gather(bf16[16,512]{1,0:T(8,128)(2,1)} %param.7), channel_id=1, replica_groups=mesh['ctx'=32,'tp'=16] {'ctx'}, dimensions={0}, use_global_device_ids=true | all-gather | bytes 540672 | tf_op jit(solution)/shard_map/all_gather | solution.py:20
  54.7 0.0 copy-start.3
  54.7 0.0 copy-start.4
  54.7 1.4 convolution_convert_fusion.1
  56.1 0.8 copy.12
  56.9 0.0 reduce-scatter.3.cloned.1.call-update
  56.9 0.0 all-gather.4.cloned.1.call-start
  56.9 108.8 %reduce-scatter.3.cloned.1.call-done = bf16[32,256]{1,0:T(8,128)(2,1)} async-done(((bf16[512,256]{1,0:T(8,128)(2,1)}), bf16[32,256]{1,0:T(8,128)(2,1)}) %reduce-scatter.3.cloned.1.call-update) | async-done | bytes 16400 | tf_op jit(solution)/shard_map/reduce_scatter | solution.py:24
  165.8 0.5 broadcast.4
  166.3 1.4 reduce.1
  167.6 14.4 %all_to_all.26 = bf16[32,2,128]{2,1,0:T(2,128)(2,1)S(1)} all-to-all(bf16[32,2,128]{2,1,0:T(2,128)(2,1)S(1)} %reshape.72), channel_id=1, replica_groups=mesh['ctx'=32,'tp'=16] {'ctx'}, dimensions={0} | all-to-all | bytes 32768 | tf_op jit(solution)/shard_map/all_to_all | solution.py:30
  182.0 0.0 copy-done.1
  182.1 0.7 multiply_reduce_fusion
  183.5 0.0 copy-done.2
  183.5 0.1 convert_bitcast_fusion
  183.6 50.3 %all-gather = bf16[16,1,8192]{2,1,0:T(2,128)(2,1)S(1)} all-gather(bf16[1,1,8192]{2,1,0:T(2,128)(2,1)S(1)} %convert_bitcast_fusion), channel_id=1, replica_groups=mesh['ctx'=32,'tp'=16] {'tp'}, dimensions={0}, use_global_device_ids=true | all-gather | bytes 278528 | tf_op jit(solution)/shard_map/all_gather | solution.py:37
  233.9 1.0 copy.19
  234.9 0.0 all-gather.4.cloned.1.call-update
  234.9 0.0 all-gather.6.cloned.1.call-start
  235.0 71.6 %all-gather.4.cloned.1.call-done = bf16[512,8192]{1,0:T(8,128)(2,1)} async-done(((bf16[16,8192]{1,0:T(8,128)(2,1)}), bf16[512,8192]{1,0:T(8,128)(2,1)}) %all-gather.4.cloned.1.call-update) | async-done | bytes 8388624 | tf_op jit(solution)/shard_map/all_gather | solution.py:39
  306.5 0.0 copy-done.3
  306.5 0.0 copy-done.4
  306.5 6.2 %fusion = f32[512,112]{0,1:T(8,128)S(1)} fusion(bf16[512,8192]{1,0:T(8,128)(2,1)} %all-gather.4.cloned.1.call-done, bf16[56,8192]{1,0:T(8,128)(2,1)S(1)} %copy-done.3, bf16[56,8192]{1,0:T(8,128)(2,1)S(1)} %copy-done.4), kind=kOutput, calls=%fused_computation | convolution fusion | flops 943194112 | bytes 10452992 | tf_op jit(solution)/shard_map/dot_general | solution.py:38
  312.8 0.7 fusion.5
  313.4 0.0 all-gather.6.cloned.1.call-update
  313.5 0.0 reduce-scatter.5.cloned.1.call-start
  313.5 64.0 %all-gather.6.cloned.1.call-done = bf16[512,1792]{0,1:T(8,128)(2,1)} async-done(((bf16[512,56]{0,1:T(8,128)(2,1)}), bf16[512,1792]{0,1:T(8,128)(2,1)}) %all-gather.6.cloned.1.call-update) | async-done | bytes 1835024 | tf_op jit(solution)/shard_map/all_gather | solution.py:49
  377.5 2.8 copy.14
  380.3 0.0 copy-done
  380.3 0.6 fusion.4
  380.9 0.8 copy.15
  381.7 0.0 reduce-scatter.5.cloned.1.call-update
  381.7 108.5 %reduce-scatter.5.cloned.1.call-done = bf16[32,256]{1,0:T(8,128)(2,1)} async-done(((bf16[512,256]{1,0:T(8,128)(2,1)}), bf16[32,256]{1,0:T(8,128)(2,1)}) %reduce-scatter.5.cloned.1.call-update) | async-done | bytes 16400 | tf_op jit(solution)/shard_map/reduce_scatter | solution.py:53
  490.3 1.4 reduce.2
  491.6 14.4 %all_to_all.27 = bf16[32,2,128]{2,1,0:T(2,128)(2,1)S(1)} all-to-all(bf16[32,2,128]{2,1,0:T(2,128)(2,1)S(1)} %reshape.74), channel_id=1, replica_groups=mesh['ctx'=32,'tp'=16] {'ctx'}, dimensions={0} | all-to-all | bytes 32768 | tf_op jit(solution)/shard_map/all_to_all | solution.py:59
  506.1 0.7 fusion.6
  (4 shorter events, 0.1 us)
Async XLA Ops:
  6.5 373.7 %copy-start = (bf16[32,56,256]{2,1,0:T(8,128)(2,1)S(1)}, bf16[32,56,256]{2,1,0:T(8,128)(2,1)}, u32[]{:S(2)}) copy-start(bf16[32,56,256]{2,1,0:T(8,128)(2,1)} %param.13) | copy-start | bytes 2752516
  6.5 175.5 %copy-start.1 = (bf16[1,8192]{1,0:T(2,128)(2,1)S(1)}, bf16[1,8192]{1,0:T(2,128)(2,1)}, u32[]{:S(2)}) copy-start(bf16[1,8192]{1,0:T(2,128)(2,1)} %param.9) | copy-start | bytes 49156
  6.5 176.9 %copy-start.2 = (f32[8192]{0:T(1024)S(1)}, f32[8192]{0:T(1024)}, u32[]{:S(2)}) copy-start(f32[8192]{0:T(1024)} %param.10) | copy-start | bytes 98308
  6.5 159.2 %reduce-scatter.3.cloned.1.call-start = ((), (), s32[]{:S(2)}) async-start(), calls=%async_computation.4 | async-start | bytes 278528 | tf_op jit(solution)/shard_map/reduce_scatter | solution.py:24
  54.7 251.8 %copy-start.3 = (bf16[56,8192]{1,0:T(8,128)(2,1)S(1)}, bf16[56,8192]{1,0:T(8,128)(2,1)}, u32[]{:S(2)}) copy-start(bf16[56,8192]{1,0:T(8,128)(2,1)} %param.12) | copy-start | bytes 2752516
  54.7 251.8 %copy-start.4 = (bf16[56,8192]{1,0:T(8,128)(2,1)S(1)}, bf16[56,8192]{1,0:T(8,128)(2,1)}, u32[]{:S(2)}) copy-start(bf16[56,8192]{1,0:T(8,128)(2,1)} %param.11) | copy-start | bytes 2752516
  56.9 249.6 %all-gather.4.cloned.1.call-start = ((), (), s32[]{:S(2)}) async-start(), calls=%async_computation.5 | async-start | bytes 8650752 | tf_op jit(solution)/shard_map/all_gather | solution.py:39
  234.9 142.6 %all-gather.6.cloned.1.call-start = ((), (), s32[]{:S(2)}) async-start(), calls=%async_computation.6 | async-start | bytes 1892352 | tf_op jit(solution)/shard_map/all_gather | solution.py:49
  313.5 176.8 %reduce-scatter.5.cloned.1.call-start = ((), (), s32[]{:S(2)}) async-start(), calls=%async_computation.7 | async-start | bytes 278528 | tf_op jit(solution)/shard_map/reduce_scatter | solution.py:53
Sparse Core Ops, SparseCore 0:
  57.0 108.6 reduce-scatter.2
  235.0 71.4 all-gather.3
  313.6 63.8 all-gather.5
  381.9 108.2 reduce-scatter.4
where the time goes:
time: 514 us; the launch traced here: 513 us
  waiting for transfers between devices  353 us (69%)
  blocking collectives  127 us (25%)
  between operations  13.9 us (3%)
  matrix products  8.23 us (2%)
  local copies, waits for them, and re-layouts  5.9 us (1%)
    reduce_scatter x1, waiting for transfers between devices, shards(): lax.psum_scatter(owner_order(partial_value, ctx_count, tp_count, row_coun...  109 us
    reduce_scatter x1, waiting for transfers between devices, shards(): lax.psum_scatter(owner_order(partial_down, ctx_count, tp_count, row_count...  109 us
    all_gather x1, waiting for transfers between devices, shards(): lax.all_gather(group, 'ctx', axis=0, tiled=True)  71.6 us
    all_gather x1, waiting for transfers between devices, shards(): lax.all_gather(hidden, 'ctx', axis=1, tiled=True)  64 us
    all_gather x1, blocking collectives, shards(): group = lax.all_gather(normed, 'tp', axis=0, tiled=True)  50.3 us
    all_gather x1, blocking collectives, shards(): lax.all_gather(attention_out, 'ctx', axis=0, tiled=True)  48.2 us
    all_to_all x1, blocking collectives, shards(): lax.all_to_all(reduced.astype(jnp.bfloat16), 'ctx', split_axis=0, concat_...  14.4 us
    all_to_all x1, blocking collectives, shards(): lax.all_to_all(summed.astype(jnp.bfloat16), 'ctx', split_axis=0, concat_a...  14.4 us
  transfers between devices with their start and end apart: 4, of which 4 were waited for; matrix products, arithmetic and copies ran while one was open for 0% of the time, Pallas kernels for 0%

commit v1 on v0

v1 whole, which is shorter than its diff:
```python
import jax
import jax.numpy as jnp
from jax import lax
from jax.sharding import Mesh, PartitionSpec as P

F32 = jnp.float32
BF16 = jnp.bfloat16
EPS = 1e-05
X, ZL, Y, ZH = 4, 4, 4, 4
CORES = 2


def exchange(value, axes):
    return lax.all_to_all(value, axes, 0, 0, tiled=True)


def replicate(value, count):
    return lax.optimization_barrier(jnp.broadcast_to(value[None], (count,) + value.shape))


def split_two(value):
    high = value.astype(BF16)
    low = (value - high.astype(F32)).astype(BF16)
    return high, low


def shards(attention_out, w_out, residual, norm_gain, w_gate, w_up, w_down):
    x_at = lax.axis_index("x")
    zl_at = lax.axis_index("zl")
    core_at = lax.axis_index("core")
    y_at = lax.axis_index("y")
    zh_at = lax.axis_index("zh")
    d = residual.shape[1]
    t_rows, heads = attention_out.shape
    cols = w_out.shape[1]
    units = w_gate.shape[0]
    tokens = t_rows * X * ZL * CORES
    chunk = tokens // Y
    ctx_at = (x_at * ZL + zl_at) * CORES + core_at

    def weight_piece(at):
        def take(w):
            return lax.dynamic_index_in_dim(
                w.reshape(units, X, ZL, CORES * cols), at, 2, keepdims=False
            )
        return jnp.concatenate([take(w_gate), take(w_up)], axis=0)

    pieces = [weight_piece(zl_at)]
    for shift in range(1, ZL):
        piece = weight_piece((zl_at + shift) % ZL)
        pieces.append(
            lax.ppermute(piece, "zl", [(i, (i + shift) % ZL) for i in range(ZL)])
        )

    rows = 24
    sent = jnp.concatenate(
        [
            jnp.broadcast_to(attention_out[None], (X * ZL, t_rows, heads)),
            residual.reshape(X * ZL, 1, CORES * cols),
            jnp.zeros((X * ZL, rows - t_rows - 1, heads), BF16),
        ],
        axis=1,
    )
    gathered = exchange(sent, ("x", "zl"))
    gathered = lax.all_gather(gathered, "core", axis=0, tiled=False)
    att = gathered[:, :, :t_rows].reshape(tokens, heads)
    res_pair = gathered[:, :, t_rows].reshape(CORES * X * ZL, CORES, cols)
    res = lax.dynamic_index_in_dim(res_pair, core_at, 1, keepdims=False)

    partial = jnp.dot(att, w_out, preferred_element_type=F32)
    own_t = lax.broadcasted_iota(jnp.int32, (1, t_rows, 1), 1) == y_at * ZH + zh_at
    partial = partial.reshape(CORES * X * ZL, t_rows, cols) + jnp.where(
        own_t, res.astype(F32)[:, None, :], 0.0
    )
    by_y = exchange(partial.astype(BF16).reshape(Y, chunk, cols), "y")
    over_y = jnp.sum(by_y.astype(F32), axis=0).astype(BF16)
    by_zh = exchange(replicate(over_y, ZH), "zh")
    carried = jnp.sum(by_zh.astype(F32), axis=0)

    gain = lax.dynamic_slice_in_dim(norm_gain, ctx_at * cols, cols, 0)
    scaled = (carried * gain[None, :]).astype(BF16)
    square = jnp.sum(carried * carried, axis=1)
    high, low = split_two(square)
    extra = 16
    to_send = jnp.concatenate(
        [
            scaled,
            jnp.concatenate([high, low])[None, :],
            jnp.zeros((extra - 1, cols), BF16),
        ],
        axis=0,
    )
    spread = exchange(replicate(to_send, X * Y), ("x", "y"))
    spread = lax.all_gather(spread, "core", axis=0, tiled=False)
    spread = spread.reshape(CORES, X, Y, chunk + extra, cols)
    values = spread[:, :, :, :chunk]
    squares = spread[:, :, :, chunk].astype(F32).reshape(CORES, X, Y, 2, chunk)
    square_sum = jnp.sum(squares, axis=(0, 1, 3)).reshape(tokens)
    s_high, s_low = split_two(square_sum)

    lhs = jnp.transpose(values, (2, 3, 1, 0, 4)).reshape(tokens, X * CORES * cols)
    pad = 16
    totals = None
    outs = []
    for shift in range(ZL):
        weight = pieces[shift].reshape(2 * units, X * CORES * cols)
        part = lax.dot_general(
            weight, lhs, (((1,), (1,)), ((), ())), preferred_element_type=F32
        ).astype(BF16)
        outs.append(
            jnp.concatenate(
                [part, s_high[None], s_low[None], jnp.zeros((pad - 2, tokens), BF16)], axis=0
            )
        )
    total = outs[0].astype(F32)
    for shift in range(1, ZL):
        got = lax.ppermute(
            outs[shift], "zl", [(i, (i - shift) % ZL) for i in range(ZL)]
        )
        total = total + got.astype(F32)
    mean_square = (total[2 * units] + total[2 * units + 1]) * (1.0 / d)
    scale = lax.rsqrt(mean_square + EPS)[None, :]
    gate = total[:units] * scale
    up = total[units : 2 * units] * scale
    hidden = (jax.nn.silu(gate) * up).astype(BF16)

    hidden = exchange(replicate(hidden, ZL), "zl")
    hidden = exchange(replicate(hidden, X), "x")
    hidden = hidden.reshape(X * ZL, units, tokens)
    hidden = lax.all_gather(hidden, "core", axis=0, tiled=False)
    down_w = w_down.reshape(X * ZL, CORES, units, cols)
    down = None
    for core in range(CORES):
        term = lax.dot_general(
            hidden[core].reshape(X * ZL * units, tokens),
            down_w[:, core].reshape(X * ZL * units, cols),
            (((0,), (0,)), ((), ())),
            preferred_element_type=F32,
        )
        down = term if down is None else down + term
    holds = (lax.broadcasted_iota(jnp.int32, (Y, 1, 1), 0) == y_at) & (zh_at == 0)
    down = down.reshape(Y, chunk, cols) + jnp.where(holds, carried[None], 0.0)
    final = exchange(
        down.astype(BF16).reshape(tokens, cols // 128, 128), ("core", "x", "zl", "y", "zh")
    )
    final = final.reshape(CORES, X * ZL, Y * ZH, cols).astype(F32)
    mixed = jnp.sum(final, axis=2)
    mixed = jnp.transpose(mixed, (1, 0, 2)).reshape(1, d)
    return mixed.astype(BF16)


def solution(mesh):
    view = Mesh(
        mesh.devices.reshape(X, ZL, CORES, Y, ZH), ("x", "zl", "core", "y", "zh")
    )
    ctx = ("x", "zl", "core")
    tp = ("y", "zh")
    in_specs = (
        P(ctx, tp),
        P(tp, ctx),
        P(ctx + tp, None),
        P(),
        P(ctx + tp, None),
        P(ctx + tp, None),
        P(None, tp, ctx),
    )
    return jax.shard_map(
        shards, mesh=view, in_specs=in_specs, out_specs=P(ctx + tp, None), check_vma=False
    )
```

time: 514 us -> 275 us (0.54)
  waiting for transfers between devices: 353 us -> 76.8 us
  starting transfers between devices: 0.13 us -> 51.1 us
  blocking collectives: 127 us -> 98.3 us
  local copies, waits for them, and re-layouts: 5.9 us -> 25.6 us
    reduce_scatter x2 -> x0, waiting for transfers between devices: 217 us -> none  [the longest x1 109 us: shards(): lax.psum_scatter(owner_order(partial_value, ctx_count, tp_count, row_coun...]
    all_gather x2, waiting for transfers between devices: 136 us -> 23.9 us  [the longest x1 23.9 us: shards(): hidden = lax.all_gather(hidden, 'core', axis=0, tiled=False)]
    all_gather x2 -> x1, blocking collectives: 98.5 us -> 3.74 us  [shards(): gathered = lax.all_gather(gathered, 'core', axis=0, tiled=False)]
    all_to_all x2 -> x5, blocking collectives: 28.8 us -> 94.5 us  [exchange(): return lax.all_to_all(value, axes, 0, 0, tiled=True)]
    ppermute x0 -> x6, starting transfers between devices: none -> 30 us  [the longest x3 17.9 us: shards(): lax.ppermute(outs[shift], 'zl', [(i, (i - shift) % ZL) for i in range(ZL)])]
    all_to_all x0 -> x2, waiting for transfers between devices: none -> 26.6 us  [exchange(): return lax.all_to_all(value, axes, 0, 0, tiled=True)]
    ppermute x0 -> x6, waiting for transfers between devices: none -> 26.2 us  [the longest x3 21.8 us: shards(): lax.ppermute(piece, 'zl', [(i, (i + shift) % ZL) for i in range(ZL)])]
    all_to_all x0 -> x2, starting transfers between devices: none -> 21.1 us  [exchange(): return lax.all_to_all(value, axes, 0, 0, tiled=True)]
  transfers between devices with their start and end apart: 4 -> 10, of which waited for: 4 -> 5; matrix products, arithmetic and copies ran while one was open for 0% -> 5% of each run, Pallas kernels for 0% -> 0%
where the time goes in v1:
time: 275 us; the launch traced here: 274 us
  blocking collectives  98.3 us (36%)
  waiting for transfers between devices  76.8 us (28%)
  starting transfers between devices  51.1 us (19%)
  local copies, waits for them, and re-layouts  25.6 us (9%)
  between operations  14 us (5%)
  matrix products  4.51 us (2%)
  other arithmetic  3.63 us (1%)
    all_to_all x5, blocking collectives, exchange(): return lax.all_to_all(value, axes, 0, 0, tiled=True)  94.5 us
    all_to_all x2, waiting for transfers between devices, exchange(): return lax.all_to_all(value, axes, 0, 0, tiled=True)  26.6 us
    all_gather x1, waiting for transfers between devices, shards(): hidden = lax.all_gather(hidden, 'core', axis=0, tiled=False)  23.9 us
    ppermute x3, waiting for transfers between devices, shards(): lax.ppermute(piece, 'zl', [(i, (i + shift) % ZL) for i in range(ZL)])  21.8 us
    all_to_all x2, starting transfers between devices, exchange(): return lax.all_to_all(value, axes, 0, 0, tiled=True)  21.1 us
    ppermute x3, starting transfers between devices, shards(): lax.ppermute(outs[shift], 'zl', [(i, (i - shift) % ZL) for i in range(ZL)])  17.9 us
    ppermute x3, starting transfers between devices, shards(): lax.ppermute(piece, 'zl', [(i, (i + shift) % ZL) for i in range(ZL)])  12.1 us
    dynamic_slice x7, local copies, waits for them, and re-layouts, take(): lax.dynamic_index_in_dim(w.reshape(units, X, ZL, CORES * cols), at, 2, ke...  6.82 us
  transfers between devices with their start and end apart: 10, of which 5 were waited for; matrix products, arithmetic and copies ran while one was open for 5% of the time, Pallas kernels for 0%

profile of v1, /device:TPU:1, one launch (start us, length us, event | category | flops | bytes accessed | tf_op | source)
XLA Modules:
  0.0 273.9 jit_solution(5397267363683698760)
XLA Ops:
  6.6 0.7 broadcast_in_dim.102
  7.4 1.6 maximum_maximum_fusion
  9.0 9.0 %all-to-all-start = ((bf16[16,24,512]{2,1,0:T(8,128)(2,1)}), bf16[16,24,512]{2,1,0:T(8,128)(2,1)S(1)}, u32[]{:S(2)}, u32[]{:S(2)}) async-start(bf16[16,24,512]{2,1,0:T(8,128)(2,1)} %maximum_maximum_fusion), calls=%async_computation | async-start | bytes 786432 | tf_op jit(solution)/shard_map/all_to_all | solution.py:14
  18.1 12.9 %all-to-all-done = bf16[16,24,512]{2,1,0:T(8,128)(2,1)S(1)} async-done(((bf16[16,24,512]{2,1,0:T(8,128)(2,1)}), bf16[16,24,512]{2,1,0:T(8,128)(2,1)S(1)}, u32[]{:S(2)}, u32[]{:S(2)}) %all-to-all-start) | async-done | bytes 393248 | tf_op jit(solution)/shard_map/all_to_all | solution.py:14
  30.9 3.7 %all-gather = bf16[32,24,512]{2,1,0:T(8,128)(2,1)S(1)} all-gather(bf16[16,24,512]{2,1,0:T(8,128)(2,1)S(1)} %all-to-all-done), channel_id=2, replica_groups=mesh['x'=4,'zl'=4,'core'=2,'y'=4,'zh'=4] {'core'}, dimensions={0}, use_global_device_ids=true | all-gather | bytes 1179648 | tf_op jit(solution)/shard_map/all_gather | solution.py:65
  34.7 0.2 slice_reduce_fusion
  35.0 0.3 fusion
  35.3 9.8 %all_to_all.35 = bf16[4,128,256]{2,1,0:T(8,128)(2,1)S(1)} all-to-all(bf16[4,128,256]{2,1,0:T(8,128)(2,1)S(1)} %bitcast.95), channel_id=1, replica_groups=mesh['x'=4,'zl'=4,'core'=2,'y'=4,'zh'=4] {'y'}, dimensions={0} | all-to-all | bytes 524288 | tf_op jit(solution)/shard_map/all_to_all | solution.py:14
  45.1 0.7 broadcast_in_dim.109
  45.8 12.1 %all-to-all-start.2 = ((bf16[4,128,256]{2,1,0:T(8,128)(2,1)}), bf16[4,128,256]{2,1,0:T(8,128)(2,1)S(1)}, u32[]{:S(2)}, u32[]{:S(2)}) async-start(bf16[4,128,256]{2,1,0:T(8,128)(2,1)} %broadcast_in_dim.109), calls=%async_computation.2 | async-start | bytes 524288 | tf_op jit(solution)/shard_map/all_to_all | solution.py:14
  58.0 0.8 dynamic_slice.35
  58.8 13.8 %all-to-all-done.2 = bf16[4,128,256]{2,1,0:T(8,128)(2,1)S(1)} async-done(((bf16[4,128,256]{2,1,0:T(8,128)(2,1)}), bf16[4,128,256]{2,1,0:T(8,128)(2,1)S(1)}, u32[]{:S(2)}, u32[]{:S(2)}) %all-to-all-start.2) | async-done | bytes 262176 | tf_op jit(solution)/shard_map/all_to_all | solution.py:14
  72.9 17.8 %all_to_all.36 = bf16[16,144,256]{2,1,0:T(8,128)(2,1)} all-to-all(bf16[16,144,256]{2,1,0:T(8,128)(2,1)S(1)} %broadcast_in_dim.112), channel_id=1, replica_groups=mesh['x'=4,'zl'=4,'core'=2,'y'=4,'zh'=4] {'x','y'}, dimensions={0} | all-to-all | bytes 2359296 | tf_op jit(solution)/shard_map/all_to_all | solution.py:14
  90.8 0.7 reshape.124
  91.5 0.4 copy-done.3
  91.9 0.7 reshape.123
  92.6 6.0 %dynamic-slice_reduce_fusion = (bf16[56,4,512]{2,1,0:T(4,128)(2,1)S(1)}, bf16[56,4,1,512]{3,2,1,0:T(2,128)(2,1)S(1)}, bf16[56,4,1,512]{3,2,1,0:T(2,128)(2,1)S(1)...) fusion(bf16[56,4,4,512]{3,2,1,0:T(4,128)(2,1)S(1)} %reshape.124, ...), kind=kLoop, calls=%fused_computation.18 | loop fusion | bytes 3670032 | tf_op jit(solution)/shard_map/jit(dynamic_index_in_dim)/dynamic_slice | solution.py:43
  98.9 6.0 %collective-permute-start = (bf16[112,4,512]{2,0,1:T(8,128)(2,1)S(1)}, bf16[112,4,512]{2,0,1:T(8,128)(2,1)S(1)}, u32[]{:S(2)}, u32[]{:S(2)}) collective-permute-start(bf16[112,4,512]{2,0,1:T(8,128)(2,1)S(1)} %pad_maximum_fusion), channel_id=1, source_target_pairs={{0,32},{32,64},{64,96},{96,0},{1,33},{33,65},{65,97},{97,1},{2,34}... | collective-permute-start | bytes 1376264 | tf_op jit(solution)/shard_map/ppermute | solution.py:52
  105.2 1.9 collective-permute-start.2
  107.5 4.2 %collective-permute-start.4 = (bf16[112,4,512]{2,0,1:T(8,128)(2,1)S(1)}, bf16[112,4,512]{2,0,1:T(8,128)(2,1)S(1)}, u32[]{:S(2)}, u32[]{:S(2)}) collective-permute-start(bf16[112,4,512]{2,0,1:T(8,128)(2,1)S(1)} %pad_maximum_fusion.2), channel_id=1, source_target_pairs={{0,96},{32,0},{64,32},{96,64},{1,97},{33,1},{65,33},{97,65},{2,98}... | collective-permute-start | bytes 1376264 | tf_op jit(solution)/shard_map/ppermute | solution.py:52
  111.7 0.7 copy.127
  112.5 0.7 copy.126
  113.2 21.8 %collective-permute-done.2 = bf16[112,4,512]{2,0,1:T(8,128)(2,1)S(1)} collective-permute-done((bf16[112,4,512]{2,0,1:T(8,128)(2,1)S(1)}, bf16[112,4,512]{2,0,1:T(8,128)(2,1)S(1)}, u32[]{:S(2)}, u32[]{:S(2)}) %collective-permute-start.2) | collective-permute-done | bytes 458784 | tf_op jit(solution)/shard_map/ppermute | solution.py:52
  135.1 0.8 copy.125
  135.9 0.9 fusion.13
  136.9 1.7 slice_bitcast_fusion
  138.6 3.5 %copy.107 = bf16[4,128,4,2,256]{4,3,2,1,0:T(2,128)(2,1)} copy(bf16[4,128,4,2,256]{4,1,0,2,3:T(8,128)(2,1)S(1)} %slice_bitcast_fusion) | data formatting | bytes 4194304 | tf_op jit(solution)/shard_map/transpose | solution.py:101
  142.1 3.3 %reshape.128 = bf16[512,2048]{1,0:T(8,128)(2,1)S(1)} reshape(bf16[4,128,4,2,256]{4,3,2,1,0:T(2,128)(2,1)} %copy.107) | data formatting | bytes 4194304 | tf_op jit(solution)/shard_map/reshape | solution.py:101
  145.4 0.8 convolution_convert_fusion.2
  146.2 0.8 convolution_convert_fusion.1
  147.1 0.8 convolution_convert_fusion
  148.0 12.0 %collective-permute-start.5 = (bf16[128,512]{1,0:T(8,128)(2,1)S(1)}, bf16[128,512]{1,0:T(8,128)(2,1)S(1)}, u32[]{:S(2)}, u32[]{:S(2)}) collective-permute-start(bf16[128,512]{1,0:T(8,128)(2,1)S(1)} %get-tuple-element.21), channel_id=1, source_target_pairs={{0,32},{32,64},{64,96},{96,0},{1,33},{33,65},{65,97},{97,1},{2,34}... | collective-permute-start | bytes 393224 | tf_op jit(solution)/shard_map/ppermute | solution.py:117
  160.0 1.9 collective-permute-start.3
  162.0 4.0 %collective-permute-start.1 = (bf16[128,512]{1,0:T(8,128)(2,1)S(1)}, bf16[128,512]{1,0:T(8,128)(2,1)S(1)}, u32[]{:S(2)}, u32[]{:S(2)}) collective-permute-start(bf16[128,512]{1,0:T(8,128)(2,1)S(1)} %get-tuple-element.19), channel_id=1, source_target_pairs={{0,96},{32,0},{64,32},{96,64},{1,97},{33,1},{65,33},{97,65},{2,98}... | collective-permute-start | bytes 393224 | tf_op jit(solution)/shard_map/ppermute | solution.py:117
  166.0 0.8 convolution_convert_fusion.3
  166.8 4.4 %collective-permute-done.3 = bf16[128,512]{1,0:T(8,128)(2,1)S(1)} collective-permute-done((bf16[128,512]{1,0:T(8,128)(2,1)S(1)}, bf16[128,512]{1,0:T(8,128)(2,1)S(1)}, u32[]{:S(2)}, u32[]{:S(2)}) %collective-permute-start.3) | collective-permute-done | bytes 131104 | tf_op jit(solution)/shard_map/ppermute | solution.py:117
  171.5 10.1 %all_to_all.37 = bf16[4,56,512]{2,1,0:T(8,128)(2,1)S(1)} all-to-all(bf16[4,56,512]{2,1,0:T(8,128)(2,1)S(1)} %broadcast_in_dim.113), channel_id=1, replica_groups=mesh['x'=4,'zl'=4,'core'=2,'y'=4,'zh'=4] {'zl'}, dimensions={0} | all-to-all | bytes 458752 | tf_op jit(solution)/shard_map/all_to_all | solution.py:14
  181.7 13.6 %all_to_all.38 = bf16[4,4,56,512]{3,2,1,0:T(8,128)(2,1)} all-to-all(bf16[4,4,56,512]{3,2,1,0:T(8,128)(2,1)S(1)} %broadcast_in_dim.114), channel_id=1, replica_groups=mesh['x'=4,'zl'=4,'core'=2,'y'=4,'zh'=4] {'x'}, dimensions={0} | all-to-all | bytes 1835008 | tf_op jit(solution)/shard_map/all_to_all | solution.py:14
  195.5 0.3 broadcast_in_dim.119
  195.8 23.9 %all-gather.5.cloned.1.call-done = bf16[2,16,56,512]{3,2,1,0:T(8,128)(2,1)} async-done(((bf16[1,16,56,512]{3,2,1,0:T(8,128)(2,1)}), bf16[2,16,56,512]{3,2,1,0:T(8,128)(2,1)}) %all-gather.5.cloned.1.call-update) | async-done | bytes 1835024 | tf_op jit(solution)/shard_map/all_gather | solution.py:130
  219.7 1.6 fusion.16
  221.3 0.5 fusion.19
  221.7 0.5 convolution_add_fusion
  222.2 0.2 copy.118
  222.6 0.3 copy.119
  222.9 43.2 %all_to_all.39 = bf16[512,2,128]{2,1,0:T(2,128)(2,1)S(1)} all-to-all(bf16[512,2,128]{2,1,0:T(2,128)(2,1)S(1)} %copy.119), channel_id=1, replica_groups=mesh['x'=4,'zl'=4,'core'=2,'y'=4,'zh'=4] {'core','x','zl','y','zh'}, dimensions={0} | all-to-all | bytes 524288 | tf_op jit(solution)/shard_map/all_to_all | solution.py:14
  266.1 0.2 convert_element_type.135
  266.4 0.6 convert_element_type.139
  (68 shorter events, 2.7 us)
Async XLA Ops:
  6.5 28.4 %copy-start = (bf16[512,256]{1,0:T(8,128)(2,1)S(1)}, bf16[512,256]{1,0:T(8,128)(2,1)}, u32[]{:S(2)}) copy-start(bf16[512,256]{1,0:T(8,128)(2,1)} %param.8) | copy-start | bytes 786436
  9.0 21.9 %all-to-all-start = ((bf16[16,24,512]{2,1,0:T(8,128)(2,1)}), bf16[16,24,512]{2,1,0:T(8,128)(2,1)S(1)}, u32[]{:S(2)}, u32[]{:S(2)}) async-start(bf16[16,24,512]{2,1,0:T(8,128)(2,1)} %maximum_maximum_fusion), calls=%async_computation | async-start | bytes 786432 | tf_op jit(solution)/shard_map/all_to_all | solution.py:14
  45.8 26.7 %all-to-all-start.2 = ((bf16[4,128,256]{2,1,0:T(8,128)(2,1)}), bf16[4,128,256]{2,1,0:T(8,128)(2,1)S(1)}, u32[]{:S(2)}, u32[]{:S(2)}) async-start(bf16[4,128,256]{2,1,0:T(8,128)(2,1)} %broadcast_in_dim.109), calls=%async_computation.2 | async-start | bytes 524288 | tf_op jit(solution)/shard_map/all_to_all | solution.py:14
  57.9 78.0 %all-gather.7.cloned.1.call-start = ((), (), s32[]{:S(2)}) async-start(), calls=%async_computation.8 | async-start | bytes 3538944 | tf_op jit(solution)/shard_map/all_gather | solution.py:94
  72.9 17.9 %copy-start.2 = (bf16[56,8192]{1,0:T(8,128)(2,1)S(1)}, bf16[56,8192]{1,0:T(8,128)(2,1)}, u32[]{:S(2)}) copy-start(bf16[56,8192]{1,0:T(8,128)(2,1)} %param.12) | copy-start | bytes 2752516
  90.7 1.2 copy-start.3
  90.7 128.9 %all-gather.5.cloned.1.call-start = ((), (), s32[]{:S(2)}) async-start(), calls=%async_computation.7 | async-start | bytes 2752512 | tf_op jit(solution)/shard_map/all_gather | solution.py:130
  98.9 14.3 %collective-permute-start = (bf16[112,4,512]{2,0,1:T(8,128)(2,1)S(1)}, bf16[112,4,512]{2,0,1:T(8,128)(2,1)S(1)}, u32[]{:S(2)}, u32[]{:S(2)}) collective-permute-start(bf16[112,4,512]{2,0,1:T(8,128)(2,1)S(1)} %pad_maximum_fusion), channel_id=1, source_target_pairs={{0,32},{32,64},{64,96},{96,0},{1,33},{33,65},{65,97},{97,1},{2,34}... | collective-permute-start | bytes 1376264 | tf_op jit(solution)/shard_map/ppermute | solution.py:52
  105.2 29.8 %collective-permute-start.2 = (bf16[112,4,512]{2,0,1:T(8,128)(2,1)S(1)}, bf16[112,4,512]{2,0,1:T(8,128)(2,1)S(1)}, u32[]{:S(2)}, u32[]{:S(2)}) collective-permute-start(bf16[112,4,512]{2,0,1:T(8,128)(2,1)S(1)} %pad_maximum_fusion.1), channel_id=1, source_target_pairs={{0,64},{32,96},{64,0},{96,32},{1,65},{33,97},{65,1},{97,33},{2,66}... | collective-permute-start | bytes 1376264 | tf_op jit(solution)/shard_map/ppermute | solution.py:52
  107.5 27.6 %collective-permute-start.4 = (bf16[112,4,512]{2,0,1:T(8,128)(2,1)S(1)}, bf16[112,4,512]{2,0,1:T(8,128)(2,1)S(1)}, u32[]{:S(2)}, u32[]{:S(2)}) collective-permute-start(bf16[112,4,512]{2,0,1:T(8,128)(2,1)S(1)} %pad_maximum_fusion.2), channel_id=1, source_target_pairs={{0,96},{32,0},{64,32},{96,64},{1,97},{33,1},{65,33},{97,65},{2,98}... | collective-permute-start | bytes 1376264 | tf_op jit(solution)/shard_map/ppermute | solution.py:52
  145.4 1.7 copy-start.1
  147.1 18.9 %copy-start.5 = (bf16[7,8,4,512]{3,1,2,0:T(8,128)(2,1)S(1)}, bf16[7,8,4,512]{3,1,2,0:T(8,128)(2,1)}, u32[]{:S(2)}) copy-start(bf16[7,8,4,512]{3,1,2,0:T(8,128)(2,1)} %copy.127) | copy-start | bytes 688132
  147.1 18.9 %copy-start.6 = (bf16[7,8,4,512]{3,1,2,0:T(8,128)(2,1)S(1)}, bf16[7,8,4,512]{3,1,2,0:T(8,128)(2,1)}, u32[]{:S(2)}) copy-start(bf16[7,8,4,512]{3,1,2,0:T(8,128)(2,1)} %copy.126) | copy-start | bytes 688132
  148.0 18.7 %collective-permute-start.5 = (bf16[128,512]{1,0:T(8,128)(2,1)S(1)}, bf16[128,512]{1,0:T(8,128)(2,1)S(1)}, u32[]{:S(2)}, u32[]{:S(2)}) collective-permute-start(bf16[128,512]{1,0:T(8,128)(2,1)S(1)} %get-tuple-element.21), channel_id=1, source_target_pairs={{0,32},{32,64},{64,96},{96,0},{1,33},{33,65},{65,97},{97,1},{2,34}... | collective-permute-start | bytes 393224 | tf_op jit(solution)/shard_map/ppermute | solution.py:117
  160.0 11.2 %collective-permute-start.3 = (bf16[128,512]{1,0:T(8,128)(2,1)S(1)}, bf16[128,512]{1,0:T(8,128)(2,1)S(1)}, u32[]{:S(2)}, u32[]{:S(2)}) collective-permute-start(bf16[128,512]{1,0:T(8,128)(2,1)S(1)} %get-tuple-element.20), channel_id=1, source_target_pairs={{0,64},{32,96},{64,0},{96,32},{1,65},{33,97},{65,1},{97,33},{2,66}... | collective-permute-start | bytes 393224 | tf_op jit(solution)/shard_map/ppermute | solution.py:117
  162.0 9.3 %collective-permute-start.1 = (bf16[128,512]{1,0:T(8,128)(2,1)S(1)}, bf16[128,512]{1,0:T(8,128)(2,1)S(1)}, u32[]{:S(2)}, u32[]{:S(2)}) collective-permute-start(bf16[128,512]{1,0:T(8,128)(2,1)S(1)} %get-tuple-element.19), channel_id=1, source_target_pairs={{0,96},{32,0},{64,32},{96,64},{1,97},{33,1},{65,33},{97,65},{2,98}... | collective-permute-start | bytes 393224 | tf_op jit(solution)/shard_map/ppermute | solution.py:117
  171.5 23.9 %copy-start.4 = (bf16[32,56,256]{2,1,0:T(8,128)(2,1)S(1)}, bf16[32,56,256]{2,1,0:T(8,128)(2,1)}, u32[]{:S(2)}) copy-start(bf16[32,56,256]{2,1,0:T(8,128)(2,1)} %param.13) | copy-start | bytes 2752516
Sparse Core Ops, SparseCore 0:
  90.9 21.9 all-gather.6
  195.4 24.2 all-gather.4

commit v2 on v0

v2 whole, which is shorter than its diff:
```python
import jax
import jax.numpy as jnp
from jax import lax
from jax.experimental import pallas as pl
from jax.experimental.pallas import tpu as pltpu
from jax.sharding import Mesh, PartitionSpec as P

F32 = jnp.float32
BF16 = jnp.bfloat16
EPS = 1e-05
X, ZL, Y, ZH = 4, 4, 4, 4
CORES = 2
EXTRA = 16


def exchange(value, axes):
    return lax.all_to_all(value, axes, 0, 0, tiled=True)


def replicate(value, count):
    return lax.optimization_barrier(jnp.broadcast_to(value[None], (count,) + value.shape))


def swap_cores(value):
    return lax.ppermute(value, "core", [(0, 1), (1, 0)])


def shift_y(value, shift):
    return lax.ppermute(value, "y", [(i, (i + shift) % Y) for i in range(Y)])


def vmem():
    return pl.BlockSpec(memory_space=pltpu.VMEM)


def smem():
    return pl.BlockSpec(memory_space=pltpu.SMEM)


def pack_rows(attention_out, residual):
    t_rows, heads = attention_out.shape
    wide = residual.shape[1] // (X * ZL)
    rows = 24

    def kernel(att_ref, res_ref, sent_ref):
        for to in range(X * ZL):
            sent_ref[to, :t_rows, :] = att_ref[...]
            sent_ref[to, t_rows:, :] = jnp.zeros((rows - t_rows, heads), BF16)
            sent_ref[to, t_rows : t_rows + 1, :] = res_ref[:, to * wide : (to + 1) * wide]

    return pl.pallas_call(
        kernel,
        out_shape=jax.ShapeDtypeStruct((X * ZL, rows, heads), BF16),
        in_specs=[vmem(), vmem()],
        out_specs=vmem(),
        compiler_params=pltpu.CompilerParams(vmem_limit_bytes=4 * 1024 * 1024),
        name="pack_rows",
    )(attention_out, residual)


def cut_weights(w_gate, w_up, norm_gain, y_at):
    units, d = w_gate.shape
    blocks = X * ZL
    wide = d // blocks
    part = wide // Y

    def kernel(at_ref, gate_ref, up_ref, gain_ref, *piece_refs):
        for shift in range(Y):
            to = lax.rem(at_ref[0] + shift, Y)
            for block in range(blocks):
                place = pl.ds(pl.multiple_of(block * wide + to * part, part), part)
                gain = gain_ref[:, place]
                both = jnp.concatenate(
                    [gate_ref[:, place].astype(F32) * gain, up_ref[:, place].astype(F32) * gain],
                    axis=0,
                )
                piece_refs[shift][:, block * part : (block + 1) * part] = both.astype(BF16)

    return pl.pallas_call(
        kernel,
        out_shape=[jax.ShapeDtypeStruct((2 * units, blocks * part), BF16)] * Y,
        in_specs=[smem(), vmem(), vmem(), vmem()],
        out_specs=[vmem()] * Y,
        compiler_params=pltpu.CompilerParams(vmem_limit_bytes=12 * 1024 * 1024),
        name="cut_weights",
    )(y_at.reshape(1), w_gate, w_up, norm_gain.reshape(1, d))


def sum_and_replicate(parts, count):
    pieces, rows, width = parts.shape

    def kernel(parts_ref, out_ref):
        total = parts_ref[0].astype(F32)
        for piece in range(1, pieces):
            total = total + parts_ref[piece].astype(F32)
        for to in range(count):
            out_ref[to] = total.astype(BF16)

    return pl.pallas_call(
        kernel,
        out_shape=jax.ShapeDtypeStruct((count, rows, width), BF16),
        in_specs=[vmem()],
        out_specs=vmem(),
        compiler_params=pltpu.CompilerParams(vmem_limit_bytes=4 * 1024 * 1024),
        name="sum_and_replicate",
    )(parts)


def carried_and_squares(parts, count):
    pieces, rows, width = parts.shape

    def kernel(parts_ref, out_ref):
        total = parts_ref[0].astype(F32)
        for piece in range(1, pieces):
            total = total + parts_ref[piece].astype(F32)
        square = jnp.sum(total * total, axis=0, keepdims=True)
        high = square.astype(BF16).astype(F32)
        tail = jnp.concatenate(
            [high, square - high, jnp.zeros((EXTRA - 2, width), F32)], axis=0
        ).astype(BF16)
        for to in range(count):
            out_ref[to, :rows, :] = total.astype(BF16)
            out_ref[to, rows:, :] = tail

    return pl.pallas_call(
        kernel,
        out_shape=jax.ShapeDtypeStruct((count, rows + EXTRA, width), BF16),
        in_specs=[vmem()],
        out_specs=vmem(),
        compiler_params=pltpu.CompilerParams(vmem_limit_bytes=4 * 1024 * 1024),
        name="carried_and_squares",
    )(parts)


def activate(parts, d, count):
    pieces, rows, tokens = parts.shape
    units = (rows - EXTRA) // 2

    def kernel(parts_ref, out_ref):
        total = parts_ref[0].astype(F32)
        for piece in range(1, pieces):
            total = total + parts_ref[piece].astype(F32)
        square = total[2 * units : 2 * units + 1] + total[2 * units + 1 : 2 * units + 2]
        scale = lax.rsqrt(square * (1.0 / d) + EPS)
        gate = total[:units] * scale
        up = total[units : 2 * units] * scale
        hidden = (gate / (1.0 + jnp.exp(-gate)) * up).astype(BF16)
        for to in range(count):
            out_ref[to] = hidden

    return pl.pallas_call(
        kernel,
        out_shape=jax.ShapeDtypeStruct((count, units, tokens), BF16),
        in_specs=[vmem()],
        out_specs=vmem(),
        compiler_params=pltpu.CompilerParams(vmem_limit_bytes=4 * 1024 * 1024),
        name="activate",
    )(parts)


def gate_up(own, other, pieces, at):
    blocks, rows, half = own.shape
    part = rows - EXTRA
    both, depth = pieces[0].shape

    def kernel(at_ref, own_ref, other_ref, *rest):
        piece_refs, out_ref, carried_ref = rest[:Y], rest[Y], rest[Y + 1]
        weights, rhs, tails, sem = rest[Y + 2 :]
        y, core, mine = at_ref[0], at_ref[1], at_ref[2]
        copies = []
        for shift in range(Y):
            to = lax.rem(y - shift + Y, Y)
            place = pl.ds(pl.multiple_of(to * both, both), both)
            copies.append(
                pltpu.make_async_copy(piece_refs[shift], weights.at[place, :], sem.at[shift])
            )
        for copy in copies:
            copy.start()
        for turn, ref in enumerate((own_ref, other_ref)):
            side = core if turn == 0 else 1 - core
            place = pl.ds(pl.multiple_of(side * half, half), half)
            square = jnp.zeros((2, half), F32)
            for block in range(blocks):
                rhs[block * part : (block + 1) * part, place] = ref[block, :part, :]
                square = square + ref[block, part : part + 2, :].astype(F32)
            square = square[0:1] + square[1:2]
            high = square.astype(BF16).astype(F32)
            tails[:, place] = jnp.concatenate(
                [high, square - high, jnp.zeros((EXTRA - 2, half), F32)], axis=0
            ).astype(BF16)
            carried_ref[:, place] = ref[mine, :part, :]
        for copy in copies:
            copy.wait()
        total = jnp.dot(weights[...], rhs[...], preferred_element_type=F32)
        for to in range(Y):
            out_ref[to, :both, :] = total[to * both : (to + 1) * both].astype(BF16)
            out_ref[to, both:, :] = tails[...]

    return pl.pallas_call(
        kernel,
        out_shape=[
            jax.ShapeDtypeStruct((Y, both + EXTRA, CORES * half), BF16),
            jax.ShapeDtypeStruct((part, CORES * half), BF16),
        ],
        in_specs=[smem(), vmem(), vmem()] + [pl.BlockSpec(memory_space=pltpu.HBM)] * Y,
        out_specs=[vmem(), vmem()],
        scratch_shapes=[
            pltpu.VMEM((Y * both, depth), BF16),
            pltpu.VMEM((depth, CORES * half), BF16),
            pltpu.VMEM((EXTRA, CORES * half), BF16),
            pltpu.SemaphoreType.DMA((Y,)),
        ],
        compiler_params=pltpu.CompilerParams(vmem_limit_bytes=8 * 1024 * 1024),
        name="gate_up",
    )(at, own, other, *pieces)


def shards(attention_out, w_out, residual, norm_gain, w_gate, w_up, w_down):
    x_at = lax.axis_index("x")
    zl_at = lax.axis_index("zl")
    core_at = lax.axis_index("core")
    y_at = lax.axis_index("y")
    zh_at = lax.axis_index("zh")
    d = residual.shape[1]
    t_rows, heads = attention_out.shape
    cols = w_out.shape[1]
    units = w_gate.shape[0]
    blocks = X * ZL
    half = t_rows * blocks
    tokens = half * CORES
    part = CORES * cols // Y

    cut = cut_weights(w_gate, w_up, norm_gain, y_at)
    first_piece, third_piece = shift_y(cut[1], 1), shift_y(cut[3], 3)
    w_other = swap_cores(w_out)
    first = core_at == 0
    w_pair = jnp.concatenate(
        [jnp.where(first, w_out, w_other), jnp.where(first, w_other, w_out)], axis=1
    )

    got = exchange(pack_rows(attention_out, residual), ("x", "zl"))
    att = got[:, :t_rows].reshape(half, heads)
    res = got[:, t_rows]
    token = lax.broadcasted_iota(jnp.int32, (blocks, half), 1)
    source = lax.broadcasted_iota(jnp.int32, (blocks, half), 0)
    place = (token == source * t_rows + (y_at * ZH + zh_at)).astype(BF16)
    partial = lax.dot_general(
        w_pair, att, (((0,), (1,)), ((), ())), preferred_element_type=F32
    ) + lax.dot_general(res, place, (((0,), (0,)), ((), ())), preferred_element_type=F32)
    partial = partial.astype(BF16).reshape(Y, part, half)
    partial, first_piece, third_piece, cut = lax.optimization_barrier(
        (partial, first_piece, third_piece, cut)
    )
    by_y = exchange(partial, "y")
    over_y, cut = lax.optimization_barrier((sum_and_replicate(by_y, ZH), cut))
    second_piece = shift_y(cut[2], 2)
    by_zh = exchange(over_y, "zh")
    by_zh, second_piece = lax.optimization_barrier((by_zh, second_piece))
    pieces = [cut[0], first_piece, second_piece, third_piece]
    spread = exchange(carried_and_squares(by_zh, ZL), "zl")
    spread = exchange(replicate(spread, X), "x")
    spread = spread.reshape(blocks, part + EXTRA, half)
    outs, kept = gate_up(
        spread,
        swap_cores(spread),
        pieces,
        jnp.stack([y_at, core_at, x_at * ZL + zl_at]),
    )
    hidden = exchange(activate(exchange(outs, "y"), d, ZL), "zl")
    hidden = exchange(replicate(hidden, X), "x")
    hidden = hidden.reshape(blocks, units, tokens)
    hidden_pair = (hidden, swap_cores(hidden))
    down_w = w_down.reshape(blocks, CORES, units, cols)
    feature = lax.broadcasted_iota(jnp.int32, (part, cols), 0)
    column = lax.broadcasted_iota(jnp.int32, (part, cols), 1)
    adds = (y_at // 2 == core_at) & (zh_at == 0)
    keep = ((column == feature + (y_at % 2) * part) & adds).astype(BF16)
    down = lax.dot_general(kept, keep, (((0,), (0,)), ((), ())), preferred_element_type=F32)
    for turn in range(CORES):
        side = core_at if turn == 0 else 1 - core_at
        down = down + lax.dot_general(
            hidden_pair[turn].reshape(blocks * units, tokens),
            lax.dynamic_index_in_dim(down_w, side, 1, keepdims=False).reshape(
                blocks * units, cols
            ),
            (((0,), (0,)), ((), ())),
            preferred_element_type=F32,
        )
    by_owner = jnp.transpose(
        down.astype(BF16).reshape(CORES, X, ZL, Y, ZH, cols), (1, 3, 0, 2, 4, 5)
    ).reshape(X * Y, CORES * ZL * ZH, cols)
    near = exchange(by_owner, ("x", "y")).reshape(X, Y, CORES * ZL * ZH, cols)
    near = jnp.sum(near.astype(F32), axis=1).astype(BF16)
    near = jnp.transpose(near, (1, 0, 2)).reshape(CORES * ZL * ZH, X * cols // 128, 128)
    final = exchange(near, ("core", "zl", "zh"))
    final = final.reshape(CORES, ZL, ZH, X, cols).astype(F32)
    mixed = jnp.sum(final, axis=2)
    mixed = jnp.transpose(mixed, (2, 1, 0, 3)).reshape(1, d)
    return mixed.astype(BF16)


def solution(mesh):
    view = Mesh(
        mesh.devices.reshape(X, ZL, CORES, Y, ZH), ("x", "zl", "core", "y", "zh")
    )
    ctx = ("x", "zl", "core")
    tp = ("y", "zh")
    in_specs = (
        P(ctx, tp),
        P(tp, ctx),
        P(ctx + tp, None),
        P(),
        P(ctx + tp, None),
        P(ctx + tp, None),
        P(None, tp, ctx),
    )
    return jax.shard_map(
        shards, mesh=view, in_specs=in_specs, out_specs=P(ctx + tp, None), check_vma=False
    )
```

time: 514 us -> 193 us (0.38)
  waiting for transfers between devices: 353 us -> 20.1 us
  starting transfers between devices: 0.13 us -> 48.3 us
  blocking collectives: 127 us -> 104 us
  between operations: 13.9 us -> 0.33 us
  Pallas kernels: 0 us -> 5.2 us
    reduce_scatter x2 -> x0, waiting for transfers between devices: 217 us -> none  [the longest x1 109 us: shards(): lax.psum_scatter(owner_order(partial_value, ctx_count, tp_count, row_coun...]
    all_gather x2 -> x0, waiting for transfers between devices: 136 us -> none  [the longest x1 71.6 us: shards(): lax.all_gather(group, 'ctx', axis=0, tiled=True)]
    all_gather x2 -> x0, blocking collectives: 98.5 us -> none  [the longest x1 50.3 us: shards(): group = lax.all_gather(normed, 'tp', axis=0, tiled=True)]
    all_to_all x2 -> x8, blocking collectives: 28.8 us -> 104 us  [exchange(): return lax.all_to_all(value, axes, 0, 0, tiled=True)]
    ppermute x0 -> x6, starting transfers between devices: none -> 28.1 us  [the longest x3 18.9 us: swap_cores(): return lax.ppermute(value, 'core', [(0, 1), (1, 0)])]
    all_to_all x0 -> x2, starting transfers between devices: none -> 20.2 us  [exchange(): return lax.all_to_all(value, axes, 0, 0, tiled=True)]
    ppermute x0 -> x6, waiting for transfers between devices: none -> 18.2 us  [the longest x3 14.2 us: shift_y(): return lax.ppermute(value, 'y', [(i, (i + shift) % Y) for i in range(Y)])]
    pallas_call x0 -> x6, Pallas kernels: none -> 5.2 us  [the longest x1 2.99 us: gate_up(): pl.pallas_call(kernel, out_shape=[jax.ShapeDtypeStruct((Y, both + EXTRA,...]
  transfers between devices with their start and end apart: 4 -> 8, of which waited for: 4 -> 6; matrix products, arithmetic and copies ran while one was open for 0% -> 3% of each run, Pallas kernels for 0% -> 0%
where the time goes in v2:
time: 193 us; the launch traced here: 192 us
  blocking collectives  104 us (54%)
  starting transfers between devices  48.3 us (25%)
  waiting for transfers between devices  20.1 us (10%)
  local copies, waits for them, and re-layouts  7.94 us (4%)
  Pallas kernels  5.2 us (3%)
  matrix products  3.98 us (2%)
  other arithmetic  1.95 us (1%)
    all_to_all x8, blocking collectives, exchange(): return lax.all_to_all(value, axes, 0, 0, tiled=True)  104 us
    all_to_all x2, starting transfers between devices, exchange(): return lax.all_to_all(value, axes, 0, 0, tiled=True)  20.2 us
    ppermute x3, starting transfers between devices, swap_cores(): return lax.ppermute(value, 'core', [(0, 1), (1, 0)])  18.9 us
    ppermute x3, waiting for transfers between devices, shift_y(): return lax.ppermute(value, 'y', [(i, (i + shift) % Y) for i in range(Y)])  14.2 us
    ppermute x3, starting transfers between devices, shift_y(): return lax.ppermute(value, 'y', [(i, (i + shift) % Y) for i in range(Y)])  9.22 us
    unnamed x22, local copies, waits for them, and re-layouts  4.79 us
    ppermute x3, waiting for transfers between devices, swap_cores(): return lax.ppermute(value, 'core', [(0, 1), (1, 0)])  3.97 us
  transfers between devices with their start and end apart: 8, of which 6 were waited for; matrix products, arithmetic and copies ran while one was open for 3% of the time, Pallas kernels for 0%

profile of v2, /device:TPU:1, one launch (start us, length us, event | category | flops | bytes accessed | tf_op | source)
XLA Modules:
  0.0 192.1 jit_solution(15002654512686400221)
XLA Ops:
  0.0 0.8 copy-done.7
  0.8 0.7 copy-done.8
  1.6 0.8 pack_rows.1
  2.3 9.1 %all-to-all-start = ((bf16[16,24,512]{2,1,0:T(8,128)(2,1)}), bf16[16,24,512]{2,1,0:T(8,128)(2,1)}, u32[]{:S(2)}, u32[]{:S(2)}) async-start(bf16[16,24,512]{2,1,0:T(8,128)(2,1)} %pack_rows.1), calls=%async_computation | async-start | bytes 786432 | tf_op jit(solution)/shard_map/all_to_all | solution.py:17
  11.4 3.9 %collective-permute-start = (bf16[512,256]{1,0:T(8,128)(2,1)S(1)}, bf16[512,256]{1,0:T(8,128)(2,1)}, u32[]{:S(2)}, u32[]{:S(2)}) collective-permute-start(bf16[512,256]{1,0:T(8,128)(2,1)S(1)} %copy-done.10), channel_id=1, source_target_pairs={{0,16},{16,0},{1,17},{17,1},{2,18},{18,2},{3,19},{19,3},{4,20},{20... | collective-permute-start | bytes 786440 | tf_op jit(solution)/shard_map/ppermute | solution.py:25
  15.4 1.2 copy-done.1
  16.6 0.5 cut_weights.1
  17.1 2.1 %collective-permute-start.1 = (bf16[112,2048]{1,0:T(8,128)(2,1)S(1)}, bf16[112,2048]{1,0:T(8,128)(2,1)S(1)}, u32[]{:S(2)}, u32[]{:S(2)}) collective-permute-start(bf16[112,2048]{1,0:T(8,128)(2,1)S(1)} %get-tuple-element.21), channel_id=1, source_target_pairs={{0,4},{4,8},{8,12},{12,0},{1,5},{5,9},{9,13},{13,1},{2,6},{6,10},{... | collective-permute-start | bytes 1376264 | tf_op jit(solution)/shard_map/ppermute | solution.py:29
  19.2 4.4 %collective-permute-start.2 = (bf16[112,2048]{1,0:T(8,128)(2,1)S(1)}, bf16[112,2048]{1,0:T(8,128)(2,1)S(1)}, u32[]{:S(2)}, u32[]{:S(2)}) collective-permute-start(bf16[112,2048]{1,0:T(8,128)(2,1)S(1)} %get-tuple-element.22), channel_id=1, source_target_pairs={{0,12},{4,0},{8,4},{12,8},{1,13},{5,1},{9,5},{13,9},{2,14},{6,2},{... | collective-permute-start | bytes 1376264 | tf_op jit(solution)/shard_map/ppermute | solution.py:29
  23.7 1.8 broadcast_select_fusion.1
  25.4 0.9 slice.9
  26.4 1.0 slice.8
  27.4 0.3 fusion.10
  27.6 1.3 fusion.1
  28.9 3.4 %collective-permute-done.1.rest_1_ = bf16[112,2048]{1,0:T(8,128)(2,1)S(1)} collective-permute-done((bf16[112,2048]{1,0:T(8,128)(2,1)S(1)}, bf16[112,2048]{1,0:T(8,128)(2,1)S(1)}, u32[]{:S(2)}, u32[]{:S(2)}) %collective-permute-start.1) | collective-permute-done | bytes 458784 | tf_op jit(solution)/shard_map/ppermute | solution.py:29
  32.4 0.9 collective-permute-done.2.rest_3_
  33.2 10.0 %all_to_all.50.parts_ref = bf16[4,128,256]{2,1,0:T(8,128)(2,1)S(1)} all-to-all(bf16[4,128,256]{2,1,0:T(8,128)(2,1)S(1)} %bitcast.33), channel_id=1, replica_groups=mesh['x'=4,'zl'=4,'core'=2,'y'=4,'zh'=4] {'y'}, dimensions={0} | all-to-all | bytes 524288 | tf_op jit(solution)/shard_map/all_to_all | solution.py:17
  43.2 0.7 sum_and_replicate.1
  44.0 11.2 %all-to-all-start.2 = ((bf16[4,128,256]{2,1,0:T(8,128)(2,1)}), bf16[4,128,256]{2,1,0:T(8,128)(2,1)S(1)}, u32[]{:S(2)}, u32[]{:S(2)}) async-start(bf16[4,128,256]{2,1,0:T(8,128)(2,1)} %sum_and_replicate.1), calls=%async_computation.2 | async-start | bytes 524288 | tf_op jit(solution)/shard_map/all_to_all | solution.py:17
  55.1 2.7 %collective-permute-start.3 = (bf16[112,2048]{1,0:T(8,128)(2,1)S(1)}, bf16[112,2048]{1,0:T(8,128)(2,1)S(1)}, u32[]{:S(2)}, u32[]{:S(2)}) collective-permute-start(bf16[112,2048]{1,0:T(8,128)(2,1)S(1)} %get-tuple-element.29), channel_id=1, source_target_pairs={{0,8},{4,12},{8,0},{12,4},{1,9},{5,13},{9,1},{13,5},{2,10},{6,14},... | collective-permute-start | bytes 1376264 | tf_op jit(solution)/shard_map/ppermute | solution.py:29
  57.9 9.9 %collective-permute-done.3.rest_2_ = bf16[112,2048]{1,0:T(8,128)(2,1)S(1)} collective-permute-done((bf16[112,2048]{1,0:T(8,128)(2,1)S(1)}, bf16[112,2048]{1,0:T(8,128)(2,1)S(1)}, u32[]{:S(2)}, u32[]{:S(2)}) %collective-permute-start.3) | collective-permute-done | bytes 458784 | tf_op jit(solution)/shard_map/ppermute | solution.py:29
  67.8 1.9 all-to-all-done.2.parts_ref
  69.7 13.6 %all_to_all.51 = bf16[4,144,256]{2,1,0:T(8,128)(2,1)S(1)} all-to-all(bf16[4,144,256]{2,1,0:T(8,128)(2,1)S(1)} %carried_and_squares.1), channel_id=1, replica_groups=mesh['x'=4,'zl'=4,'core'=2,'y'=4,'zh'=4] {'zl'}, dimensions={0} | all-to-all | bytes 589824 | tf_op jit(solution)/shard_map/all_to_all | solution.py:17
  83.3 0.1 broadcast_in_dim.4
  83.4 14.9 %all_to_all.52 = bf16[4,4,144,256]{3,2,1,0:T(8,128)(2,1)S(1)} all-to-all(bf16[4,4,144,256]{3,2,1,0:T(8,128)(2,1)S(1)} %broadcast_in_dim.4), channel_id=1, replica_groups=mesh['x'=4,'zl'=4,'core'=2,'y'=4,'zh'=4] {'x'}, dimensions={0} | all-to-all | bytes 2359296 | tf_op jit(solution)/shard_map/all_to_all | solution.py:17
  98.3 8.8 %collective-permute-start.4 = (bf16[16,144,256]{2,1,0:T(8,128)(2,1)S(1)}, bf16[16,144,256]{2,1,0:T(8,128)(2,1)S(1)}, u32[]{:S(2)}, u32[]{:S(2)}) collective-permute-start(bf16[16,144,256]{2,1,0:T(8,128)(2,1)S(1)} %bitcast.29), channel_id=1, source_target_pairs={{0,16},{16,0},{1,17},{17,1},{2,18},{18,2},{3,19},{19,3},{4,20},{20... | collective-permute-start | bytes 3538952 | tf_op jit(solution)/shard_map/ppermute | solution.py:25
  107.1 0.1 pad_add_fusion.at_ref
  107.2 2.4 %collective-permute-done.4.other_ref = bf16[16,144,256]{2,1,0:T(8,128)(2,1)S(1)} collective-permute-done((bf16[16,144,256]{2,1,0:T(8,128)(2,1)S(1)}, bf16[16,144,256]{2,1,0:T(8,128)(2,1)S(1)}, u32[]{:S(2)}, u32[]{:S(2)}) %collective-permute-start.4) | collective-permute-done | bytes 1179680 | tf_op jit(solution)/shard_map/ppermute | solution.py:25
  109.6 1.0 copy-done.3
  110.6 1.0 copy-done.5
  111.6 3.0 %gate_up.1 = (bf16[4,128,512]{2,1,0:T(8,128)(2,1)S(1)}, bf16[128,512]{1,0:T(8,128)(2,1)S(1)}) custom-call(s32[3]{0:T(128)S(1)} %pad_add_fusion.at_ref, bf16[16,144,256]{2,1,0:T(8,128)(2,1)S(1)} %bitcast.30, bf16[16,144,256]{2,1,0:T(8,128)(2,1)S(1)} %collective-permute-done.4.other_ref, bf16[112,2048]{1,0:T(8,128)(2,1)S(1)} %get-tuple-element.31.rest_0_, ...), custom_call_target="tpu_custom_call" | custom-call | tf_op jit(solution)/shard_map/gate_up/pallas_call | solution.py:199
  114.6 11.0 %all_to_all.53.parts_ref = bf16[4,128,512]{2,1,0:T(8,128)(2,1)S(1)} all-to-all(bf16[4,128,512]{2,1,0:T(8,128)(2,1)S(1)} %get-tuple-element.36), channel_id=1, replica_groups=mesh['x'=4,'zl'=4,'core'=2,'y'=4,'zh'=4] {'y'}, dimensions={0} | all-to-all | bytes 1048576 | tf_op jit(solution)/shard_map/all_to_all | solution.py:17
  125.7 0.1 activate.1
  125.8 8.2 %all_to_all.54 = bf16[4,56,512]{2,1,0:T(8,128)(2,1)S(1)} all-to-all(bf16[4,56,512]{2,1,0:T(8,128)(2,1)S(1)} %activate.1), channel_id=1, replica_groups=mesh['x'=4,'zl'=4,'core'=2,'y'=4,'zh'=4] {'zl'}, dimensions={0} | all-to-all | bytes 458752 | tf_op jit(solution)/shard_map/all_to_all | solution.py:17
  134.0 0.1 broadcast_in_dim.5
  134.1 13.0 %all_to_all.55 = bf16[4,4,56,512]{3,2,1,0:T(8,128)(2,1)S(1)} all-to-all(bf16[4,4,56,512]{3,2,1,0:T(8,128)(2,1)S(1)} %broadcast_in_dim.5), channel_id=1, replica_groups=mesh['x'=4,'zl'=4,'core'=2,'y'=4,'zh'=4] {'x'}, dimensions={0} | all-to-all | bytes 1835008 | tf_op jit(solution)/shard_map/all_to_all | solution.py:17
  147.1 6.1 %collective-permute-start.5 = (bf16[16,56,512]{2,1,0:T(8,128)(2,1)S(1)}, bf16[16,56,512]{2,1,0:T(8,128)(2,1)}, u32[]{:S(2)}, u32[]{:S(2)}) collective-permute-start(bf16[16,56,512]{2,1,0:T(8,128)(2,1)S(1)} %bitcast.36), channel_id=1, source_target_pairs={{0,16},{16,0},{1,17},{17,1},{2,18},{18,2},{3,19},{19,3},{4,20},{20... | collective-permute-start | bytes 2752520 | tf_op jit(solution)/shard_map/ppermute | solution.py:25
  153.2 0.1 constant_dynamic-slice_fusion.1
  153.3 0.5 fusion.15
  153.8 1.6 collective-permute-done.5
  155.4 1.7 fusion.16
  157.1 0.3 fusion.2
  157.4 0.1 reshape.70
  157.4 0.1 copy.20
  157.6 0.1 reshape.71
  157.6 10.2 %all_to_all.56 = bf16[16,32,256]{2,1,0:T(8,128)(2,1)S(1)} all-to-all(bf16[16,32,256]{2,1,0:T(8,128)(2,1)S(1)} %reshape.71), channel_id=1, replica_groups=mesh['x'=4,'zl'=4,'core'=2,'y'=4,'zh'=4] {'x','y'}, dimensions={0} | all-to-all | bytes 524288 | tf_op jit(solution)/shard_map/all_to_all | solution.py:17
  168.0 23.3 %all_to_all.57 = bf16[32,8,128]{2,1,0:T(8,128)(2,1)S(1)} all-to-all(bf16[32,8,128]{2,1,0:T(8,128)(2,1)S(1)} %reshape.73), channel_id=1, replica_groups=mesh['x'=4,'zl'=4,'core'=2,'y'=4,'zh'=4] {'core','zl','zh'}, dimensions={0} | all-to-all | bytes 131072 | tf_op jit(solution)/shard_map/all_to_all | solution.py:17
  191.5 0.6 convert_element_type.39
  (28 shorter events, 0.3 us)
Async XLA Ops:
  0.0 15.4 %copy-start.6 = (f32[8192]{0:T(1024)S(1)}, f32[8192]{0:T(1024)}, u32[]{:S(2)}) copy-start(f32[8192]{0:T(1024)} %param.10) | copy-start | bytes 98308
  0.0 15.4 %copy-start = (bf16[56,8192]{1,0:T(8,128)(2,1)S(1)}, bf16[56,8192]{1,0:T(8,128)(2,1)}, u32[]{:S(2)}) copy-start(bf16[56,8192]{1,0:T(8,128)(2,1)} %gate_ref.1) | copy-start | bytes 2752516
  0.0 0.8 copy-start.7
  0.8 0.7 copy-start.8
  1.6 9.9 %copy-start.10 = (bf16[512,256]{1,0:T(8,128)(2,1)S(1)}, bf16[512,256]{1,0:T(8,128)(2,1)}, u32[]{:S(2)}) copy-start(bf16[512,256]{1,0:T(8,128)(2,1)} %param.8) | copy-start | bytes 786436
  2.3 23.1 %all-to-all-start = ((bf16[16,24,512]{2,1,0:T(8,128)(2,1)}), bf16[16,24,512]{2,1,0:T(8,128)(2,1)}, u32[]{:S(2)}, u32[]{:S(2)}) async-start(bf16[16,24,512]{2,1,0:T(8,128)(2,1)} %pack_rows.1), calls=%async_computation | async-start | bytes 786432 | tf_op jit(solution)/shard_map/all_to_all | solution.py:17
  11.4 12.2 %collective-permute-start = (bf16[512,256]{1,0:T(8,128)(2,1)S(1)}, bf16[512,256]{1,0:T(8,128)(2,1)}, u32[]{:S(2)}, u32[]{:S(2)}) collective-permute-start(bf16[512,256]{1,0:T(8,128)(2,1)S(1)} %copy-done.10), channel_id=1, source_target_pairs={{0,16},{16,0},{1,17},{17,1},{2,18},{18,2},{3,19},{19,3},{4,20},{20... | collective-permute-start | bytes 786440 | tf_op jit(solution)/shard_map/ppermute | solution.py:25
  15.4 1.2 copy-start.1
  17.1 15.2 %collective-permute-start.1 = (bf16[112,2048]{1,0:T(8,128)(2,1)S(1)}, bf16[112,2048]{1,0:T(8,128)(2,1)S(1)}, u32[]{:S(2)}, u32[]{:S(2)}) collective-permute-start(bf16[112,2048]{1,0:T(8,128)(2,1)S(1)} %get-tuple-element.21), channel_id=1, source_target_pairs={{0,4},{4,8},{8,12},{12,0},{1,5},{5,9},{9,13},{13,1},{2,6},{6,10},{... | collective-permute-start | bytes 1376264 | tf_op jit(solution)/shard_map/ppermute | solution.py:29
  19.2 14.0 %collective-permute-start.2 = (bf16[112,2048]{1,0:T(8,128)(2,1)S(1)}, bf16[112,2048]{1,0:T(8,128)(2,1)S(1)}, u32[]{:S(2)}, u32[]{:S(2)}) collective-permute-start(bf16[112,2048]{1,0:T(8,128)(2,1)S(1)} %get-tuple-element.22), channel_id=1, source_target_pairs={{0,12},{4,0},{8,4},{12,8},{1,13},{5,1},{9,5},{13,9},{2,14},{6,2},{... | collective-permute-start | bytes 1376264 | tf_op jit(solution)/shard_map/ppermute | solution.py:29
  33.2 10.7 %copy-start.2 = (bf16[112,2048]{1,0:T(8,128)(2,1)}, bf16[112,2048]{1,0:T(8,128)(2,1)S(1)}, u32[]{:S(2)}) copy-start(bf16[112,2048]{1,0:T(8,128)(2,1)S(1)} %collective-permute-done.2.rest_3_) | copy-start | bytes 1376260
  44.0 25.7 %all-to-all-start.2 = ((bf16[4,128,256]{2,1,0:T(8,128)(2,1)}), bf16[4,128,256]{2,1,0:T(8,128)(2,1)S(1)}, u32[]{:S(2)}, u32[]{:S(2)}) async-start(bf16[4,128,256]{2,1,0:T(8,128)(2,1)} %sum_and_replicate.1), calls=%async_computation.2 | async-start | bytes 524288 | tf_op jit(solution)/shard_map/all_to_all | solution.py:17
  55.1 12.7 %collective-permute-start.3 = (bf16[112,2048]{1,0:T(8,128)(2,1)S(1)}, bf16[112,2048]{1,0:T(8,128)(2,1)S(1)}, u32[]{:S(2)}, u32[]{:S(2)}) collective-permute-start(bf16[112,2048]{1,0:T(8,128)(2,1)S(1)} %get-tuple-element.29), channel_id=1, source_target_pairs={{0,8},{4,12},{8,0},{12,4},{1,9},{5,13},{9,1},{13,5},{2,10},{6,14},... | collective-permute-start | bytes 1376264 | tf_op jit(solution)/shard_map/ppermute | solution.py:29
  67.8 15.5 %copy-start.4 = (bf16[112,2048]{1,0:T(8,128)(2,1)}, bf16[112,2048]{1,0:T(8,128)(2,1)S(1)}, u32[]{:S(2)}) copy-start(bf16[112,2048]{1,0:T(8,128)(2,1)S(1)} %collective-permute-done.3.rest_2_) | copy-start | bytes 1376260
  98.3 11.3 %collective-permute-start.4 = (bf16[16,144,256]{2,1,0:T(8,128)(2,1)S(1)}, bf16[16,144,256]{2,1,0:T(8,128)(2,1)S(1)}, u32[]{:S(2)}, u32[]{:S(2)}) collective-permute-start(bf16[16,144,256]{2,1,0:T(8,128)(2,1)S(1)} %bitcast.29), channel_id=1, source_target_pairs={{0,16},{16,0},{1,17},{17,1},{2,18},{18,2},{3,19},{19,3},{4,20},{20... | collective-permute-start | bytes 3538952 | tf_op jit(solution)/shard_map/ppermute | solution.py:25
  109.6 1.0 copy-start.3
  110.6 1.0 copy-start.5
  134.1 19.2 %copy-start.9 = (bf16[32,56,256]{2,1,0:T(8,128)(2,1)S(1)}, bf16[32,56,256]{2,1,0:T(8,128)(2,1)}, u32[]{:S(2)}) copy-start(bf16[32,56,256]{2,1,0:T(8,128)(2,1)} %param.13) | copy-start | bytes 2752516
  147.1 8.3 %collective-permute-start.5 = (bf16[16,56,512]{2,1,0:T(8,128)(2,1)S(1)}, bf16[16,56,512]{2,1,0:T(8,128)(2,1)}, u32[]{:S(2)}, u32[]{:S(2)}) collective-permute-start(bf16[16,56,512]{2,1,0:T(8,128)(2,1)S(1)} %bitcast.36), channel_id=1, source_target_pairs={{0,16},{16,0},{1,17},{17,1},{2,18},{18,2},{3,19},{19,3},{4,20},{20... | collective-permute-start | bytes 2752520 | tf_op jit(solution)/shard_map/ppermute | solution.py:25

commit v3 on v2

--- a/solution.py
+++ b/solution.py
@@ -25,8 +25,8 @@
     return lax.ppermute(value, "core", [(0, 1), (1, 0)])
 
 
-def shift_y(value, shift):
-    return lax.ppermute(value, "y", [(i, (i + shift) % Y) for i in range(Y)])
+def shift_along(value, axis, shift):
+    return lax.ppermute(value, axis, [(i, (i + shift) % 4) for i in range(4)])
 
 
 def vmem():
@@ -84,6 +84,93 @@
         compiler_params=pltpu.CompilerParams(vmem_limit_bytes=12 * 1024 * 1024),
         name="cut_weights",
     )(y_at.reshape(1), w_gate, w_up, norm_gain.reshape(1, d))
+
+
+def project(got, w_out, w_other, at):
+    blocks, _, heads = got.shape
+    cols = w_out.shape[1]
+    t_rows = Y * ZH
+    half = blocks * t_rows
+    part = CORES * cols // Y
+
+    def kernel(at_ref, got_ref, own_ref, other_ref, out_ref, att, res):
+        y, zh, core = at_ref[0], at_ref[1], at_ref[2]
+        for x in range(X):
+            for zl in range(ZL):
+                block = x * ZL + zl
+                for row in range(Y):
+                    to = ((x * Y + row) * ZL + zl) * ZH
+                    att[to : to + ZH, :] = got_ref[block, row * ZH : (row + 1) * ZH, :]
+                res[block : block + 1, :] = got_ref[block, t_rows : t_rows + 1, :]
+        token = lax.broadcasted_iota(jnp.int32, (half, blocks), 0)
+        source = lax.broadcasted_iota(jnp.int32, (half, blocks), 1)
+        place = ((source // ZL) * Y + y) * t_rows + lax.rem(source, ZL) * ZH + zh
+        pick = jnp.where(token == place, 1.0, 0.0).astype(BF16)
+        for turn, ref in enumerate((own_ref, other_ref)):
+            side = core if turn == 0 else 1 - core
+            columns = pl.ds(pl.multiple_of(side * cols, cols), cols)
+            total = jnp.dot(att[...], ref[...], preferred_element_type=F32) + jnp.dot(
+                pick, res[:, columns], preferred_element_type=F32
+            )
+            total = total.T.astype(BF16)
+            for piece in range(cols // part):
+                out_ref[side * (cols // part) + piece] = total[piece * part : (piece + 1) * part]
+
+    return pl.pallas_call(
+        kernel,
+        out_shape=jax.ShapeDtypeStruct((Y, part, half), BF16),
+        in_specs=[smem(), vmem(), vmem(), vmem()],
+        out_specs=vmem(),
+        scratch_shapes=[pltpu.VMEM((half, heads), BF16), pltpu.VMEM((blocks, heads), BF16)],
+        compiler_params=pltpu.CompilerParams(vmem_limit_bytes=6 * 1024 * 1024),
+        name="project",
+    )(at, got, w_out, w_other)
+
+
+def down(hidden, pieces, kept, at):
+    depth, tokens = hidden.shape
+    cols = pieces[0].shape[1]
+    part = kept.shape[0]
+    near = tokens // (X * Y * CORES)
+
+    def kernel(at_ref, hidden_ref, kept_ref, *rest):
+        piece_refs, out_ref = rest[:X], rest[X]
+        x, y, core, zh = at_ref[0], at_ref[1], at_ref[2], at_ref[3]
+        rows = hidden_ref[...].astype(F32)
+        units = depth // (CORES * ZL)
+        rows = jnp.concatenate(
+            [
+                rows[(side * ZL + zl) * units : (side * ZL + zl + 1) * units]
+                for zl in range(ZL)
+                for side in range(CORES)
+            ],
+            axis=0,
+        )
+        lhs = rows.T.astype(BF16)
+        kept_rows = kept_ref[...].astype(F32).T
+        adds = (y // 2 == core) & (zh == 0)
+        left = jnp.where(adds & (lax.rem(y, 2) == 0), 1.0, 0.0)
+        right = jnp.where(adds & (lax.rem(y, 2) == 1), 1.0, 0.0)
+        for shift in range(X):
+            total = jnp.dot(lhs, piece_refs[shift][...], preferred_element_type=F32)
+            if shift == 0:
+                total = total + jnp.concatenate([kept_rows * left, kept_rows * right], axis=1)
+            total = total.astype(BF16)
+            start = lax.rem(x - shift + X, X) * cols
+            place = pl.ds(pl.multiple_of(start, cols), cols)
+            for side in range(CORES):
+                for to in range(X * Y):
+                    row = side * (tokens // CORES) + to * near
+                    out_ref[to, side * near : (side + 1) * near, place] = total[row : row + near]
+
+    return pl.pallas_call(
+        kernel,
+        out_shape=jax.ShapeDtypeStruct((X * Y, CORES * near, X * cols), BF16),
+        in_specs=[smem(), vmem(), vmem()] + [vmem()] * X,
+        out_specs=vmem(),
+        compiler_params=pltpu.CompilerParams(vmem_limit_bytes=10 * 1024 * 1024),
+        name="down",
+    )(at, hidden, kept, *pieces)
 
 
 def sum_and_replicate(parts, count):
@@ -165,17 +252,11 @@
 
     def kernel(at_ref, own_ref, other_ref, *rest):
         piece_refs, out_ref, carried_ref = rest[:Y], rest[Y], rest[Y + 1]
-        weights, rhs, tails, sem = rest[Y + 2 :]
+        weights, rhs, tails = rest[Y + 2 :]
         y, core, mine = at_ref[0], at_ref[1], at_ref[2]
-        copies = []
         for shift in range(Y):
             to = lax.rem(y - shift + Y, Y)
-            place = pl.ds(pl.multiple_of(to * both, both), both)
-            copies.append(
-                pltpu.make_async_copy(piece_refs[shift], weights.at[place, :], sem.at[shift])
-            )
-        for copy in copies:
-            copy.start()
+            weights[pl.ds(pl.multiple_of(to * both, both), both), :] = piece_refs[shift][...]
         for turn, ref in enumerate((own_ref, other_ref)):
             side = core if turn == 0 else 1 - core
             place = pl.ds(pl.multiple_of(side * half, half), half)
@@ -189,8 +270,6 @@
                 [high, square - high, jnp.zeros((EXTRA - 2, half), F32)], axis=0
             ).astype(BF16)
             carried_ref[:, place] = ref[mine, :part, :]
-        for copy in copies:
-            copy.wait()
         total = jnp.dot(weights[...], rhs[...], preferred_element_type=F32)
         for to in range(Y):
             out_ref[to, :both, :] = total[to * both : (to + 1) * both].astype(BF16)
@@ -202,13 +281,12 @@
             jax.ShapeDtypeStruct((Y, both + EXTRA, CORES * half), BF16),
             jax.ShapeDtypeStruct((part, CORES * half), BF16),
         ],
-        in_specs=[smem(), vmem(), vmem()] + [pl.BlockSpec(memory_space=pltpu.HBM)] * Y,
+        in_specs=[smem(), vmem(), vmem()] + [vmem()] * Y,
         out_specs=[vmem(), vmem()],
         scratch_shapes=[
             pltpu.VMEM((Y * both, depth), BF16),
             pltpu.VMEM((depth, CORES * half), BF16),
             pltpu.VMEM((EXTRA, CORES * half), BF16),
-            pltpu.SemaphoreType.DMA((Y,)),
         ],
         compiler_params=pltpu.CompilerParams(vmem_limit_bytes=8 * 1024 * 1024),
         name="gate_up",
@@ -222,7 +300,7 @@
     y_at = lax.axis_index("y")
     zh_at = lax.axis_index("zh")
     d = residual.shape[1]
-    t_rows, heads = attention_out.shape
+    t_rows = attention_out.shape[0]
     cols = w_out.shape[1]
     units = w_gate.shape[0]
     blocks = X * ZL
@@ -231,31 +309,31 @@
     part = CORES * cols // Y
 
     cut = cut_weights(w_gate, w_up, norm_gain, y_at)
-    first_piece, third_piece = shift_y(cut[1], 1), shift_y(cut[3], 3)
+    first_piece, third_piece = shift_along(cut[1], "y", 1), shift_along(cut[3], "y", 3)
+    by_x = w_down.reshape(X, ZL * CORES * units, cols)
+    down_cut = [
+        lax.dynamic_index_in_dim(by_x, (x_at + shift) % X, 0, keepdims=False)
+        for shift in range(X)
+    ]
     w_other = swap_cores(w_out)
-    first = core_at == 0
-    w_pair = jnp.concatenate(
-        [jnp.where(first, w_out, w_other), jnp.where(first, w_other, w_out)], axis=1
-    )
 
     got = exchange(pack_rows(attention_out, residual), ("x", "zl"))
-    att = got[:, :t_rows].reshape(half, heads)
-    res = got[:, t_rows]
-    token = lax.broadcasted_iota(jnp.int32, (blocks, half), 1)
-    source = lax.broadcasted_iota(jnp.int32, (blocks, half), 0)
-    place = (token == source * t_rows + (y_at * ZH + zh_at)).astype(BF16)
-    partial = lax.dot_general(
-        w_pair, att, (((0,), (1,)), ((), ())), preferred_element_type=F32
-    ) + lax.dot_general(res, place, (((0,), (0,)), ((), ())), preferred_element_type=F32)
-    partial = partial.astype(BF16).reshape(Y, part, half)
-    partial, first_piece, third_piece, cut = lax.optimization_barrier(
-        (partial, first_piece, third_piece, cut)
+    partial = project(got, w_out, w_other, jnp.stack([y_at, zh_at, core_at]))
+    partial, first_piece, third_piece, cut, down_cut = lax.optimization_barrier(
+        (partial, first_piece, third_piece, cut, down_cut)
     )
     by_y = exchange(partial, "y")
-    over_y, cut = lax.optimization_barrier((sum_and_replicate(by_y, ZH), cut))
-    second_piece = shift_y(cut[2], 2)
+    over_y, cut, down_cut = lax.optimization_barrier(
+        (sum_and_replicate(by_y, ZH), cut, down_cut)
+    )
+    second_piece = shift_along(cut[2], "y", 2)
+    down_pieces = [down_cut[0]] + [
+        shift_along(down_cut[shift], "x", shift) for shift in range(1, X)
+    ]
     by_zh = exchange(over_y, "zh")
-    by_zh, second_piece = lax.optimization_barrier((by_zh, second_piece))
+    by_zh, second_piece, down_pieces = lax.optimization_barrier(
+        (by_zh, second_piece, down_pieces)
+    )
     pieces = [cut[0], first_piece, second_piece, third_piece]
     spread = exchange(carried_and_squares(by_zh, ZL), "zl")
     spread = exchange(replicate(spread, X), "x")
@@ -267,31 +345,15 @@
         jnp.stack([y_at, core_at, x_at * ZL + zl_at]),
     )
     hidden = exchange(activate(exchange(outs, "y"), d, ZL), "zl")
-    hidden = exchange(replicate(hidden, X), "x")
-    hidden = hidden.reshape(blocks, units, tokens)
-    hidden_pair = (hidden, swap_cores(hidden))
-    down_w = w_down.reshape(blocks, CORES, units, cols)
-    feature = lax.broadcasted_iota(jnp.int32, (part, cols), 0)
-    column = lax.broadcasted_iota(jnp.int32, (part, cols), 1)
-    adds = (y_at // 2 == core_at) & (zh_at == 0)
-    keep = ((column == feature + (y_at % 2) * part) & adds).astype(BF16)
-    down = lax.dot_general(kept, keep, (((0,), (0,)), ((), ())), preferred_element_type=F32)
-    for turn in range(CORES):
-        side = core_at if turn == 0 else 1 - core_at
-        down = down + lax.dot_general(
-            hidden_pair[turn].reshape(blocks * units, tokens),
-            lax.dynamic_index_in_dim(down_w, side, 1, keepdims=False).reshape(
-                blocks * units, cols
-            ),
-            (((0,), (0,)), ((), ())),
-            preferred_element_type=F32,
-        )
-    by_owner = jnp.transpose(
-        down.astype(BF16).reshape(CORES, X, ZL, Y, ZH, cols), (1, 3, 0, 2, 4, 5)
-    ).reshape(X * Y, CORES * ZL * ZH, cols)
-    near = exchange(by_owner, ("x", "y")).reshape(X, Y, CORES * ZL * ZH, cols)
-    near = jnp.sum(near.astype(F32), axis=1).astype(BF16)
-    near = jnp.transpose(near, (1, 0, 2)).reshape(CORES * ZL * ZH, X * cols // 128, 128)
+    hidden = lax.all_gather(hidden, "core", axis=0, tiled=False)
+    by_owner = down(
+        hidden.reshape(CORES * ZL * units, tokens),
+        down_pieces,
+        kept,
+        jnp.stack([x_at, y_at, core_at, zh_at]),
+    )
+    near = sum_and_replicate(exchange(by_owner, ("x", "y")), 1)
+    near = near.reshape(CORES * ZL * ZH, X * cols // 128, 128)
     final = exchange(near, ("core", "zl", "zh"))
     final = final.reshape(CORES, ZL, ZH, X, cols).astype(F32)
     mixed = jnp.sum(final, axis=2)

time: 193 us -> 186 us (0.964)
  starting transfers between devices: 48.3 us -> 57.8 us
  blocking collectives: 104 us -> 96.4 us
  waiting for transfers between devices: 20.1 us -> 14.7 us
  matrix products: 3.98 us -> 0 us
  Pallas kernels: 5.2 us -> 8.12 us
    all_to_all x8 -> x6, blocking collectives: 104 us -> 90.6 us  [exchange(): return lax.all_to_all(value, axes, 0, 0, tiled=True)]
    ppermute x3 -> x6, starting transfers between devices: 9.22 us -> 19.4 us  [shift_along(): return lax.ppermute(value, axis, [(i, (i + shift) % 4) for i in range(4)])]
    ppermute x3 -> x6, waiting for transfers between devices: 14.2 us -> 7.07 us  [shift_along(): return lax.ppermute(value, axis, [(i, (i + shift) % 4) for i in range(4)])]
    all_gather x0 -> x1, blocking collectives: none -> 5.75 us  [shards(): hidden = lax.all_gather(hidden, 'core', axis=0, tiled=False)]
    ppermute x3 -> x2, starting transfers between devices: 18.9 us -> 13.6 us  [swap_cores(): return lax.ppermute(value, 'core', [(0, 1), (1, 0)])]
    all_to_all x2 -> x3, starting transfers between devices: 20.2 us -> 24.9 us  [exchange(): return lax.all_to_all(value, axes, 0, 0, tiled=True)]
    dot_general x5 -> x0, matrix products: 3.98 us -> none  [the longest x2 2.13 us: shards(): lax.dot_general(hidden_pair[turn].reshape(blocks * units, tokens), lax.dy...]
    all_to_all x2 -> x3, waiting for transfers between devices: 1.88 us -> 5.3 us  [exchange(): return lax.all_to_all(value, axes, 0, 0, tiled=True)]
  transfers between devices with their start and end apart: 8 -> 11, of which waited for: 6 -> 6; matrix products, arithmetic and copies ran while one was open for 3% -> 1% of each run, Pallas kernels for 0% -> 1%
where the time goes in v3:
time: 186 us; the launch traced here: 185 us
  blocking collectives  96.4 us (52%)
  starting transfers between devices  57.8 us (31%)
  waiting for transfers between devices  14.7 us (8%)
  Pallas kernels  8.12 us (4%)
  local copies, waits for them, and re-layouts  7.73 us (4%)
    all_to_all x6, blocking collectives, exchange(): return lax.all_to_all(value, axes, 0, 0, tiled=True)  90.6 us
    all_to_all x3, starting transfers between devices, exchange(): return lax.all_to_all(value, axes, 0, 0, tiled=True)  24.9 us
    ppermute x6, starting transfers between devices, shift_along(): return lax.ppermute(value, axis, [(i, (i + shift) % 4) for i in range(4)])  19.4 us
    ppermute x2, starting transfers between devices, swap_cores(): return lax.ppermute(value, 'core', [(0, 1), (1, 0)])  13.6 us
    ppermute x6, waiting for transfers between devices, shift_along(): return lax.ppermute(value, axis, [(i, (i + shift) % 4) for i in range(4)])  7.07 us
    all_gather x1, blocking collectives, shards(): hidden = lax.all_gather(hidden, 'core', axis=0, tiled=False)  5.75 us
    all_to_all x3, waiting for transfers between devices, exchange(): return lax.all_to_all(value, axes, 0, 0, tiled=True)  5.3 us
    unnamed x37, local copies, waits for them, and re-layouts  4.82 us
  transfers between devices with their start and end apart: 11, of which 6 were waited for; matrix products, arithmetic and copies ran while one was open for 1% of the time, Pallas kernels for 1%

profile of v3, /device:TPU:1, one launch (start us, length us, event | category | flops | bytes accessed | tf_op | source)
XLA Modules:
  0.0 185.4 jit_solution(16985840169078717552)
XLA Ops:
  0.0 0.8 copy-done.16
  0.8 0.7 copy-done.17
  1.6 0.8 pack_rows.1
  2.4 9.1 %all-to-all-start = ((bf16[16,24,512]{2,1,0:T(8,128)(2,1)}), bf16[16,24,512]{2,1,0:T(8,128)(2,1)S(1)}, u32[]{:S(2)}, u32[]{:S(2)}) async-start(bf16[16,24,512]{2,1,0:T(8,128)(2,1)} %pack_rows.1), calls=%async_computation | async-start | bytes 786432 | tf_op jit(solution)/shard_map/all_to_all | solution.py:17
  11.6 0.0 copy-start.1
  11.6 1.2 copy-done.1
  12.7 1.4 cut_weights.1
  14.1 3.2 %collective-permute-start.1 = (bf16[112,2048]{1,0:T(8,128)(2,1)}, bf16[112,2048]{1,0:T(8,128)(2,1)S(1)}, u32[]{:S(2)}, u32[]{:S(2)}) collective-permute-start(bf16[112,2048]{1,0:T(8,128)(2,1)} %get-tuple-element.33), channel_id=1, source_target_pairs={{0,4},{4,8},{8,12},{12,0},{1,5},{5,9},{9,13},{13,1},{2,6},{6,10},{... | collective-permute-start | bytes 1376264 | tf_op jit(solution)/shard_map/ppermute | solution.py:29
  17.3 3.4 %collective-permute-start.2 = (bf16[112,2048]{1,0:T(8,128)(2,1)S(1)}, bf16[112,2048]{1,0:T(8,128)(2,1)S(1)}, u32[]{:S(2)}, u32[]{:S(2)}) collective-permute-start(bf16[112,2048]{1,0:T(8,128)(2,1)S(1)} %get-tuple-element.34), channel_id=1, source_target_pairs={{0,12},{4,0},{8,4},{12,8},{1,13},{5,1},{9,5},{13,9},{2,14},{6,2},{... | collective-permute-start | bytes 1376264 | tf_op jit(solution)/shard_map/ppermute | solution.py:29
  20.7 3.8 %collective-permute-start = (bf16[512,256]{1,0:T(8,128)(2,1)S(1)}, bf16[512,256]{1,0:T(8,128)(2,1)S(1)}, u32[]{:S(2)}, u32[]{:S(2)}) collective-permute-start(bf16[512,256]{1,0:T(8,128)(2,1)S(1)} %copy-done.6), channel_id=1, source_target_pairs={{0,16},{16,0},{1,17},{17,1},{2,18},{18,2},{3,19},{19,3},{4,20},{20... | collective-permute-start | bytes 786440 | tf_op jit(solution)/shard_map/ppermute | solution.py:25
  24.6 0.1 pad_add_fusion.2.at_ref
  24.6 2.1 %dynamic-slice_bitcast_fusion = (bf16[448,256]{1,0:T(8,128)(2,1)S(1)}, bf16[448,256]{1,0:T(8,128)(2,1)}, bf16[448,256]{1,0:T(8,128)(2,1)}, bf16[448,256]{1,0:T(8,128)(2,1)S(1)}) fusion(bf16[4,448,256]{2,1,0:T(8,128)(2,1)} %bitcast.26, s32[]{:T(128)S(6)} %select_n.39, s32[]{:T(128)S(6)} %select_n.37, s32[]{:T(128)S(6)} %select_n.35, s32[]{:T(128)S(6)} %select_n.33), kind=kLoop, calls=%fused_computation | loop fusion | bytes 1835024 | tf_op jit(solution)/shard_map/jit(dynamic_index_in_dim)/squeeze | solution.py:315
  26.8 0.0 collective-permute-done.other_ref
  26.8 0.0 all-to-all-done.got_ref
  26.8 1.0 project.1
  27.8 0.3 collective-permute-done.1.rest_1_
  28.1 1.8 collective-permute-done.2.rest_3_
  30.0 9.2 %all_to_all.45.parts_ref = bf16[4,128,256]{2,1,0:T(8,128)(2,1)S(1)} all-to-all(bf16[4,128,256]{2,1,0:T(8,128)(2,1)S(1)} %project.1), channel_id=1, replica_groups=mesh['x'=4,'zl'=4,'core'=2,'y'=4,'zh'=4] {'y'}, dimensions={0} | all-to-all | bytes 524288 | tf_op jit(solution)/shard_map/all_to_all | solution.py:17
  39.2 0.7 sum_and_replicate.2
  39.9 12.2 %all-to-all-start.2 = ((bf16[4,128,256]{2,1,0:T(8,128)(2,1)}), bf16[4,128,256]{2,1,0:T(8,128)(2,1)S(1)}, u32[]{:S(2)}, u32[]{:S(2)}) async-start(bf16[4,128,256]{2,1,0:T(8,128)(2,1)} %sum_and_replicate.2), calls=%async_computation.2 | async-start | bytes 524288 | tf_op jit(solution)/shard_map/all_to_all | solution.py:17
  52.1 2.4 %collective-permute-start.3 = (bf16[112,2048]{1,0:T(8,128)(2,1)}, bf16[112,2048]{1,0:T(8,128)(2,1)S(1)}, u32[]{:S(2)}, u32[]{:S(2)}) collective-permute-start(bf16[112,2048]{1,0:T(8,128)(2,1)} %get-tuple-element.45), channel_id=1, source_target_pairs={{0,8},{4,12},{8,0},{12,4},{1,9},{5,13},{9,1},{13,5},{2,10},{6,14},... | collective-permute-start | bytes 1376264 | tf_op jit(solution)/shard_map/ppermute | solution.py:29
  54.6 3.0 %collective-permute-start.4 = (bf16[448,256]{1,0:T(8,128)(2,1)}, bf16[448,256]{1,0:T(8,128)(2,1)S(1)}, u32[]{:S(2)}, u32[]{:S(2)}) collective-permute-start(bf16[448,256]{1,0:T(8,128)(2,1)} %get-tuple-element.47), channel_id=1, source_target_pairs={{0,128},{128,256},{256,384},{384,0},{1,129},{129,257},{257,385},{3... | collective-permute-start | bytes 688136 | tf_op jit(solution)/shard_map/ppermute | solution.py:29
  57.6 4.3 %collective-permute-start.5 = (bf16[448,256]{1,0:T(8,128)(2,1)}, bf16[448,256]{1,0:T(8,128)(2,1)S(1)}, u32[]{:S(2)}, u32[]{:S(2)}) collective-permute-start(bf16[448,256]{1,0:T(8,128)(2,1)} %get-tuple-element.48), channel_id=1, source_target_pairs={{0,256},{128,384},{256,0},{384,128},{1,257},{129,385},{257,1},{385... | collective-permute-start | bytes 688136 | tf_op jit(solution)/shard_map/ppermute | solution.py:29
  61.9 3.1 %collective-permute-start.6 = (bf16[448,256]{1,0:T(8,128)(2,1)S(1)}, bf16[448,256]{1,0:T(8,128)(2,1)S(1)}, u32[]{:S(2)}, u32[]{:S(2)}) collective-permute-start(bf16[448,256]{1,0:T(8,128)(2,1)S(1)} %get-tuple-element.49), channel_id=1, source_target_pairs={{0,384},{128,0},{256,128},{384,256},{1,385},{129,1},{257,129},{385... | collective-permute-start | bytes 688136 | tf_op jit(solution)/shard_map/ppermute | solution.py:29
  65.0 0.0 collective-permute-done.4.rest_1_
  65.0 2.2 %collective-permute-done.5.rest_2_ = bf16[448,256]{1,0:T(8,128)(2,1)S(1)} collective-permute-done((bf16[448,256]{1,0:T(8,128)(2,1)}, bf16[448,256]{1,0:T(8,128)(2,1)S(1)}, u32[]{:S(2)}, u32[]{:S(2)}) %collective-permute-start.5) | collective-permute-done | bytes 229408 | tf_op jit(solution)/shard_map/ppermute | solution.py:29
  67.2 2.8 %collective-permute-done.6.rest_3_ = bf16[448,256]{1,0:T(8,128)(2,1)S(1)} collective-permute-done((bf16[448,256]{1,0:T(8,128)(2,1)S(1)}, bf16[448,256]{1,0:T(8,128)(2,1)S(1)}, u32[]{:S(2)}, u32[]{:S(2)}) %collective-permute-start.6) | collective-permute-done | bytes 229408 | tf_op jit(solution)/shard_map/ppermute | solution.py:29
  69.9 0.1 carried_and_squares.1
  70.0 10.5 %all_to_all.46 = bf16[4,144,256]{2,1,0:T(8,128)(2,1)S(1)} all-to-all(bf16[4,144,256]{2,1,0:T(8,128)(2,1)S(1)} %carried_and_squares.1), channel_id=1, replica_groups=mesh['x'=4,'zl'=4,'core'=2,'y'=4,'zh'=4] {'zl'}, dimensions={0} | all-to-all | bytes 589824 | tf_op jit(solution)/shard_map/all_to_all | solution.py:17
  80.5 0.1 broadcast_in_dim.2
  80.6 13.9 %all_to_all.47 = bf16[4,4,144,256]{3,2,1,0:T(8,128)(2,1)S(1)} all-to-all(bf16[4,4,144,256]{3,2,1,0:T(8,128)(2,1)S(1)} %broadcast_in_dim.2), channel_id=1, replica_groups=mesh['x'=4,'zl'=4,'core'=2,'y'=4,'zh'=4] {'x'}, dimensions={0} | all-to-all | bytes 2359296 | tf_op jit(solution)/shard_map/all_to_all | solution.py:17
  94.5 9.7 %collective-permute-start.7 = (bf16[16,144,256]{2,1,0:T(8,128)(2,1)S(1)}, bf16[16,144,256]{2,1,0:T(8,128)(2,1)S(1)}, u32[]{:S(2)}, u32[]{:S(2)}) collective-permute-start(bf16[16,144,256]{2,1,0:T(8,128)(2,1)S(1)} %bitcast.21), channel_id=1, source_target_pairs={{0,16},{16,0},{1,17},{17,1},{2,18},{18,2},{3,19},{19,3},{4,20},{20... | collective-permute-start | bytes 3538952 | tf_op jit(solution)/shard_map/ppermute | solution.py:25
  104.3 0.1 pad_add_fusion.1.at_ref
  104.3 2.4 %collective-permute-done.7.other_ref = bf16[16,144,256]{2,1,0:T(8,128)(2,1)S(1)} collective-permute-done((bf16[16,144,256]{2,1,0:T(8,128)(2,1)S(1)}, bf16[16,144,256]{2,1,0:T(8,128)(2,1)S(1)}, u32[]{:S(2)}, u32[]{:S(2)}) %collective-permute-start.7) | collective-permute-done | bytes 1179680 | tf_op jit(solution)/shard_map/ppermute | solution.py:25
  106.7 1.0 copy-done.3
  107.7 1.0 copy-done.5
  108.7 1.9 %gate_up.1 = (bf16[4,128,512]{2,1,0:T(8,128)(2,1)S(1)}, bf16[128,512]{1,0:T(8,128)(2,1)S(1)}) custom-call(s32[3]{0:T(128)S(1)} %pad_add_fusion.1.at_ref, bf16[16,144,256]{2,1,0:T(8,128)(2,1)S(1)} %bitcast.22, bf16[16,144,256]{2,1,0:T(8,128)(2,1)S(1)} %collective-permute-done.7.other_ref, bf16[112,2048]{1,0:T(8,128)(2,1)S(1)} %get-tuple-element.51.rest_0_, ...), custom_call_target="tpu_custom_call" | custom-call | tf_op jit(solution)/shard_map/gate_up/pallas_call | solution.py:278
  110.6 12.1 %all_to_all.48.parts_ref = bf16[4,128,512]{2,1,0:T(8,128)(2,1)S(1)} all-to-all(bf16[4,128,512]{2,1,0:T(8,128)(2,1)S(1)} %get-tuple-element.55), channel_id=1, replica_groups=mesh['x'=4,'zl'=4,'core'=2,'y'=4,'zh'=4] {'y'}, dimensions={0} | all-to-all | bytes 1048576 | tf_op jit(solution)/shard_map/all_to_all | solution.py:17
  122.8 0.8 activate.1
  123.5 3.5 %all-to-all-start.6 = ((bf16[4,56,512]{2,1,0:T(8,128)(2,1)}), bf16[4,56,512]{2,1,0:T(8,128)(2,1)S(1)}, u32[]{:S(2)}, u32[]{:S(2)}) async-start(bf16[4,56,512]{2,1,0:T(8,128)(2,1)} %activate.1), calls=%async_computation.6 | async-start | bytes 458752 | tf_op jit(solution)/shard_map/all_to_all | solution.py:17
  127.1 0.1 pad_add_fusion.at_ref
  127.2 5.3 %all-to-all-done.6 = bf16[4,56,512]{2,1,0:T(8,128)(2,1)S(1)} async-done(((bf16[4,56,512]{2,1,0:T(8,128)(2,1)}), bf16[4,56,512]{2,1,0:T(8,128)(2,1)S(1)}, u32[]{:S(2)}, u32[]{:S(2)}) %all-to-all-start.6) | async-done | bytes 229408 | tf_op jit(solution)/shard_map/all_to_all | solution.py:17
  132.5 5.7 %all-gather = bf16[8,56,512]{2,1,0:T(8,128)(2,1)S(1)} all-gather(bf16[4,56,512]{2,1,0:T(8,128)(2,1)S(1)} %all-to-all-done.6), channel_id=2, replica_groups=mesh['x'=4,'zl'=4,'core'=2,'y'=4,'zh'=4] {'core'}, dimensions={0}, use_global_device_ids=true | all-gather | bytes 688128 | tf_op jit(solution)/shard_map/all_gather | solution.py:348
  138.2 1.3 down.1
  139.5 18.6 %all_to_all.49.parts_ref = bf16[16,32,1024]{2,1,0:T(8,128)(2,1)S(1)} all-to-all(bf16[16,32,1024]{2,1,0:T(8,128)(2,1)S(1)} %down.1), channel_id=1, replica_groups=mesh['x'=4,'zl'=4,'core'=2,'y'=4,'zh'=4] {'x','y'}, dimensions={0} | all-to-all | bytes 2097152 | tf_op jit(solution)/shard_map/all_to_all | solution.py:17
  158.2 0.1 sum_and_replicate.3
  158.3 26.3 %all_to_all.50 = bf16[32,8,128]{2,1,0:T(8,128)(2,1)S(1)} all-to-all(bf16[32,8,128]{2,1,0:T(8,128)(2,1)S(1)} %bitcast.27), channel_id=1, replica_groups=mesh['x'=4,'zl'=4,'core'=2,'y'=4,'zh'=4] {'core','zl','zh'}, dimensions={0} | all-to-all | bytes 131072 | tf_op jit(solution)/shard_map/all_to_all | solution.py:17
  184.7 0.6 convert_element_type.27
  (36 shorter events, 0.2 us)
Async XLA Ops:
  0.0 11.5 %copy-start = (bf16[56,8192]{1,0:T(8,128)(2,1)S(1)}, bf16[56,8192]{1,0:T(8,128)(2,1)}, u32[]{:S(2)}) copy-start(bf16[56,8192]{1,0:T(8,128)(2,1)} %gate_ref.1) | copy-start | bytes 2752516
  0.0 11.5 %copy-start.15 = (f32[8192]{0:T(1024)S(1)}, f32[8192]{0:T(1024)}, u32[]{:S(2)}) copy-start(f32[8192]{0:T(1024)} %param.10) | copy-start | bytes 98308
  0.0 0.8 copy-start.16
  0.8 0.7 copy-start.17
  2.4 18.3 %copy-start.6 = (bf16[512,256]{1,0:T(8,128)(2,1)S(1)}, bf16[512,256]{1,0:T(8,128)(2,1)}, u32[]{:S(2)}) copy-start(bf16[512,256]{1,0:T(8,128)(2,1)} %own_ref.1) | copy-start | bytes 786436
  2.4 24.4 %all-to-all-start = ((bf16[16,24,512]{2,1,0:T(8,128)(2,1)}), bf16[16,24,512]{2,1,0:T(8,128)(2,1)S(1)}, u32[]{:S(2)}, u32[]{:S(2)}) async-start(bf16[16,24,512]{2,1,0:T(8,128)(2,1)} %pack_rows.1), calls=%async_computation | async-start | bytes 786432 | tf_op jit(solution)/shard_map/all_to_all | solution.py:17
  11.6 1.2 copy-start.1
  14.1 14.0 %collective-permute-start.1 = (bf16[112,2048]{1,0:T(8,128)(2,1)}, bf16[112,2048]{1,0:T(8,128)(2,1)S(1)}, u32[]{:S(2)}, u32[]{:S(2)}) collective-permute-start(bf16[112,2048]{1,0:T(8,128)(2,1)} %get-tuple-element.33), channel_id=1, source_target_pairs={{0,4},{4,8},{8,12},{12,0},{1,5},{5,9},{9,13},{13,1},{2,6},{6,10},{... | collective-permute-start | bytes 1376264 | tf_op jit(solution)/shard_map/ppermute | solution.py:29
  17.3 12.7 %collective-permute-start.2 = (bf16[112,2048]{1,0:T(8,128)(2,1)S(1)}, bf16[112,2048]{1,0:T(8,128)(2,1)S(1)}, u32[]{:S(2)}, u32[]{:S(2)}) collective-permute-start(bf16[112,2048]{1,0:T(8,128)(2,1)S(1)} %get-tuple-element.34), channel_id=1, source_target_pairs={{0,12},{4,0},{8,4},{12,8},{1,13},{5,1},{9,5},{13,9},{2,14},{6,2},{... | collective-permute-start | bytes 1376264 | tf_op jit(solution)/shard_map/ppermute | solution.py:29
  20.7 6.1 %collective-permute-start = (bf16[512,256]{1,0:T(8,128)(2,1)S(1)}, bf16[512,256]{1,0:T(8,128)(2,1)S(1)}, u32[]{:S(2)}, u32[]{:S(2)}) collective-permute-start(bf16[512,256]{1,0:T(8,128)(2,1)S(1)} %copy-done.6), channel_id=1, source_target_pairs={{0,16},{16,0},{1,17},{17,1},{2,18},{18,2},{3,19},{19,3},{4,20},{20... | collective-permute-start | bytes 786440 | tf_op jit(solution)/shard_map/ppermute | solution.py:25
  30.0 50.5 %copy-start.2 = (bf16[112,2048]{1,0:T(8,128)(2,1)}, bf16[112,2048]{1,0:T(8,128)(2,1)S(1)}, u32[]{:S(2)}) copy-start(bf16[112,2048]{1,0:T(8,128)(2,1)S(1)} %collective-permute-done.2.rest_3_) | copy-start | bytes 1376260
  39.9 30.0 %all-to-all-start.2 = ((bf16[4,128,256]{2,1,0:T(8,128)(2,1)}), bf16[4,128,256]{2,1,0:T(8,128)(2,1)S(1)}, u32[]{:S(2)}, u32[]{:S(2)}) async-start(bf16[4,128,256]{2,1,0:T(8,128)(2,1)} %sum_and_replicate.2), calls=%async_computation.2 | async-start | bytes 524288 | tf_op jit(solution)/shard_map/all_to_all | solution.py:17
  52.1 17.8 %collective-permute-start.3 = (bf16[112,2048]{1,0:T(8,128)(2,1)}, bf16[112,2048]{1,0:T(8,128)(2,1)S(1)}, u32[]{:S(2)}, u32[]{:S(2)}) collective-permute-start(bf16[112,2048]{1,0:T(8,128)(2,1)} %get-tuple-element.45), channel_id=1, source_target_pairs={{0,8},{4,12},{8,0},{12,4},{1,9},{5,13},{9,1},{13,5},{2,10},{6,14},... | collective-permute-start | bytes 1376264 | tf_op jit(solution)/shard_map/ppermute | solution.py:29
  54.6 10.4 %collective-permute-start.4 = (bf16[448,256]{1,0:T(8,128)(2,1)}, bf16[448,256]{1,0:T(8,128)(2,1)S(1)}, u32[]{:S(2)}, u32[]{:S(2)}) collective-permute-start(bf16[448,256]{1,0:T(8,128)(2,1)} %get-tuple-element.47), channel_id=1, source_target_pairs={{0,128},{128,256},{256,384},{384,0},{1,129},{129,257},{257,385},{3... | collective-permute-start | bytes 688136 | tf_op jit(solution)/shard_map/ppermute | solution.py:29
  57.6 9.6 %collective-permute-start.5 = (bf16[448,256]{1,0:T(8,128)(2,1)}, bf16[448,256]{1,0:T(8,128)(2,1)S(1)}, u32[]{:S(2)}, u32[]{:S(2)}) collective-permute-start(bf16[448,256]{1,0:T(8,128)(2,1)} %get-tuple-element.48), channel_id=1, source_target_pairs={{0,256},{128,384},{256,0},{384,128},{1,257},{129,385},{257,1},{385... | collective-permute-start | bytes 688136 | tf_op jit(solution)/shard_map/ppermute | solution.py:29
  61.9 8.0 %collective-permute-start.6 = (bf16[448,256]{1,0:T(8,128)(2,1)S(1)}, bf16[448,256]{1,0:T(8,128)(2,1)S(1)}, u32[]{:S(2)}, u32[]{:S(2)}) collective-permute-start(bf16[448,256]{1,0:T(8,128)(2,1)S(1)} %get-tuple-element.49), channel_id=1, source_target_pairs={{0,384},{128,0},{256,128},{384,256},{1,385},{129,1},{257,129},{385... | collective-permute-start | bytes 688136 | tf_op jit(solution)/shard_map/ppermute | solution.py:29
  65.0 15.6 %copy-start.7 = (bf16[448,256]{1,0:T(8,128)(2,1)}, bf16[448,256]{1,0:T(8,128)(2,1)S(1)}, u32[]{:S(2)}) copy-start(bf16[448,256]{1,0:T(8,128)(2,1)S(1)} %collective-permute-done.4.rest_1_) | copy-start | bytes 688132
  67.2 13.4 %copy-start.9 = (bf16[448,256]{1,0:T(8,128)(2,1)}, bf16[448,256]{1,0:T(8,128)(2,1)S(1)}, u32[]{:S(2)}) copy-start(bf16[448,256]{1,0:T(8,128)(2,1)S(1)} %collective-permute-done.5.rest_2_) | copy-start | bytes 688132
  69.9 10.7 %copy-start.11 = (bf16[448,256]{1,0:T(8,128)(2,1)}, bf16[448,256]{1,0:T(8,128)(2,1)S(1)}, u32[]{:S(2)}) copy-start(bf16[448,256]{1,0:T(8,128)(2,1)S(1)} %collective-permute-done.6.rest_3_) | copy-start | bytes 688132
  69.9 10.6 %copy-start.4 = (bf16[112,2048]{1,0:T(8,128)(2,1)}, bf16[112,2048]{1,0:T(8,128)(2,1)S(1)}, u32[]{:S(2)}) copy-start(bf16[112,2048]{1,0:T(8,128)(2,1)S(1)} %collective-permute-done.3.rest_2_) | copy-start | bytes 1376260
  94.5 12.2 %collective-permute-start.7 = (bf16[16,144,256]{2,1,0:T(8,128)(2,1)S(1)}, bf16[16,144,256]{2,1,0:T(8,128)(2,1)S(1)}, u32[]{:S(2)}, u32[]{:S(2)}) collective-permute-start(bf16[16,144,256]{2,1,0:T(8,128)(2,1)S(1)} %bitcast.21), channel_id=1, source_target_pairs={{0,16},{16,0},{1,17},{17,1},{2,18},{18,2},{3,19},{19,3},{4,20},{20... | collective-permute-start | bytes 3538952 | tf_op jit(solution)/shard_map/ppermute | solution.py:25
  106.7 1.0 copy-start.3
  107.7 1.0 copy-start.5
  110.6 12.1 %copy-start.13 = (bf16[128,512]{1,0:T(8,128)(2,1)}, bf16[128,512]{1,0:T(8,128)(2,1)S(1)}, u32[]{:S(2)}) copy-start(bf16[128,512]{1,0:T(8,128)(2,1)S(1)} %get-tuple-element.56.kept_ref) | copy-start | bytes 393220
  122.7 15.5 %copy-start.8 = (bf16[448,256]{1,0:T(8,128)(2,1)S(1)}, bf16[448,256]{1,0:T(8,128)(2,1)}, u32[]{:S(2)}) copy-start(bf16[448,256]{1,0:T(8,128)(2,1)} %copy-done.7) | copy-start | bytes 688132
  122.7 15.5 %copy-start.10 = (bf16[448,256]{1,0:T(8,128)(2,1)S(1)}, bf16[448,256]{1,0:T(8,128)(2,1)}, u32[]{:S(2)}) copy-start(bf16[448,256]{1,0:T(8,128)(2,1)} %copy-done.9) | copy-start | bytes 688132
  122.7 15.5 %copy-start.12 = (bf16[448,256]{1,0:T(8,128)(2,1)S(1)}, bf16[448,256]{1,0:T(8,128)(2,1)}, u32[]{:S(2)}) copy-start(bf16[448,256]{1,0:T(8,128)(2,1)} %copy-done.11) | copy-start | bytes 688132
  123.5 14.7 %copy-start.14 = (bf16[128,512]{1,0:T(8,128)(2,1)S(1)}, bf16[128,512]{1,0:T(8,128)(2,1)}, u32[]{:S(2)}) copy-start(bf16[128,512]{1,0:T(8,128)(2,1)} %copy-done.13) | copy-start | bytes 393220
  123.5 8.9 %all-to-all-start.6 = ((bf16[4,56,512]{2,1,0:T(8,128)(2,1)}), bf16[4,56,512]{2,1,0:T(8,128)(2,1)S(1)}, u32[]{:S(2)}, u32[]{:S(2)}) async-start(bf16[4,56,512]{2,1,0:T(8,128)(2,1)} %activate.1), calls=%async_computation.6 | async-start | bytes 458752 | tf_op jit(solution)/shard_map/all_to_all | solution.py:17

commit v4 on v3

--- a/solution.py
+++ b/solution.py
@@ -319,23 +319,23 @@
 
     got = exchange(pack_rows(attention_out, residual), ("x", "zl"))
     partial = project(got, w_out, w_other, jnp.stack([y_at, zh_at, core_at]))
-    partial, first_piece, third_piece, cut, down_cut = lax.optimization_barrier(
-        (partial, first_piece, third_piece, cut, down_cut)
-    )
     by_y = exchange(partial, "y")
-    over_y, cut, down_cut = lax.optimization_barrier(
-        (sum_and_replicate(by_y, ZH), cut, down_cut)
+    over_y, first_piece, third_piece, cut, down_cut = lax.optimization_barrier(
+        (sum_and_replicate(by_y, ZH), first_piece, third_piece, cut, down_cut)
     )
     second_piece = shift_along(cut[2], "y", 2)
     down_pieces = [down_cut[0]] + [
-        shift_along(down_cut[shift], "x", shift) for shift in range(1, X)
+        shift_along(down_cut[shift], "x", shift) if shift != 2 else None for shift in range(1, X)
     ]
     by_zh = exchange(over_y, "zh")
-    by_zh, second_piece, down_pieces = lax.optimization_barrier(
-        (by_zh, second_piece, down_pieces)
-    )
+    by_zh, second_piece, down_pieces[1], down_pieces[3], down_cut = lax.optimization_barrier(
+        (by_zh, second_piece, down_pieces[1], down_pieces[3], down_cut)
+    )
+    down_pieces[2] = shift_along(down_cut[2], "x", 2)
     pieces = [cut[0], first_piece, second_piece, third_piece]
-    spread = exchange(carried_and_squares(by_zh, ZL), "zl")
+    spread, down_pieces[2] = lax.optimization_barrier(
+        (exchange(carried_and_squares(by_zh, ZL), "zl"), down_pieces[2])
+    )
     spread = exchange(replicate(spread, X), "x")
     spread = spread.reshape(blocks, part + EXTRA, half)
     outs, kept = gate_up(

time: 186 us -> 183 us (0.984)
  blocking collectives: 96.4 us -> 75.9 us
  starting transfers between devices: 57.8 us -> 69 us
  waiting for transfers between devices: 14.7 us -> 19.6 us
    all_to_all x6 -> x4, blocking collectives: 90.6 us -> 70.7 us  [exchange(): return lax.all_to_all(value, axes, 0, 0, tiled=True)]
    all_to_all x3 -> x5, starting transfers between devices: 24.9 us -> 36.8 us  [exchange(): return lax.all_to_all(value, axes, 0, 0, tiled=True)]
    ppermute x2, starting transfers between devices: 13.6 us -> 9.33 us  [swap_cores(): return lax.ppermute(value, 'core', [(0, 1), (1, 0)])]
    all_to_all x3 -> x5, waiting for transfers between devices: 5.3 us -> 9.36 us  [exchange(): return lax.all_to_all(value, axes, 0, 0, tiled=True)]
    ppermute x6, starting transfers between devices: 19.4 us -> 22.9 us  [shift_along(): return lax.ppermute(value, axis, [(i, (i + shift) % 4) for i in range(4)])]
  transfers between devices with their start and end apart: 11 -> 13, of which waited for: 6 -> 8; matrix products, arithmetic and copies ran while one was open for 1% -> 1% of each run, Pallas kernels for 1% -> 2%
where the time goes in v4:
time: 183 us; the launch traced here: 182 us
  blocking collectives  75.9 us (41%)
  starting transfers between devices  69 us (38%)
  waiting for transfers between devices  19.6 us (11%)
  Pallas kernels  9.53 us (5%)
  local copies, waits for them, and re-layouts  7.76 us (4%)
    all_to_all x4, blocking collectives, exchange(): return lax.all_to_all(value, axes, 0, 0, tiled=True)  70.7 us
    all_to_all x5, starting transfers between devices, exchange(): return lax.all_to_all(value, axes, 0, 0, tiled=True)  36.8 us
    ppermute x6, starting transfers between devices, shift_along(): return lax.ppermute(value, axis, [(i, (i + shift) % 4) for i in range(4)])  22.9 us
    all_to_all x5, waiting for transfers between devices, exchange(): return lax.all_to_all(value, axes, 0, 0, tiled=True)  9.36 us
    ppermute x2, starting transfers between devices, swap_cores(): return lax.ppermute(value, 'core', [(0, 1), (1, 0)])  9.33 us
    ppermute x6, waiting for transfers between devices, shift_along(): return lax.ppermute(value, axis, [(i, (i + shift) % 4) for i in range(4)])  7.88 us
    all_gather x1, blocking collectives, shards(): hidden = lax.all_gather(hidden, 'core', axis=0, tiled=False)  5.16 us
    unnamed x37, local copies, waits for them, and re-layouts  4.83 us
  transfers between devices with their start and end apart: 13, of which 8 were waited for; matrix products, arithmetic and copies ran while one was open for 1% of the time, Pallas kernels for 2%

profile of v4, /device:TPU:1, one launch (start us, length us, event | category | flops | bytes accessed | tf_op | source)
XLA Modules:
  0.0 182.3 jit_solution(8502891348169086918)
XLA Ops:
  0.0 0.8 copy-done.16
  0.9 0.7 copy-done.17
  1.6 0.8 pack_rows.1
  2.4 9.0 %all-to-all-start = ((bf16[16,24,512]{2,1,0:T(8,128)(2,1)}), bf16[16,24,512]{2,1,0:T(8,128)(2,1)S(1)}, u32[]{:S(2)}, u32[]{:S(2)}) async-start(bf16[16,24,512]{2,1,0:T(8,128)(2,1)} %pack_rows.1), calls=%async_computation | async-start | bytes 786432 | tf_op jit(solution)/shard_map/all_to_all | solution.py:17
  11.4 3.3 %collective-permute-start = (bf16[512,256]{1,0:T(8,128)(2,1)S(1)}, bf16[512,256]{1,0:T(8,128)(2,1)S(1)}, u32[]{:S(2)}, u32[]{:S(2)}) collective-permute-start(bf16[512,256]{1,0:T(8,128)(2,1)S(1)} %copy-done.6), channel_id=1, source_target_pairs={{0,16},{16,0},{1,17},{17,1},{2,18},{18,2},{3,19},{19,3},{4,20},{20... | collective-permute-start | bytes 786440 | tf_op jit(solution)/shard_map/ppermute | solution.py:25
  14.8 0.0 copy-start.1
  14.8 1.2 copy-done.1
  15.9 1.4 cut_weights.1
  17.3 2.7 %collective-permute-start.1 = (bf16[112,2048]{1,0:T(8,128)(2,1)}, bf16[112,2048]{1,0:T(8,128)(2,1)S(1)}, u32[]{:S(2)}, u32[]{:S(2)}) collective-permute-start(bf16[112,2048]{1,0:T(8,128)(2,1)} %get-tuple-element.27), channel_id=1, source_target_pairs={{0,4},{4,8},{8,12},{12,0},{1,5},{5,9},{9,13},{13,1},{2,6},{6,10},{... | collective-permute-start | bytes 1376264 | tf_op jit(solution)/shard_map/ppermute | solution.py:29
  20.1 3.7 %collective-permute-start.2 = (bf16[112,2048]{1,0:T(8,128)(2,1)}, bf16[112,2048]{1,0:T(8,128)(2,1)S(1)}, u32[]{:S(2)}, u32[]{:S(2)}) collective-permute-start(bf16[112,2048]{1,0:T(8,128)(2,1)} %get-tuple-element.28), channel_id=1, source_target_pairs={{0,12},{4,0},{8,4},{12,8},{1,13},{5,1},{9,5},{13,9},{2,14},{6,2},{... | collective-permute-start | bytes 1376264 | tf_op jit(solution)/shard_map/ppermute | solution.py:29
  23.8 0.1 pad_add_fusion.2.at_ref
  23.9 0.0 collective-permute-done.other_ref
  23.9 0.4 all-to-all-done.got_ref
  24.3 1.7 project.1
  26.0 4.2 %all-to-all-start.1 = ((bf16[4,128,256]{2,1,0:T(8,128)(2,1)}), bf16[4,128,256]{2,1,0:T(8,128)(2,1)S(1)}, u32[]{:S(2)}, u32[]{:S(2)}) async-start(bf16[4,128,256]{2,1,0:T(8,128)(2,1)} %project.1), calls=%async_computation.1 | async-start | bytes 524288 | tf_op jit(solution)/shard_map/all_to_all | solution.py:17
  30.2 2.2 %dynamic-slice_bitcast_fusion = (bf16[448,256]{1,0:T(8,128)(2,1)}, bf16[448,256]{1,0:T(8,128)(2,1)}, bf16[448,256]{1,0:T(8,128)(2,1)}, bf16[448,256]{1,0:T(8,128)(2,1)S(1)}) fusion(bf16[4,448,256]{2,1,0:T(8,128)(2,1)} %bitcast.26, s32[]{:T(128)S(6)} %select_n.39, s32[]{:T(128)S(6)} %select_n.37, s32[]{:T(128)S(6)} %select_n.35, s32[]{:T(128)S(6)} %select_n.33), kind=kLoop, calls=%fused_computation | loop fusion | bytes 1835024 | tf_op jit(solution)/shard_map/jit(dynamic_index_in_dim)/squeeze | solution.py:315
  32.4 3.4 %all-to-all-done.1.parts_ref = bf16[4,128,256]{2,1,0:T(8,128)(2,1)S(1)} async-done(((bf16[4,128,256]{2,1,0:T(8,128)(2,1)}), bf16[4,128,256]{2,1,0:T(8,128)(2,1)S(1)}, u32[]{:S(2)}, u32[]{:S(2)}) %all-to-all-start.1) | async-done | bytes 262176 | tf_op jit(solution)/shard_map/all_to_all | solution.py:17
  35.7 0.7 sum_and_replicate.2
  36.5 12.1 %all-to-all-start.2 = ((bf16[4,128,256]{2,1,0:T(8,128)(2,1)}), bf16[4,128,256]{2,1,0:T(8,128)(2,1)S(1)}, u32[]{:S(2)}, u32[]{:S(2)}) async-start(bf16[4,128,256]{2,1,0:T(8,128)(2,1)} %sum_and_replicate.2), calls=%async_computation.2 | async-start | bytes 524288 | tf_op jit(solution)/shard_map/all_to_all | solution.py:17
  48.6 4.2 %collective-permute-start.3 = (bf16[112,2048]{1,0:T(8,128)(2,1)S(1)}, bf16[112,2048]{1,0:T(8,128)(2,1)S(1)}, u32[]{:S(2)}, u32[]{:S(2)}) collective-permute-start(bf16[112,2048]{1,0:T(8,128)(2,1)S(1)} %get-tuple-element.32), channel_id=1, source_target_pairs={{0,8},{4,12},{8,0},{12,4},{1,9},{5,13},{9,1},{13,5},{2,10},{6,14},... | collective-permute-start | bytes 1376264 | tf_op jit(solution)/shard_map/ppermute | solution.py:29
  52.8 3.6 %collective-permute-start.4 = (bf16[448,256]{1,0:T(8,128)(2,1)}, bf16[448,256]{1,0:T(8,128)(2,1)S(1)}, u32[]{:S(2)}, u32[]{:S(2)}) collective-permute-start(bf16[448,256]{1,0:T(8,128)(2,1)} %get-tuple-element.33), channel_id=1, source_target_pairs={{0,128},{128,256},{256,384},{384,0},{1,129},{129,257},{257,385},{3... | collective-permute-start | bytes 688136 | tf_op jit(solution)/shard_map/ppermute | solution.py:29
  56.3 3.1 %collective-permute-start.5 = (bf16[448,256]{1,0:T(8,128)(2,1)}, bf16[448,256]{1,0:T(8,128)(2,1)S(1)}, u32[]{:S(2)}, u32[]{:S(2)}) collective-permute-start(bf16[448,256]{1,0:T(8,128)(2,1)} %get-tuple-element.34), channel_id=1, source_target_pairs={{0,384},{128,0},{256,128},{384,256},{1,385},{129,1},{257,129},{385... | collective-permute-start | bytes 688136 | tf_op jit(solution)/shard_map/ppermute | solution.py:29
  59.5 2.0 %collective-permute-done.4.rest_1_ = bf16[448,256]{1,0:T(8,128)(2,1)S(1)} collective-permute-done((bf16[448,256]{1,0:T(8,128)(2,1)}, bf16[448,256]{1,0:T(8,128)(2,1)S(1)}, u32[]{:S(2)}, u32[]{:S(2)}) %collective-permute-start.4) | collective-permute-done | bytes 229408 | tf_op jit(solution)/shard_map/ppermute | solution.py:29
  61.5 2.2 %collective-permute-done.5.rest_3_ = bf16[448,256]{1,0:T(8,128)(2,1)S(1)} collective-permute-done((bf16[448,256]{1,0:T(8,128)(2,1)}, bf16[448,256]{1,0:T(8,128)(2,1)S(1)}, u32[]{:S(2)}, u32[]{:S(2)}) %collective-permute-start.5) | collective-permute-done | bytes 229408 | tf_op jit(solution)/shard_map/ppermute | solution.py:29
  63.6 0.3 all-to-all-done.2.parts_ref
  63.9 0.8 carried_and_squares.1
  64.7 7.1 %all-to-all-start.3 = ((bf16[4,144,256]{2,1,0:T(8,128)(2,1)}), bf16[4,144,256]{2,1,0:T(8,128)(2,1)S(1)}, u32[]{:S(2)}, u32[]{:S(2)}) async-start(bf16[4,144,256]{2,1,0:T(8,128)(2,1)} %carried_and_squares.1), calls=%async_computation.3 | async-start | bytes 589824 | tf_op jit(solution)/shard_map/all_to_all | solution.py:17
  71.8 5.6 %collective-permute-start.6 = (bf16[448,256]{1,0:T(8,128)(2,1)}, bf16[448,256]{1,0:T(8,128)(2,1)S(1)}, u32[]{:S(2)}, u32[]{:S(2)}) collective-permute-start(bf16[448,256]{1,0:T(8,128)(2,1)} %get-tuple-element.38), channel_id=1, source_target_pairs={{0,256},{128,384},{256,0},{384,128},{1,257},{129,385},{257,1},{385... | collective-permute-start | bytes 688136 | tf_op jit(solution)/shard_map/ppermute | solution.py:29
  77.4 3.7 %collective-permute-done.6.rest_2_ = bf16[448,256]{1,0:T(8,128)(2,1)S(1)} collective-permute-done((bf16[448,256]{1,0:T(8,128)(2,1)}, bf16[448,256]{1,0:T(8,128)(2,1)S(1)}, u32[]{:S(2)}, u32[]{:S(2)}) %collective-permute-start.6) | collective-permute-done | bytes 229408 | tf_op jit(solution)/shard_map/ppermute | solution.py:29
  81.2 0.1 broadcast_in_dim.2
  81.3 17.5 %all_to_all.45 = bf16[4,4,144,256]{3,2,1,0:T(8,128)(2,1)S(1)} all-to-all(bf16[4,4,144,256]{3,2,1,0:T(8,128)(2,1)S(1)} %broadcast_in_dim.2), channel_id=1, replica_groups=mesh['x'=4,'zl'=4,'core'=2,'y'=4,'zh'=4] {'x'}, dimensions={0} | all-to-all | bytes 2359296 | tf_op jit(solution)/shard_map/all_to_all | solution.py:17
  98.8 6.0 %collective-permute-start.7 = (bf16[16,144,256]{2,1,0:T(8,128)(2,1)S(1)}, bf16[16,144,256]{2,1,0:T(8,128)(2,1)S(1)}, u32[]{:S(2)}, u32[]{:S(2)}) collective-permute-start(bf16[16,144,256]{2,1,0:T(8,128)(2,1)S(1)} %bitcast.21), channel_id=1, source_target_pairs={{0,16},{16,0},{1,17},{17,1},{2,18},{18,2},{3,19},{19,3},{4,20},{20... | collective-permute-start | bytes 3538952 | tf_op jit(solution)/shard_map/ppermute | solution.py:25
  104.8 0.1 pad_add_fusion.1.at_ref
  104.9 2.4 %collective-permute-done.7.other_ref = bf16[16,144,256]{2,1,0:T(8,128)(2,1)S(1)} collective-permute-done((bf16[16,144,256]{2,1,0:T(8,128)(2,1)S(1)}, bf16[16,144,256]{2,1,0:T(8,128)(2,1)S(1)}, u32[]{:S(2)}, u32[]{:S(2)}) %collective-permute-start.7) | collective-permute-done | bytes 1179680 | tf_op jit(solution)/shard_map/ppermute | solution.py:25
  107.3 1.0 copy-done.3
  108.3 1.0 copy-done.5
  109.3 1.9 %gate_up.1 = (bf16[4,128,512]{2,1,0:T(8,128)(2,1)S(1)}, bf16[128,512]{1,0:T(8,128)(2,1)S(1)}) custom-call(s32[3]{0:T(128)S(1)} %pad_add_fusion.1.at_ref, bf16[16,144,256]{2,1,0:T(8,128)(2,1)S(1)} %bitcast.22, bf16[16,144,256]{2,1,0:T(8,128)(2,1)S(1)} %collective-permute-done.7.other_ref, bf16[112,2048]{1,0:T(8,128)(2,1)S(1)} %get-tuple-element.40.rest_0_, ...), custom_call_target="tpu_custom_call" | custom-call | tf_op jit(solution)/shard_map/gate_up/pallas_call | solution.py:278
  111.2 12.6 %all_to_all.46.parts_ref = bf16[4,128,512]{2,1,0:T(8,128)(2,1)S(1)} all-to-all(bf16[4,128,512]{2,1,0:T(8,128)(2,1)S(1)} %get-tuple-element.44), channel_id=1, replica_groups=mesh['x'=4,'zl'=4,'core'=2,'y'=4,'zh'=4] {'y'}, dimensions={0} | all-to-all | bytes 1048576 | tf_op jit(solution)/shard_map/all_to_all | solution.py:17
  123.8 0.8 activate.1
  124.6 4.4 %all-to-all-start.6 = ((bf16[4,56,512]{2,1,0:T(8,128)(2,1)}), bf16[4,56,512]{2,1,0:T(8,128)(2,1)S(1)}, u32[]{:S(2)}, u32[]{:S(2)}) async-start(bf16[4,56,512]{2,1,0:T(8,128)(2,1)} %activate.1), calls=%async_computation.6 | async-start | bytes 458752 | tf_op jit(solution)/shard_map/all_to_all | solution.py:17
  128.9 0.1 pad_add_fusion.at_ref
  129.0 5.3 %all-to-all-done.6 = bf16[4,56,512]{2,1,0:T(8,128)(2,1)S(1)} async-done(((bf16[4,56,512]{2,1,0:T(8,128)(2,1)}), bf16[4,56,512]{2,1,0:T(8,128)(2,1)S(1)}, u32[]{:S(2)}, u32[]{:S(2)}) %all-to-all-start.6) | async-done | bytes 229408 | tf_op jit(solution)/shard_map/all_to_all | solution.py:17
  134.3 5.2 %all-gather = bf16[8,56,512]{2,1,0:T(8,128)(2,1)S(1)} all-gather(bf16[4,56,512]{2,1,0:T(8,128)(2,1)S(1)} %all-to-all-done.6), channel_id=2, replica_groups=mesh['x'=4,'zl'=4,'core'=2,'y'=4,'zh'=4] {'core'}, dimensions={0}, use_global_device_ids=true | all-gather | bytes 688128 | tf_op jit(solution)/shard_map/all_gather | solution.py:348
  139.5 1.3 down.1
  140.8 18.6 %all_to_all.47.parts_ref = bf16[16,32,1024]{2,1,0:T(8,128)(2,1)S(1)} all-to-all(bf16[16,32,1024]{2,1,0:T(8,128)(2,1)S(1)} %down.1), channel_id=1, replica_groups=mesh['x'=4,'zl'=4,'core'=2,'y'=4,'zh'=4] {'x','y'}, dimensions={0} | all-to-all | bytes 2097152 | tf_op jit(solution)/shard_map/all_to_all | solution.py:17
  159.5 0.1 sum_and_replicate.3
  159.6 22.0 %all_to_all.48 = bf16[32,8,128]{2,1,0:T(8,128)(2,1)S(1)} all-to-all(bf16[32,8,128]{2,1,0:T(8,128)(2,1)S(1)} %bitcast.27), channel_id=1, replica_groups=mesh['x'=4,'zl'=4,'core'=2,'y'=4,'zh'=4] {'core','zl','zh'}, dimensions={0} | all-to-all | bytes 131072 | tf_op jit(solution)/shard_map/all_to_all | solution.py:17
  181.7 0.6 convert_element_type.27
  (38 shorter events, 0.2 us)
Async XLA Ops:
  0.0 11.4 %copy-start.6 = (bf16[512,256]{1,0:T(8,128)(2,1)S(1)}, bf16[512,256]{1,0:T(8,128)(2,1)}, u32[]{:S(2)}) copy-start(bf16[512,256]{1,0:T(8,128)(2,1)} %own_ref.1) | copy-start | bytes 786436
  0.0 14.7 %copy-start = (bf16[56,8192]{1,0:T(8,128)(2,1)S(1)}, bf16[56,8192]{1,0:T(8,128)(2,1)}, u32[]{:S(2)}) copy-start(bf16[56,8192]{1,0:T(8,128)(2,1)} %gate_ref.1) | copy-start | bytes 2752516
  0.0 14.7 %copy-start.15 = (f32[8192]{0:T(1024)S(1)}, f32[8192]{0:T(1024)}, u32[]{:S(2)}) copy-start(f32[8192]{0:T(1024)} %param.10) | copy-start | bytes 98308
  0.0 0.9 copy-start.16
  0.9 0.7 copy-start.17
  2.4 21.9 %all-to-all-start = ((bf16[16,24,512]{2,1,0:T(8,128)(2,1)}), bf16[16,24,512]{2,1,0:T(8,128)(2,1)S(1)}, u32[]{:S(2)}, u32[]{:S(2)}) async-start(bf16[16,24,512]{2,1,0:T(8,128)(2,1)} %pack_rows.1), calls=%async_computation | async-start | bytes 786432 | tf_op jit(solution)/shard_map/all_to_all | solution.py:17
  11.4 12.5 %collective-permute-start = (bf16[512,256]{1,0:T(8,128)(2,1)S(1)}, bf16[512,256]{1,0:T(8,128)(2,1)S(1)}, u32[]{:S(2)}, u32[]{:S(2)}) collective-permute-start(bf16[512,256]{1,0:T(8,128)(2,1)S(1)} %copy-done.6), channel_id=1, source_target_pairs={{0,16},{16,0},{1,17},{17,1},{2,18},{18,2},{3,19},{19,3},{4,20},{20... | collective-permute-start | bytes 786440 | tf_op jit(solution)/shard_map/ppermute | solution.py:25
  14.8 1.2 copy-start.1
  17.3 19.2 %collective-permute-start.1 = (bf16[112,2048]{1,0:T(8,128)(2,1)}, bf16[112,2048]{1,0:T(8,128)(2,1)S(1)}, u32[]{:S(2)}, u32[]{:S(2)}) collective-permute-start(bf16[112,2048]{1,0:T(8,128)(2,1)} %get-tuple-element.27), channel_id=1, source_target_pairs={{0,4},{4,8},{8,12},{12,0},{1,5},{5,9},{9,13},{13,1},{2,6},{6,10},{... | collective-permute-start | bytes 1376264 | tf_op jit(solution)/shard_map/ppermute | solution.py:29
  20.1 16.4 %collective-permute-start.2 = (bf16[112,2048]{1,0:T(8,128)(2,1)}, bf16[112,2048]{1,0:T(8,128)(2,1)S(1)}, u32[]{:S(2)}, u32[]{:S(2)}) collective-permute-start(bf16[112,2048]{1,0:T(8,128)(2,1)} %get-tuple-element.28), channel_id=1, source_target_pairs={{0,12},{4,0},{8,4},{12,8},{1,13},{5,1},{9,5},{13,9},{2,14},{6,2},{... | collective-permute-start | bytes 1376264 | tf_op jit(solution)/shard_map/ppermute | solution.py:29
  26.0 9.7 %all-to-all-start.1 = ((bf16[4,128,256]{2,1,0:T(8,128)(2,1)}), bf16[4,128,256]{2,1,0:T(8,128)(2,1)S(1)}, u32[]{:S(2)}, u32[]{:S(2)}) async-start(bf16[4,128,256]{2,1,0:T(8,128)(2,1)} %project.1), calls=%async_computation.1 | async-start | bytes 524288 | tf_op jit(solution)/shard_map/all_to_all | solution.py:17
  36.5 44.6 %copy-start.2 = (bf16[112,2048]{1,0:T(8,128)(2,1)}, bf16[112,2048]{1,0:T(8,128)(2,1)S(1)}, u32[]{:S(2)}) copy-start(bf16[112,2048]{1,0:T(8,128)(2,1)S(1)} %collective-permute-done.2.rest_3_) | copy-start | bytes 1376260
  36.5 27.4 %all-to-all-start.2 = ((bf16[4,128,256]{2,1,0:T(8,128)(2,1)}), bf16[4,128,256]{2,1,0:T(8,128)(2,1)S(1)}, u32[]{:S(2)}, u32[]{:S(2)}) async-start(bf16[4,128,256]{2,1,0:T(8,128)(2,1)} %sum_and_replicate.2), calls=%async_computation.2 | async-start | bytes 524288 | tf_op jit(solution)/shard_map/all_to_all | solution.py:17
  48.6 15.0 %collective-permute-start.3 = (bf16[112,2048]{1,0:T(8,128)(2,1)S(1)}, bf16[112,2048]{1,0:T(8,128)(2,1)S(1)}, u32[]{:S(2)}, u32[]{:S(2)}) collective-permute-start(bf16[112,2048]{1,0:T(8,128)(2,1)S(1)} %get-tuple-element.32), channel_id=1, source_target_pairs={{0,8},{4,12},{8,0},{12,4},{1,9},{5,13},{9,1},{13,5},{2,10},{6,14},... | collective-permute-start | bytes 1376264 | tf_op jit(solution)/shard_map/ppermute | solution.py:29
  52.8 8.7 %collective-permute-start.4 = (bf16[448,256]{1,0:T(8,128)(2,1)}, bf16[448,256]{1,0:T(8,128)(2,1)S(1)}, u32[]{:S(2)}, u32[]{:S(2)}) collective-permute-start(bf16[448,256]{1,0:T(8,128)(2,1)} %get-tuple-element.33), channel_id=1, source_target_pairs={{0,128},{128,256},{256,384},{384,0},{1,129},{129,257},{257,385},{3... | collective-permute-start | bytes 688136 | tf_op jit(solution)/shard_map/ppermute | solution.py:29
  56.3 7.3 %collective-permute-start.5 = (bf16[448,256]{1,0:T(8,128)(2,1)}, bf16[448,256]{1,0:T(8,128)(2,1)S(1)}, u32[]{:S(2)}, u32[]{:S(2)}) collective-permute-start(bf16[448,256]{1,0:T(8,128)(2,1)} %get-tuple-element.34), channel_id=1, source_target_pairs={{0,384},{128,0},{256,128},{384,256},{1,385},{129,1},{257,129},{385... | collective-permute-start | bytes 688136 | tf_op jit(solution)/shard_map/ppermute | solution.py:29
  61.5 19.8 %copy-start.7 = (bf16[448,256]{1,0:T(8,128)(2,1)}, bf16[448,256]{1,0:T(8,128)(2,1)S(1)}, u32[]{:S(2)}) copy-start(bf16[448,256]{1,0:T(8,128)(2,1)S(1)} %collective-permute-done.4.rest_1_) | copy-start | bytes 688132
  63.6 17.6 %copy-start.9 = (bf16[448,256]{1,0:T(8,128)(2,1)}, bf16[448,256]{1,0:T(8,128)(2,1)S(1)}, u32[]{:S(2)}) copy-start(bf16[448,256]{1,0:T(8,128)(2,1)S(1)} %collective-permute-done.5.rest_3_) | copy-start | bytes 688132
  63.6 17.5 %copy-start.4 = (bf16[112,2048]{1,0:T(8,128)(2,1)}, bf16[112,2048]{1,0:T(8,128)(2,1)S(1)}, u32[]{:S(2)}) copy-start(bf16[112,2048]{1,0:T(8,128)(2,1)S(1)} %collective-permute-done.3.rest_2_) | copy-start | bytes 1376260
  64.7 16.4 %all-to-all-start.3 = ((bf16[4,144,256]{2,1,0:T(8,128)(2,1)}), bf16[4,144,256]{2,1,0:T(8,128)(2,1)S(1)}, u32[]{:S(2)}, u32[]{:S(2)}) async-start(bf16[4,144,256]{2,1,0:T(8,128)(2,1)} %carried_and_squares.1), calls=%async_computation.3 | async-start | bytes 589824 | tf_op jit(solution)/shard_map/all_to_all | solution.py:17
  71.8 9.4 %collective-permute-start.6 = (bf16[448,256]{1,0:T(8,128)(2,1)}, bf16[448,256]{1,0:T(8,128)(2,1)S(1)}, u32[]{:S(2)}, u32[]{:S(2)}) collective-permute-start(bf16[448,256]{1,0:T(8,128)(2,1)} %get-tuple-element.38), channel_id=1, source_target_pairs={{0,256},{128,384},{256,0},{384,128},{1,257},{129,385},{257,1},{385... | collective-permute-start | bytes 688136 | tf_op jit(solution)/shard_map/ppermute | solution.py:29
  81.1 17.7 %copy-start.11 = (bf16[448,256]{1,0:T(8,128)(2,1)}, bf16[448,256]{1,0:T(8,128)(2,1)S(1)}, u32[]{:S(2)}) copy-start(bf16[448,256]{1,0:T(8,128)(2,1)S(1)} %collective-permute-done.6.rest_2_) | copy-start | bytes 688132
  98.8 8.5 %collective-permute-start.7 = (bf16[16,144,256]{2,1,0:T(8,128)(2,1)S(1)}, bf16[16,144,256]{2,1,0:T(8,128)(2,1)S(1)}, u32[]{:S(2)}, u32[]{:S(2)}) collective-permute-start(bf16[16,144,256]{2,1,0:T(8,128)(2,1)S(1)} %bitcast.21), channel_id=1, source_target_pairs={{0,16},{16,0},{1,17},{17,1},{2,18},{18,2},{3,19},{19,3},{4,20},{20... | collective-permute-start | bytes 3538952 | tf_op jit(solution)/shard_map/ppermute | solution.py:25
  107.3 1.0 copy-start.3
  108.3 1.0 copy-start.5
  111.2 12.6 %copy-start.13 = (bf16[128,512]{1,0:T(8,128)(2,1)}, bf16[128,512]{1,0:T(8,128)(2,1)S(1)}, u32[]{:S(2)}) copy-start(bf16[128,512]{1,0:T(8,128)(2,1)S(1)} %get-tuple-element.45.kept_ref) | copy-start | bytes 393220
  123.8 15.7 %copy-start.8 = (bf16[448,256]{1,0:T(8,128)(2,1)S(1)}, bf16[448,256]{1,0:T(8,128)(2,1)}, u32[]{:S(2)}) copy-start(bf16[448,256]{1,0:T(8,128)(2,1)} %copy-done.7) | copy-start | bytes 688132
  123.8 15.7 %copy-start.10 = (bf16[448,256]{1,0:T(8,128)(2,1)S(1)}, bf16[448,256]{1,0:T(8,128)(2,1)}, u32[]{:S(2)}) copy-start(bf16[448,256]{1,0:T(8,128)(2,1)} %copy-done.9) | copy-start | bytes 688132
  123.8 15.7 %copy-start.12 = (bf16[448,256]{1,0:T(8,128)(2,1)S(1)}, bf16[448,256]{1,0:T(8,128)(2,1)}, u32[]{:S(2)}) copy-start(bf16[448,256]{1,0:T(8,128)(2,1)} %copy-done.11) | copy-start | bytes 688132
  124.6 14.9 %copy-start.14 = (bf16[128,512]{1,0:T(8,128)(2,1)S(1)}, bf16[128,512]{1,0:T(8,128)(2,1)}, u32[]{:S(2)}) copy-start(bf16[128,512]{1,0:T(8,128)(2,1)} %copy-done.13) | copy-start | bytes 393220
  124.6 9.7 %all-to-all-start.6 = ((bf16[4,56,512]{2,1,0:T(8,128)(2,1)}), bf16[4,56,512]{2,1,0:T(8,128)(2,1)S(1)}, u32[]{:S(2)}, u32[]{:S(2)}) async-start(bf16[4,56,512]{2,1,0:T(8,128)(2,1)} %activate.1), calls=%async_computation.6 | async-start | bytes 458752 | tf_op jit(solution)/shard_map/all_to_all | solution.py:17

commit v5 on v4

--- a/solution.py
+++ b/solution.py
@@ -53,7 +53,7 @@
         out_shape=jax.ShapeDtypeStruct((X * ZL, rows, heads), BF16),
         in_specs=[vmem(), vmem()],
         out_specs=vmem(),
-        compiler_params=pltpu.CompilerParams(vmem_limit_bytes=4 * 1024 * 1024),
+        compiler_params=pltpu.CompilerParams(vmem_limit_bytes=56 * 1024 * 1024),
         name="pack_rows",
     )(attention_out, residual)
 
@@ -245,52 +245,58 @@
     )(parts)
 
 
-def gate_up(own, other, pieces, at):
-    blocks, rows, half = own.shape
+def gate_up(spread, pieces, at, done=None):
+    blocks, rows, half = spread.shape
     part = rows - EXTRA
     both, depth = pieces[0].shape
-
-    def kernel(at_ref, own_ref, other_ref, *rest):
-        piece_refs, out_ref, carried_ref = rest[:Y], rest[Y], rest[Y + 1]
-        weights, rhs, tails = rest[Y + 2 :]
+    width = half if done is None else CORES * half
+
+    def kernel(at_ref, spread_ref, *rest):
+        piece_refs, rest = rest[:Y], rest[Y:]
+        if done is not None:
+            done_refs, rest = rest[:2], rest[2:]
+        out_ref, carried_ref, weights, rhs = rest
         y, core, mine = at_ref[0], at_ref[1], at_ref[2]
+        place = slice(None)
+        if done is not None:
+            own = pl.ds(pl.multiple_of(core * half, half), half)
+            place = pl.ds(pl.multiple_of((1 - core) * half, half), half)
+            out_ref[:, :, own] = done_refs[0][...]
+            carried_ref[:, own] = done_refs[1][...]
         for shift in range(Y):
             to = lax.rem(y - shift + Y, Y)
             weights[pl.ds(pl.multiple_of(to * both, both), both), :] = piece_refs[shift][...]
-        for turn, ref in enumerate((own_ref, other_ref)):
-            side = core if turn == 0 else 1 - core
-            place = pl.ds(pl.multiple_of(side * half, half), half)
-            square = jnp.zeros((2, half), F32)
-            for block in range(blocks):
-                rhs[block * part : (block + 1) * part, place] = ref[block, :part, :]
-                square = square + ref[block, part : part + 2, :].astype(F32)
-            square = square[0:1] + square[1:2]
-            high = square.astype(BF16).astype(F32)
-            tails[:, place] = jnp.concatenate(
-                [high, square - high, jnp.zeros((EXTRA - 2, half), F32)], axis=0
-            ).astype(BF16)
-            carried_ref[:, place] = ref[mine, :part, :]
+        square = jnp.zeros((2, half), F32)
+        for block in range(blocks):
+            rhs[block * part : (block + 1) * part, :] = spread_ref[block, :part, :]
+            square = square + spread_ref[block, part : part + 2, :].astype(F32)
+        square = square[0:1] + square[1:2]
+        high = square.astype(BF16).astype(F32)
+        tail = jnp.concatenate(
+            [high, square - high, jnp.zeros((EXTRA - 2, half), F32)], axis=0
+        ).astype(BF16)
+        carried_ref[:, place] = spread_ref[mine, :part, :]
         total = jnp.dot(weights[...], rhs[...], preferred_element_type=F32)
         for to in range(Y):
-            out_ref[to, :both, :] = total[to * both : (to + 1) * both].astype(BF16)
-            out_ref[to, both:, :] = tails[...]
-
+            out_ref[to, :both, place] = total[to * both : (to + 1) * both].astype(BF16)
+            out_ref[to, both:, place] = tail
+
+    extra = () if done is None else tuple(done)
     return pl.pallas_call(
         kernel,
         out_shape=[
-            jax.ShapeDtypeStruct((Y, both + EXTRA, CORES * half), BF16),
-            jax.ShapeDtypeStruct((part, CORES * half), BF16),
+            jax.ShapeDtypeStruct((Y, both + EXTRA, width), BF16),
+            jax.ShapeDtypeStruct((part, width), BF16),
         ],
-        in_specs=[smem(), vmem(), vmem()] + [vmem()] * Y,
+        in_specs=[smem(), vmem()] + [vmem()] * (Y + len(extra)),
         out_specs=[vmem(), vmem()],
         scratch_shapes=[
             pltpu.VMEM((Y * both, depth), BF16),
-            pltpu.VMEM((depth, CORES * half), BF16),
-            pltpu.VMEM((EXTRA, CORES * half), BF16),
+            pltpu.VMEM((depth, half), BF16),
         ],
         compiler_params=pltpu.CompilerParams(vmem_limit_bytes=8 * 1024 * 1024),
-        name="gate_up",
-    )(at, own, other, *pieces)
+        name="gate_up" if done is None else "gate_up_both",
+    )(at, spread, *pieces, *extra)
 
 
 def shards(attention_out, w_out, residual, norm_gain, w_gate, w_up, w_down):
@@ -338,12 +344,9 @@
     )
     spread = exchange(replicate(spread, X), "x")
     spread = spread.reshape(blocks, part + EXTRA, half)
-    outs, kept = gate_up(
-        spread,
-        swap_cores(spread),
-        pieces,
-        jnp.stack([y_at, core_at, x_at * ZL + zl_at]),
-    )
+    other = swap_cores(spread)
+    at = jnp.stack([y_at, core_at, x_at * ZL + zl_at])
+    outs, kept = gate_up(other, pieces, at, gate_up(spread, pieces, at))
     hidden = exchange(activate(exchange(outs, "y"), d, ZL), "zl")
     hidden = lax.all_gather(hidden, "core", axis=0, tiled=False)
     by_owner = down(

time: 183 us -> 182 us (level)
  Pallas kernels: 9.53 us -> 11.9 us
  blocking collectives: 75.9 us -> 73.6 us
  starting transfers between devices: 69 us -> 71.3 us
  local copies, waits for them, and re-layouts: 7.76 us -> 5.58 us
    all_to_all x4, blocking collectives: 70.7 us -> 68.4 us  [exchange(): return lax.all_to_all(value, axes, 0, 0, tiled=True)]
    unnamed x37 -> x21, local copies, waits for them, and re-layouts: 4.83 us -> 2.66 us
    ppermute x6, starting transfers between devices: 22.9 us -> 24.9 us  [shift_along(): return lax.ppermute(value, axis, [(i, (i + shift) % 4) for i in range(4)])]
  transfers between devices with their start and end apart: 13 -> 13, of which waited for: 8 -> 6; matrix products, arithmetic and copies ran while one was open for 1% -> 1% of each run, Pallas kernels for 2% -> 3%
where the time goes in v5:
time: 182 us; the launch traced here: 181 us
  blocking collectives  73.6 us (40%)
  starting transfers between devices  71.3 us (39%)
  waiting for transfers between devices  17.8 us (10%)
  Pallas kernels  11.9 us (7%)
  local copies, waits for them, and re-layouts  5.58 us (3%)
    all_to_all x4, blocking collectives, exchange(): return lax.all_to_all(value, axes, 0, 0, tiled=True)  68.4 us
    all_to_all x5, starting transfers between devices, exchange(): return lax.all_to_all(value, axes, 0, 0, tiled=True)  36.4 us
    ppermute x6, starting transfers between devices, shift_along(): return lax.ppermute(value, axis, [(i, (i + shift) % 4) for i in range(4)])  24.9 us
    ppermute x2, starting transfers between devices, swap_cores(): return lax.ppermute(value, 'core', [(0, 1), (1, 0)])  9.96 us
    all_to_all x5, waiting for transfers between devices, exchange(): return lax.all_to_all(value, axes, 0, 0, tiled=True)  8.72 us
    ppermute x6, waiting for transfers between devices, shift_along(): return lax.ppermute(value, axis, [(i, (i + shift) % 4) for i in range(4)])  7.91 us
    all_gather x1, blocking collectives, shards(): hidden = lax.all_gather(hidden, 'core', axis=0, tiled=False)  5.16 us
  transfers between devices with their start and end apart: 13, of which 6 were waited for; matrix products, arithmetic and copies ran while one was open for 1% of the time, Pallas kernels for 3%

profile of v5, /device:TPU:1, one launch (start us, length us, event | category | flops | bytes accessed | tf_op | source)
XLA Modules:
  0.0 180.5 jit_solution(13432913293914565468)
XLA Ops:
  0.0 1.7 pack_rows.1
  1.7 9.0 %all-to-all-start = ((bf16[16,24,512]{2,1,0:T(8,128)(2,1)}), bf16[16,24,512]{2,1,0:T(8,128)(2,1)S(1)}, u32[]{:S(2)}, u32[]{:S(2)}) async-start(bf16[16,24,512]{2,1,0:T(8,128)(2,1)} %pack_rows.1), calls=%async_computation | async-start | bytes 786432 | tf_op jit(solution)/shard_map/all_to_all | solution.py:17
  10.7 3.3 %collective-permute-start = (bf16[512,256]{1,0:T(8,128)(2,1)S(1)}, bf16[512,256]{1,0:T(8,128)(2,1)S(1)}, u32[]{:S(2)}, u32[]{:S(2)}) collective-permute-start(bf16[512,256]{1,0:T(8,128)(2,1)S(1)} %copy-done.2), channel_id=1, source_target_pairs={{0,16},{16,0},{1,17},{17,1},{2,18},{18,2},{3,19},{19,3},{4,20},{20... | collective-permute-start | bytes 786440 | tf_op jit(solution)/shard_map/ppermute | solution.py:25
  14.1 0.0 copy-start.1
  14.1 1.2 copy-done.1
  15.2 1.2 cut_weights.1
  16.5 0.8 copy-done.8
  17.2 2.7 %collective-permute-start.1 = (bf16[112,2048]{1,0:T(8,128)(2,1)}, bf16[112,2048]{1,0:T(8,128)(2,1)S(1)}, u32[]{:S(2)}, u32[]{:S(2)}) collective-permute-start(bf16[112,2048]{1,0:T(8,128)(2,1)} %get-tuple-element.29), channel_id=1, source_target_pairs={{0,4},{4,8},{8,12},{12,0},{1,5},{5,9},{9,13},{13,1},{2,6},{6,10},{... | collective-permute-start | bytes 1376264 | tf_op jit(solution)/shard_map/ppermute | solution.py:29
  20.0 3.7 %collective-permute-start.2 = (bf16[112,2048]{1,0:T(8,128)(2,1)S(1)}, bf16[112,2048]{1,0:T(8,128)(2,1)S(1)}, u32[]{:S(2)}, u32[]{:S(2)}) collective-permute-start(bf16[112,2048]{1,0:T(8,128)(2,1)S(1)} %get-tuple-element.30), channel_id=1, source_target_pairs={{0,12},{4,0},{8,4},{12,8},{1,13},{5,1},{9,5},{13,9},{2,14},{6,2},{... | collective-permute-start | bytes 1376264 | tf_op jit(solution)/shard_map/ppermute | solution.py:29
  23.7 0.1 pad_add_fusion.2.at_ref
  23.8 0.0 collective-permute-done.other_ref
  23.8 0.0 all-to-all-done.got_ref
  23.8 1.7 project.1
  25.5 4.0 %all-to-all-start.1 = ((bf16[4,128,256]{2,1,0:T(8,128)(2,1)}), bf16[4,128,256]{2,1,0:T(8,128)(2,1)S(1)}, u32[]{:S(2)}, u32[]{:S(2)}) async-start(bf16[4,128,256]{2,1,0:T(8,128)(2,1)} %project.1), calls=%async_computation.1 | async-start | bytes 524288 | tf_op jit(solution)/shard_map/all_to_all | solution.py:17
  29.5 2.2 %dynamic-slice_bitcast_fusion = (bf16[448,256]{1,0:T(8,128)(2,1)}, bf16[448,256]{1,0:T(8,128)(2,1)S(1)}, bf16[448,256]{1,0:T(8,128)(2,1)}, bf16[448,256]{1,0:T(8,128)(2,1)S(1)}) fusion(bf16[4,448,256]{2,1,0:T(8,128)(2,1)} %bitcast.26, s32[]{:T(128)S(6)} %select_n.39, s32[]{:T(128)S(6)} %select_n.37, s32[]{:T(128)S(6)} %select_n.35, s32[]{:T(128)S(6)} %select_n.33), kind=kLoop, calls=%fused_computation | loop fusion | bytes 1835024 | tf_op jit(solution)/shard_map/jit(dynamic_index_in_dim)/squeeze | solution.py:321
  31.7 3.4 %all-to-all-done.1.parts_ref = bf16[4,128,256]{2,1,0:T(8,128)(2,1)S(1)} async-done(((bf16[4,128,256]{2,1,0:T(8,128)(2,1)}), bf16[4,128,256]{2,1,0:T(8,128)(2,1)S(1)}, u32[]{:S(2)}, u32[]{:S(2)}) %all-to-all-start.1) | async-done | bytes 262176 | tf_op jit(solution)/shard_map/all_to_all | solution.py:17
  35.1 0.7 sum_and_replicate.2
  35.8 0.0 collective-permute-done.1.rest_1_
  35.8 12.1 %all-to-all-start.2 = ((bf16[4,128,256]{2,1,0:T(8,128)(2,1)}), bf16[4,128,256]{2,1,0:T(8,128)(2,1)S(1)}, u32[]{:S(2)}, u32[]{:S(2)}) async-start(bf16[4,128,256]{2,1,0:T(8,128)(2,1)} %sum_and_replicate.2), calls=%async_computation.2 | async-start | bytes 524288 | tf_op jit(solution)/shard_map/all_to_all | solution.py:17
  47.9 4.5 %collective-permute-start.3 = (bf16[112,2048]{1,0:T(8,128)(2,1)S(1)}, bf16[112,2048]{1,0:T(8,128)(2,1)S(1)}, u32[]{:S(2)}, u32[]{:S(2)}) collective-permute-start(bf16[112,2048]{1,0:T(8,128)(2,1)S(1)} %copy-done.9), channel_id=1, source_target_pairs={{0,8},{4,12},{8,0},{12,4},{1,9},{5,13},{9,1},{13,5},{2,10},{6,14},... | collective-permute-start | bytes 1376264 | tf_op jit(solution)/shard_map/ppermute | solution.py:29
  52.5 3.6 %collective-permute-start.4 = (bf16[448,256]{1,0:T(8,128)(2,1)}, bf16[448,256]{1,0:T(8,128)(2,1)S(1)}, u32[]{:S(2)}, u32[]{:S(2)}) collective-permute-start(bf16[448,256]{1,0:T(8,128)(2,1)} %get-tuple-element.35), channel_id=1, source_target_pairs={{0,128},{128,256},{256,384},{384,0},{1,129},{129,257},{257,385},{3... | collective-permute-start | bytes 688136 | tf_op jit(solution)/shard_map/ppermute | solution.py:29
  56.0 3.1 %collective-permute-start.5 = (bf16[448,256]{1,0:T(8,128)(2,1)}, bf16[448,256]{1,0:T(8,128)(2,1)S(1)}, u32[]{:S(2)}, u32[]{:S(2)}) collective-permute-start(bf16[448,256]{1,0:T(8,128)(2,1)} %get-tuple-element.36), channel_id=1, source_target_pairs={{0,384},{128,0},{256,128},{384,256},{1,385},{129,1},{257,129},{385... | collective-permute-start | bytes 688136 | tf_op jit(solution)/shard_map/ppermute | solution.py:29
  59.2 2.0 %collective-permute-done.4.rest_1_ = bf16[448,256]{1,0:T(8,128)(2,1)S(1)} collective-permute-done((bf16[448,256]{1,0:T(8,128)(2,1)}, bf16[448,256]{1,0:T(8,128)(2,1)S(1)}, u32[]{:S(2)}, u32[]{:S(2)}) %collective-permute-start.4) | collective-permute-done | bytes 229408 | tf_op jit(solution)/shard_map/ppermute | solution.py:29
  61.1 2.2 %collective-permute-done.5.rest_3_ = bf16[448,256]{1,0:T(8,128)(2,1)S(1)} collective-permute-done((bf16[448,256]{1,0:T(8,128)(2,1)}, bf16[448,256]{1,0:T(8,128)(2,1)S(1)}, u32[]{:S(2)}, u32[]{:S(2)}) %collective-permute-start.5) | collective-permute-done | bytes 229408 | tf_op jit(solution)/shard_map/ppermute | solution.py:29
  63.3 0.0 collective-permute-done.3.rest_2_
  63.3 0.8 carried_and_squares.1
  64.1 7.1 %all-to-all-start.3 = ((bf16[4,144,256]{2,1,0:T(8,128)(2,1)}), bf16[4,144,256]{2,1,0:T(8,128)(2,1)S(1)}, u32[]{:S(2)}, u32[]{:S(2)}) async-start(bf16[4,144,256]{2,1,0:T(8,128)(2,1)} %carried_and_squares.1), calls=%async_computation.3 | async-start | bytes 589824 | tf_op jit(solution)/shard_map/all_to_all | solution.py:17
  71.2 7.2 %collective-permute-start.6 = (bf16[448,256]{1,0:T(8,128)(2,1)S(1)}, bf16[448,256]{1,0:T(8,128)(2,1)S(1)}, u32[]{:S(2)}, u32[]{:S(2)}) collective-permute-start(bf16[448,256]{1,0:T(8,128)(2,1)S(1)} %get-tuple-element.40), channel_id=1, source_target_pairs={{0,256},{128,384},{256,0},{384,128},{1,257},{129,385},{257,1},{385... | collective-permute-start | bytes 688136 | tf_op jit(solution)/shard_map/ppermute | solution.py:29
  78.4 3.8 %collective-permute-done.6.rest_2_ = bf16[448,256]{1,0:T(8,128)(2,1)S(1)} collective-permute-done((bf16[448,256]{1,0:T(8,128)(2,1)S(1)}, bf16[448,256]{1,0:T(8,128)(2,1)S(1)}, u32[]{:S(2)}, u32[]{:S(2)}) %collective-permute-start.6) | collective-permute-done | bytes 229408 | tf_op jit(solution)/shard_map/ppermute | solution.py:29
  82.2 0.7 copy-done.5
  82.9 0.1 broadcast_in_dim.2
  82.9 16.4 %all_to_all.45 = bf16[4,4,144,256]{3,2,1,0:T(8,128)(2,1)S(1)} all-to-all(bf16[4,4,144,256]{3,2,1,0:T(8,128)(2,1)S(1)} %broadcast_in_dim.2), channel_id=1, replica_groups=mesh['x'=4,'zl'=4,'core'=2,'y'=4,'zh'=4] {'x'}, dimensions={0} | all-to-all | bytes 2359296 | tf_op jit(solution)/shard_map/all_to_all | solution.py:17
  99.3 6.6 %collective-permute-start.7 = (bf16[16,144,256]{2,1,0:T(8,128)(2,1)S(1)}, bf16[16,144,256]{2,1,0:T(8,128)(2,1)}, u32[]{:S(2)}, u32[]{:S(2)}) collective-permute-start(bf16[16,144,256]{2,1,0:T(8,128)(2,1)S(1)} %bitcast.21), channel_id=1, source_target_pairs={{0,16},{16,0},{1,17},{17,1},{2,18},{18,2},{3,19},{19,3},{4,20},{20... | collective-permute-start | bytes 3538952 | tf_op jit(solution)/shard_map/ppermute | solution.py:25
  106.0 0.1 pad_add_fusion.1.at_ref
  106.0 1.4 gate_up.1
  107.4 1.1 collective-permute-done.7.spread_ref
  108.5 2.1 %gate_up_both.1 = (bf16[4,128,512]{2,1,0:T(8,128)(2,1)S(1)}, bf16[128,512]{1,0:T(8,128)(2,1)S(1)}) custom-call(s32[3]{0:T(128)S(1)} %pad_add_fusion.1.at_ref, bf16[16,144,256]{2,1,0:T(8,128)(2,1)} %collective-permute-done.7.spread_ref, bf16[112,2048]{1,0:T(8,128)(2,1)S(1)} %get-tuple-element.42.rest_0_, ...), custom_call_target="tpu_custom_call" | custom-call | tf_op jit(solution)/shard_map/gate_up_both/pallas_call | solution.py:285
  110.6 11.6 %all_to_all.46.parts_ref = bf16[4,128,512]{2,1,0:T(8,128)(2,1)S(1)} all-to-all(bf16[4,128,512]{2,1,0:T(8,128)(2,1)S(1)} %get-tuple-element.48), channel_id=1, replica_groups=mesh['x'=4,'zl'=4,'core'=2,'y'=4,'zh'=4] {'y'}, dimensions={0} | all-to-all | bytes 1048576 | tf_op jit(solution)/shard_map/all_to_all | solution.py:17
  122.2 0.8 activate.1
  123.0 4.2 %all-to-all-start.6 = ((bf16[4,56,512]{2,1,0:T(8,128)(2,1)}), bf16[4,56,512]{2,1,0:T(8,128)(2,1)S(1)}, u32[]{:S(2)}, u32[]{:S(2)}) async-start(bf16[4,56,512]{2,1,0:T(8,128)(2,1)} %activate.1), calls=%async_computation.6 | async-start | bytes 458752 | tf_op jit(solution)/shard_map/all_to_all | solution.py:17
  127.2 0.1 pad_add_fusion.at_ref
  127.3 5.3 %all-to-all-done.6 = bf16[4,56,512]{2,1,0:T(8,128)(2,1)S(1)} async-done(((bf16[4,56,512]{2,1,0:T(8,128)(2,1)}), bf16[4,56,512]{2,1,0:T(8,128)(2,1)S(1)}, u32[]{:S(2)}, u32[]{:S(2)}) %all-to-all-start.6) | async-done | bytes 229408 | tf_op jit(solution)/shard_map/all_to_all | solution.py:17
  132.6 5.2 %all-gather = bf16[8,56,512]{2,1,0:T(8,128)(2,1)S(1)} all-gather(bf16[4,56,512]{2,1,0:T(8,128)(2,1)S(1)} %all-to-all-done.6), channel_id=2, replica_groups=mesh['x'=4,'zl'=4,'core'=2,'y'=4,'zh'=4] {'core'}, dimensions={0}, use_global_device_ids=true | all-gather | bytes 688128 | tf_op jit(solution)/shard_map/all_gather | solution.py:351
  137.8 1.3 down.1
  139.1 18.7 %all_to_all.47.parts_ref = bf16[16,32,1024]{2,1,0:T(8,128)(2,1)S(1)} all-to-all(bf16[16,32,1024]{2,1,0:T(8,128)(2,1)S(1)} %down.1), channel_id=1, replica_groups=mesh['x'=4,'zl'=4,'core'=2,'y'=4,'zh'=4] {'x','y'}, dimensions={0} | all-to-all | bytes 2097152 | tf_op jit(solution)/shard_map/all_to_all | solution.py:17
  157.8 0.1 sum_and_replicate.3
  157.9 21.9 %all_to_all.48 = bf16[32,8,128]{2,1,0:T(8,128)(2,1)S(1)} all-to-all(bf16[32,8,128]{2,1,0:T(8,128)(2,1)S(1)} %bitcast.27), channel_id=1, replica_groups=mesh['x'=4,'zl'=4,'core'=2,'y'=4,'zh'=4] {'core','zl','zh'}, dimensions={0} | all-to-all | bytes 131072 | tf_op jit(solution)/shard_map/all_to_all | solution.py:17
  179.9 0.6 convert_element_type.27
  (23 shorter events, 0.2 us)
Async XLA Ops:
  0.0 10.7 %copy-start.2 = (bf16[512,256]{1,0:T(8,128)(2,1)S(1)}, bf16[512,256]{1,0:T(8,128)(2,1)}, u32[]{:S(2)}) copy-start(bf16[512,256]{1,0:T(8,128)(2,1)} %own_ref.1) | copy-start | bytes 786436
  0.0 14.0 %copy-start = (bf16[56,8192]{1,0:T(8,128)(2,1)S(1)}, bf16[56,8192]{1,0:T(8,128)(2,1)}, u32[]{:S(2)}) copy-start(bf16[56,8192]{1,0:T(8,128)(2,1)} %gate_ref.1) | copy-start | bytes 2752516
  0.0 14.1 %copy-start.7 = (f32[8192]{0:T(1024)S(1)}, f32[8192]{0:T(1024)}, u32[]{:S(2)}) copy-start(f32[8192]{0:T(1024)} %param.10) | copy-start | bytes 98308
  1.7 22.1 %all-to-all-start = ((bf16[16,24,512]{2,1,0:T(8,128)(2,1)}), bf16[16,24,512]{2,1,0:T(8,128)(2,1)S(1)}, u32[]{:S(2)}, u32[]{:S(2)}) async-start(bf16[16,24,512]{2,1,0:T(8,128)(2,1)} %pack_rows.1), calls=%async_computation | async-start | bytes 786432 | tf_op jit(solution)/shard_map/all_to_all | solution.py:17
  10.7 13.1 %collective-permute-start = (bf16[512,256]{1,0:T(8,128)(2,1)S(1)}, bf16[512,256]{1,0:T(8,128)(2,1)S(1)}, u32[]{:S(2)}, u32[]{:S(2)}) collective-permute-start(bf16[512,256]{1,0:T(8,128)(2,1)S(1)} %copy-done.2), channel_id=1, source_target_pairs={{0,16},{16,0},{1,17},{17,1},{2,18},{18,2},{3,19},{19,3},{4,20},{20... | collective-permute-start | bytes 786440 | tf_op jit(solution)/shard_map/ppermute | solution.py:25
  14.1 1.2 copy-start.1
  16.5 0.8 copy-start.8
  17.2 18.6 %collective-permute-start.1 = (bf16[112,2048]{1,0:T(8,128)(2,1)}, bf16[112,2048]{1,0:T(8,128)(2,1)S(1)}, u32[]{:S(2)}, u32[]{:S(2)}) collective-permute-start(bf16[112,2048]{1,0:T(8,128)(2,1)} %get-tuple-element.29), channel_id=1, source_target_pairs={{0,4},{4,8},{8,12},{12,0},{1,5},{5,9},{9,13},{13,1},{2,6},{6,10},{... | collective-permute-start | bytes 1376264 | tf_op jit(solution)/shard_map/ppermute | solution.py:29
  20.0 15.9 %collective-permute-start.2 = (bf16[112,2048]{1,0:T(8,128)(2,1)S(1)}, bf16[112,2048]{1,0:T(8,128)(2,1)S(1)}, u32[]{:S(2)}, u32[]{:S(2)}) collective-permute-start(bf16[112,2048]{1,0:T(8,128)(2,1)S(1)} %get-tuple-element.30), channel_id=1, source_target_pairs={{0,12},{4,0},{8,4},{12,8},{1,13},{5,1},{9,5},{13,9},{2,14},{6,2},{... | collective-permute-start | bytes 1376264 | tf_op jit(solution)/shard_map/ppermute | solution.py:29
  25.5 9.5 %all-to-all-start.1 = ((bf16[4,128,256]{2,1,0:T(8,128)(2,1)}), bf16[4,128,256]{2,1,0:T(8,128)(2,1)S(1)}, u32[]{:S(2)}, u32[]{:S(2)}) async-start(bf16[4,128,256]{2,1,0:T(8,128)(2,1)} %project.1), calls=%async_computation.1 | async-start | bytes 524288 | tf_op jit(solution)/shard_map/all_to_all | solution.py:17
  29.5 18.4 %copy-start.9 = (bf16[112,2048]{1,0:T(8,128)(2,1)S(1)}, bf16[112,2048]{1,0:T(8,128)(2,1)}, u32[]{:S(2)}) copy-start(bf16[112,2048]{1,0:T(8,128)(2,1)} %copy-done.8) | copy-start | bytes 1376260
  35.8 27.5 %all-to-all-start.2 = ((bf16[4,128,256]{2,1,0:T(8,128)(2,1)}), bf16[4,128,256]{2,1,0:T(8,128)(2,1)S(1)}, u32[]{:S(2)}, u32[]{:S(2)}) async-start(bf16[4,128,256]{2,1,0:T(8,128)(2,1)} %sum_and_replicate.2), calls=%async_computation.2 | async-start | bytes 524288 | tf_op jit(solution)/shard_map/all_to_all | solution.py:17
  47.9 15.4 %collective-permute-start.3 = (bf16[112,2048]{1,0:T(8,128)(2,1)S(1)}, bf16[112,2048]{1,0:T(8,128)(2,1)S(1)}, u32[]{:S(2)}, u32[]{:S(2)}) collective-permute-start(bf16[112,2048]{1,0:T(8,128)(2,1)S(1)} %copy-done.9), channel_id=1, source_target_pairs={{0,8},{4,12},{8,0},{12,4},{1,9},{5,13},{9,1},{13,5},{2,10},{6,14},... | collective-permute-start | bytes 1376264 | tf_op jit(solution)/shard_map/ppermute | solution.py:29
  52.5 8.7 %collective-permute-start.4 = (bf16[448,256]{1,0:T(8,128)(2,1)}, bf16[448,256]{1,0:T(8,128)(2,1)S(1)}, u32[]{:S(2)}, u32[]{:S(2)}) collective-permute-start(bf16[448,256]{1,0:T(8,128)(2,1)} %get-tuple-element.35), channel_id=1, source_target_pairs={{0,128},{128,256},{256,384},{384,0},{1,129},{129,257},{257,385},{3... | collective-permute-start | bytes 688136 | tf_op jit(solution)/shard_map/ppermute | solution.py:29
  56.0 7.3 %collective-permute-start.5 = (bf16[448,256]{1,0:T(8,128)(2,1)}, bf16[448,256]{1,0:T(8,128)(2,1)S(1)}, u32[]{:S(2)}, u32[]{:S(2)}) collective-permute-start(bf16[448,256]{1,0:T(8,128)(2,1)} %get-tuple-element.36), channel_id=1, source_target_pairs={{0,384},{128,0},{256,128},{384,256},{1,385},{129,1},{257,129},{385... | collective-permute-start | bytes 688136 | tf_op jit(solution)/shard_map/ppermute | solution.py:29
  63.3 19.6 %copy-start.3 = (bf16[448,256]{1,0:T(8,128)(2,1)}, bf16[448,256]{1,0:T(8,128)(2,1)S(1)}, u32[]{:S(2)}) copy-start(bf16[448,256]{1,0:T(8,128)(2,1)S(1)} %collective-permute-done.5.rest_3_) | copy-start | bytes 688132
  64.1 18.8 %all-to-all-start.3 = ((bf16[4,144,256]{2,1,0:T(8,128)(2,1)}), bf16[4,144,256]{2,1,0:T(8,128)(2,1)S(1)}, u32[]{:S(2)}, u32[]{:S(2)}) async-start(bf16[4,144,256]{2,1,0:T(8,128)(2,1)} %carried_and_squares.1), calls=%async_computation.3 | async-start | bytes 589824 | tf_op jit(solution)/shard_map/all_to_all | solution.py:17
  71.2 11.0 %collective-permute-start.6 = (bf16[448,256]{1,0:T(8,128)(2,1)S(1)}, bf16[448,256]{1,0:T(8,128)(2,1)S(1)}, u32[]{:S(2)}, u32[]{:S(2)}) collective-permute-start(bf16[448,256]{1,0:T(8,128)(2,1)S(1)} %get-tuple-element.40), channel_id=1, source_target_pairs={{0,256},{128,384},{256,0},{384,128},{1,257},{129,385},{257,1},{385... | collective-permute-start | bytes 688136 | tf_op jit(solution)/shard_map/ppermute | solution.py:29
  82.2 0.7 copy-start.5
  99.3 9.2 %collective-permute-start.7 = (bf16[16,144,256]{2,1,0:T(8,128)(2,1)S(1)}, bf16[16,144,256]{2,1,0:T(8,128)(2,1)}, u32[]{:S(2)}, u32[]{:S(2)}) collective-permute-start(bf16[16,144,256]{2,1,0:T(8,128)(2,1)S(1)} %bitcast.21), channel_id=1, source_target_pairs={{0,16},{16,0},{1,17},{17,1},{2,18},{18,2},{3,19},{19,3},{4,20},{20... | collective-permute-start | bytes 3538952 | tf_op jit(solution)/shard_map/ppermute | solution.py:25
  122.2 15.6 %copy-start.4 = (bf16[448,256]{1,0:T(8,128)(2,1)S(1)}, bf16[448,256]{1,0:T(8,128)(2,1)}, u32[]{:S(2)}) copy-start(bf16[448,256]{1,0:T(8,128)(2,1)} %copy-done.3) | copy-start | bytes 688132
  122.2 15.6 %copy-start.6 = (bf16[448,256]{1,0:T(8,128)(2,1)S(1)}, bf16[448,256]{1,0:T(8,128)(2,1)}, u32[]{:S(2)}) copy-start(bf16[448,256]{1,0:T(8,128)(2,1)} %copy-done.5) | copy-start | bytes 688132
  123.0 9.6 %all-to-all-start.6 = ((bf16[4,56,512]{2,1,0:T(8,128)(2,1)}), bf16[4,56,512]{2,1,0:T(8,128)(2,1)S(1)}, u32[]{:S(2)}, u32[]{:S(2)}) async-start(bf16[4,56,512]{2,1,0:T(8,128)(2,1)} %activate.1), calls=%async_computation.6 | async-start | bytes 458752 | tf_op jit(solution)/shard_map/all_to_all | solution.py:17

commit v6 on v5

--- a/solution.py
+++ b/solution.py
@@ -10,7 +10,7 @@
 EPS = 1e-05
 X, ZL, Y, ZH = 4, 4, 4, 4
 CORES = 2
-EXTRA = 16
+EXTRA = 8
 
 
 def exchange(value, axes):

time: 182 us -> 180 us (0.989)
  no operation moved by 1% of the time
where the time goes in v6:
time: 180 us; the launch traced here: 179 us
  blocking collectives  73 us (41%)
  starting transfers between devices  70.9 us (39%)
  waiting for transfers between devices  17.7 us (10%)
  Pallas kernels  11.8 us (7%)
  local copies, waits for them, and re-layouts  5.58 us (3%)
    all_to_all x4, blocking collectives, exchange(): return lax.all_to_all(value, axes, 0, 0, tiled=True)  67.9 us
    all_to_all x5, starting transfers between devices, exchange(): return lax.all_to_all(value, axes, 0, 0, tiled=True)  36.4 us
    ppermute x6, starting transfers between devices, shift_along(): return lax.ppermute(value, axis, [(i, (i + shift) % 4) for i in range(4)])  24.9 us
    ppermute x2, starting transfers between devices, swap_cores(): return lax.ppermute(value, 'core', [(0, 1), (1, 0)])  9.56 us
    all_to_all x5, waiting for transfers between devices, exchange(): return lax.all_to_all(value, axes, 0, 0, tiled=True)  8.73 us
    ppermute x6, waiting for transfers between devices, shift_along(): return lax.ppermute(value, axis, [(i, (i + shift) % 4) for i in range(4)])  7.91 us
    all_gather x1, blocking collectives, shards(): hidden = lax.all_gather(hidden, 'core', axis=0, tiled=False)  5.15 us
  transfers between devices with their start and end apart: 13, of which 6 were waited for; matrix products, arithmetic and copies ran while one was open for 1% of the time, Pallas kernels for 3%

profile of v6, /device:TPU:1, one launch (start us, length us, event | category | flops | bytes accessed | tf_op | source)
XLA Modules:
  0.0 179.4 jit_solution(3077266377727599235)
XLA Ops:
  0.0 1.7 pack_rows.1
  1.7 9.0 %all-to-all-start = ((bf16[16,24,512]{2,1,0:T(8,128)(2,1)}), bf16[16,24,512]{2,1,0:T(8,128)(2,1)S(1)}, u32[]{:S(2)}, u32[]{:S(2)}) async-start(bf16[16,24,512]{2,1,0:T(8,128)(2,1)} %pack_rows.1), calls=%async_computation | async-start | bytes 786432 | tf_op jit(solution)/shard_map/all_to_all | solution.py:17
  10.7 3.3 %collective-permute-start = (bf16[512,256]{1,0:T(8,128)(2,1)S(1)}, bf16[512,256]{1,0:T(8,128)(2,1)S(1)}, u32[]{:S(2)}, u32[]{:S(2)}) collective-permute-start(bf16[512,256]{1,0:T(8,128)(2,1)S(1)} %copy-done.2), channel_id=1, source_target_pairs={{0,16},{16,0},{1,17},{17,1},{2,18},{18,2},{3,19},{19,3},{4,20},{20... | collective-permute-start | bytes 786440 | tf_op jit(solution)/shard_map/ppermute | solution.py:25
  14.1 0.0 copy-start.1
  14.1 1.2 copy-done.1
  15.2 1.2 cut_weights.1
  16.5 0.8 copy-done.8
  17.2 2.7 %collective-permute-start.1 = (bf16[112,2048]{1,0:T(8,128)(2,1)}, bf16[112,2048]{1,0:T(8,128)(2,1)S(1)}, u32[]{:S(2)}, u32[]{:S(2)}) collective-permute-start(bf16[112,2048]{1,0:T(8,128)(2,1)} %get-tuple-element.29), channel_id=1, source_target_pairs={{0,4},{4,8},{8,12},{12,0},{1,5},{5,9},{9,13},{13,1},{2,6},{6,10},{... | collective-permute-start | bytes 1376264 | tf_op jit(solution)/shard_map/ppermute | solution.py:29
  20.0 3.7 %collective-permute-start.2 = (bf16[112,2048]{1,0:T(8,128)(2,1)S(1)}, bf16[112,2048]{1,0:T(8,128)(2,1)S(1)}, u32[]{:S(2)}, u32[]{:S(2)}) collective-permute-start(bf16[112,2048]{1,0:T(8,128)(2,1)S(1)} %get-tuple-element.30), channel_id=1, source_target_pairs={{0,12},{4,0},{8,4},{12,8},{1,13},{5,1},{9,5},{13,9},{2,14},{6,2},{... | collective-permute-start | bytes 1376264 | tf_op jit(solution)/shard_map/ppermute | solution.py:29
  23.7 0.1 pad_add_fusion.2.at_ref
  23.8 0.0 collective-permute-done.other_ref
  23.8 0.0 all-to-all-done.got_ref
  23.8 1.7 project.1
  25.5 4.0 %all-to-all-start.1 = ((bf16[4,128,256]{2,1,0:T(8,128)(2,1)}), bf16[4,128,256]{2,1,0:T(8,128)(2,1)S(1)}, u32[]{:S(2)}, u32[]{:S(2)}) async-start(bf16[4,128,256]{2,1,0:T(8,128)(2,1)} %project.1), calls=%async_computation.1 | async-start | bytes 524288 | tf_op jit(solution)/shard_map/all_to_all | solution.py:17
  29.5 2.2 %dynamic-slice_bitcast_fusion = (bf16[448,256]{1,0:T(8,128)(2,1)}, bf16[448,256]{1,0:T(8,128)(2,1)S(1)}, bf16[448,256]{1,0:T(8,128)(2,1)}, bf16[448,256]{1,0:T(8,128)(2,1)S(1)}) fusion(bf16[4,448,256]{2,1,0:T(8,128)(2,1)} %bitcast.26, s32[]{:T(128)S(6)} %select_n.39, s32[]{:T(128)S(6)} %select_n.37, s32[]{:T(128)S(6)} %select_n.35, s32[]{:T(128)S(6)} %select_n.33), kind=kLoop, calls=%fused_computation | loop fusion | bytes 1835024 | tf_op jit(solution)/shard_map/jit(dynamic_index_in_dim)/squeeze | solution.py:321
  31.7 3.4 %all-to-all-done.1.parts_ref = bf16[4,128,256]{2,1,0:T(8,128)(2,1)S(1)} async-done(((bf16[4,128,256]{2,1,0:T(8,128)(2,1)}), bf16[4,128,256]{2,1,0:T(8,128)(2,1)S(1)}, u32[]{:S(2)}, u32[]{:S(2)}) %all-to-all-start.1) | async-done | bytes 262176 | tf_op jit(solution)/shard_map/all_to_all | solution.py:17
  35.1 0.7 sum_and_replicate.2
  35.8 12.1 %all-to-all-start.2 = ((bf16[4,128,256]{2,1,0:T(8,128)(2,1)}), bf16[4,128,256]{2,1,0:T(8,128)(2,1)S(1)}, u32[]{:S(2)}, u32[]{:S(2)}) async-start(bf16[4,128,256]{2,1,0:T(8,128)(2,1)} %sum_and_replicate.2), calls=%async_computation.2 | async-start | bytes 524288 | tf_op jit(solution)/shard_map/all_to_all | solution.py:17
  47.9 4.5 %collective-permute-start.3 = (bf16[112,2048]{1,0:T(8,128)(2,1)S(1)}, bf16[112,2048]{1,0:T(8,128)(2,1)S(1)}, u32[]{:S(2)}, u32[]{:S(2)}) collective-permute-start(bf16[112,2048]{1,0:T(8,128)(2,1)S(1)} %copy-done.9), channel_id=1, source_target_pairs={{0,8},{4,12},{8,0},{12,4},{1,9},{5,13},{9,1},{13,5},{2,10},{6,14},... | collective-permute-start | bytes 1376264 | tf_op jit(solution)/shard_map/ppermute | solution.py:29
  52.5 3.6 %collective-permute-start.4 = (bf16[448,256]{1,0:T(8,128)(2,1)}, bf16[448,256]{1,0:T(8,128)(2,1)S(1)}, u32[]{:S(2)}, u32[]{:S(2)}) collective-permute-start(bf16[448,256]{1,0:T(8,128)(2,1)} %get-tuple-element.35), channel_id=1, source_target_pairs={{0,128},{128,256},{256,384},{384,0},{1,129},{129,257},{257,385},{3... | collective-permute-start | bytes 688136 | tf_op jit(solution)/shard_map/ppermute | solution.py:29
  56.0 3.1 %collective-permute-start.5 = (bf16[448,256]{1,0:T(8,128)(2,1)}, bf16[448,256]{1,0:T(8,128)(2,1)S(1)}, u32[]{:S(2)}, u32[]{:S(2)}) collective-permute-start(bf16[448,256]{1,0:T(8,128)(2,1)} %get-tuple-element.36), channel_id=1, source_target_pairs={{0,384},{128,0},{256,128},{384,256},{1,385},{129,1},{257,129},{385... | collective-permute-start | bytes 688136 | tf_op jit(solution)/shard_map/ppermute | solution.py:29
  59.2 2.0 %collective-permute-done.4.rest_1_ = bf16[448,256]{1,0:T(8,128)(2,1)S(1)} collective-permute-done((bf16[448,256]{1,0:T(8,128)(2,1)}, bf16[448,256]{1,0:T(8,128)(2,1)S(1)}, u32[]{:S(2)}, u32[]{:S(2)}) %collective-permute-start.4) | collective-permute-done | bytes 229408 | tf_op jit(solution)/shard_map/ppermute | solution.py:29
  61.1 2.2 %collective-permute-done.5.rest_3_ = bf16[448,256]{1,0:T(8,128)(2,1)S(1)} collective-permute-done((bf16[448,256]{1,0:T(8,128)(2,1)}, bf16[448,256]{1,0:T(8,128)(2,1)S(1)}, u32[]{:S(2)}, u32[]{:S(2)}) %collective-permute-start.5) | collective-permute-done | bytes 229408 | tf_op jit(solution)/shard_map/ppermute | solution.py:29
  63.3 0.0 collective-permute-done.3.rest_2_
  63.3 0.8 carried_and_squares.1
  64.1 7.1 %all-to-all-start.3 = ((bf16[4,136,256]{2,1,0:T(8,128)(2,1)}), bf16[4,136,256]{2,1,0:T(8,128)(2,1)S(1)}, u32[]{:S(2)}, u32[]{:S(2)}) async-start(bf16[4,136,256]{2,1,0:T(8,128)(2,1)} %carried_and_squares.1), calls=%async_computation.3 | async-start | bytes 557056 | tf_op jit(solution)/shard_map/all_to_all | solution.py:17
  71.2 7.2 %collective-permute-start.6 = (bf16[448,256]{1,0:T(8,128)(2,1)S(1)}, bf16[448,256]{1,0:T(8,128)(2,1)S(1)}, u32[]{:S(2)}, u32[]{:S(2)}) collective-permute-start(bf16[448,256]{1,0:T(8,128)(2,1)S(1)} %get-tuple-element.40), channel_id=1, source_target_pairs={{0,256},{128,384},{256,0},{384,128},{1,257},{129,385},{257,1},{385... | collective-permute-start | bytes 688136 | tf_op jit(solution)/shard_map/ppermute | solution.py:29
  78.4 3.8 %collective-permute-done.6.rest_2_ = bf16[448,256]{1,0:T(8,128)(2,1)S(1)} collective-permute-done((bf16[448,256]{1,0:T(8,128)(2,1)S(1)}, bf16[448,256]{1,0:T(8,128)(2,1)S(1)}, u32[]{:S(2)}, u32[]{:S(2)}) %collective-permute-start.6) | collective-permute-done | bytes 229408 | tf_op jit(solution)/shard_map/ppermute | solution.py:29
  82.2 0.7 copy-done.5
  82.8 0.0 all-to-all-done.3
  82.9 0.1 broadcast_in_dim.2
  82.9 16.4 %all_to_all.45 = bf16[4,4,136,256]{3,2,1,0:T(8,128)(2,1)S(1)} all-to-all(bf16[4,4,136,256]{3,2,1,0:T(8,128)(2,1)S(1)} %broadcast_in_dim.2), channel_id=1, replica_groups=mesh['x'=4,'zl'=4,'core'=2,'y'=4,'zh'=4] {'x'}, dimensions={0} | all-to-all | bytes 2228224 | tf_op jit(solution)/shard_map/all_to_all | solution.py:17
  99.3 6.2 %collective-permute-start.7 = (bf16[16,136,256]{2,1,0:T(8,128)(2,1)S(1)}, bf16[16,136,256]{2,1,0:T(8,128)(2,1)}, u32[]{:S(2)}, u32[]{:S(2)}) collective-permute-start(bf16[16,136,256]{2,1,0:T(8,128)(2,1)S(1)} %bitcast.21), channel_id=1, source_target_pairs={{0,16},{16,0},{1,17},{17,1},{2,18},{18,2},{3,19},{19,3},{4,20},{20... | collective-permute-start | bytes 3342344 | tf_op jit(solution)/shard_map/ppermute | solution.py:25
  105.5 0.1 pad_add_fusion.1.at_ref
  105.6 1.4 gate_up.1
  107.0 1.0 collective-permute-done.7.spread_ref
  108.0 2.1 %gate_up_both.1 = (bf16[4,120,512]{2,1,0:T(8,128)(2,1)S(1)}, bf16[128,512]{1,0:T(8,128)(2,1)S(1)}) custom-call(s32[3]{0:T(128)S(1)} %pad_add_fusion.1.at_ref, bf16[16,136,256]{2,1,0:T(8,128)(2,1)} %collective-permute-done.7.spread_ref, bf16[112,2048]{1,0:T(8,128)(2,1)S(1)} %get-tuple-element.42.rest_0_, ...), custom_call_target="tpu_custom_call" | custom-call | tf_op jit(solution)/shard_map/gate_up_both/pallas_call | solution.py:285
  110.1 11.0 %all_to_all.46.parts_ref = bf16[4,120,512]{2,1,0:T(8,128)(2,1)S(1)} all-to-all(bf16[4,120,512]{2,1,0:T(8,128)(2,1)S(1)} %get-tuple-element.48), channel_id=1, replica_groups=mesh['x'=4,'zl'=4,'core'=2,'y'=4,'zh'=4] {'y'}, dimensions={0} | all-to-all | bytes 983040 | tf_op jit(solution)/shard_map/all_to_all | solution.py:17
  121.1 0.8 activate.1
  121.9 4.2 %all-to-all-start.6 = ((bf16[4,56,512]{2,1,0:T(8,128)(2,1)}), bf16[4,56,512]{2,1,0:T(8,128)(2,1)S(1)}, u32[]{:S(2)}, u32[]{:S(2)}) async-start(bf16[4,56,512]{2,1,0:T(8,128)(2,1)} %activate.1), calls=%async_computation.6 | async-start | bytes 458752 | tf_op jit(solution)/shard_map/all_to_all | solution.py:17
  126.1 0.1 pad_add_fusion.at_ref
  126.2 5.3 %all-to-all-done.6 = bf16[4,56,512]{2,1,0:T(8,128)(2,1)S(1)} async-done(((bf16[4,56,512]{2,1,0:T(8,128)(2,1)}), bf16[4,56,512]{2,1,0:T(8,128)(2,1)S(1)}, u32[]{:S(2)}, u32[]{:S(2)}) %all-to-all-start.6) | async-done | bytes 229408 | tf_op jit(solution)/shard_map/all_to_all | solution.py:17
  131.5 5.2 %all-gather = bf16[8,56,512]{2,1,0:T(8,128)(2,1)S(1)} all-gather(bf16[4,56,512]{2,1,0:T(8,128)(2,1)S(1)} %all-to-all-done.6), channel_id=2, replica_groups=mesh['x'=4,'zl'=4,'core'=2,'y'=4,'zh'=4] {'core'}, dimensions={0}, use_global_device_ids=true | all-gather | bytes 688128 | tf_op jit(solution)/shard_map/all_gather | solution.py:351
  136.7 1.3 down.1
  138.0 18.7 %all_to_all.47.parts_ref = bf16[16,32,1024]{2,1,0:T(8,128)(2,1)S(1)} all-to-all(bf16[16,32,1024]{2,1,0:T(8,128)(2,1)S(1)} %down.1), channel_id=1, replica_groups=mesh['x'=4,'zl'=4,'core'=2,'y'=4,'zh'=4] {'x','y'}, dimensions={0} | all-to-all | bytes 2097152 | tf_op jit(solution)/shard_map/all_to_all | solution.py:17
  156.7 0.1 sum_and_replicate.3
  156.8 21.8 %all_to_all.48 = bf16[32,8,128]{2,1,0:T(8,128)(2,1)S(1)} all-to-all(bf16[32,8,128]{2,1,0:T(8,128)(2,1)S(1)} %bitcast.27), channel_id=1, replica_groups=mesh['x'=4,'zl'=4,'core'=2,'y'=4,'zh'=4] {'core','zl','zh'}, dimensions={0} | all-to-all | bytes 131072 | tf_op jit(solution)/shard_map/all_to_all | solution.py:17
  178.8 0.6 convert_element_type.27
  (23 shorter events, 0.2 us)
Async XLA Ops:
  0.0 10.7 %copy-start.2 = (bf16[512,256]{1,0:T(8,128)(2,1)S(1)}, bf16[512,256]{1,0:T(8,128)(2,1)}, u32[]{:S(2)}) copy-start(bf16[512,256]{1,0:T(8,128)(2,1)} %own_ref.1) | copy-start | bytes 786436
  0.0 14.0 %copy-start = (bf16[56,8192]{1,0:T(8,128)(2,1)S(1)}, bf16[56,8192]{1,0:T(8,128)(2,1)}, u32[]{:S(2)}) copy-start(bf16[56,8192]{1,0:T(8,128)(2,1)} %gate_ref.1) | copy-start | bytes 2752516
  0.0 14.1 %copy-start.7 = (f32[8192]{0:T(1024)S(1)}, f32[8192]{0:T(1024)}, u32[]{:S(2)}) copy-start(f32[8192]{0:T(1024)} %param.10) | copy-start | bytes 98308
  1.7 22.1 %all-to-all-start = ((bf16[16,24,512]{2,1,0:T(8,128)(2,1)}), bf16[16,24,512]{2,1,0:T(8,128)(2,1)S(1)}, u32[]{:S(2)}, u32[]{:S(2)}) async-start(bf16[16,24,512]{2,1,0:T(8,128)(2,1)} %pack_rows.1), calls=%async_computation | async-start | bytes 786432 | tf_op jit(solution)/shard_map/all_to_all | solution.py:17
  10.7 13.1 %collective-permute-start = (bf16[512,256]{1,0:T(8,128)(2,1)S(1)}, bf16[512,256]{1,0:T(8,128)(2,1)S(1)}, u32[]{:S(2)}, u32[]{:S(2)}) collective-permute-start(bf16[512,256]{1,0:T(8,128)(2,1)S(1)} %copy-done.2), channel_id=1, source_target_pairs={{0,16},{16,0},{1,17},{17,1},{2,18},{18,2},{3,19},{19,3},{4,20},{20... | collective-permute-start | bytes 786440 | tf_op jit(solution)/shard_map/ppermute | solution.py:25
  14.1 1.2 copy-start.1
  16.5 0.8 copy-start.8
  17.2 18.6 %collective-permute-start.1 = (bf16[112,2048]{1,0:T(8,128)(2,1)}, bf16[112,2048]{1,0:T(8,128)(2,1)S(1)}, u32[]{:S(2)}, u32[]{:S(2)}) collective-permute-start(bf16[112,2048]{1,0:T(8,128)(2,1)} %get-tuple-element.29), channel_id=1, source_target_pairs={{0,4},{4,8},{8,12},{12,0},{1,5},{5,9},{9,13},{13,1},{2,6},{6,10},{... | collective-permute-start | bytes 1376264 | tf_op jit(solution)/shard_map/ppermute | solution.py:29
  20.0 15.9 %collective-permute-start.2 = (bf16[112,2048]{1,0:T(8,128)(2,1)S(1)}, bf16[112,2048]{1,0:T(8,128)(2,1)S(1)}, u32[]{:S(2)}, u32[]{:S(2)}) collective-permute-start(bf16[112,2048]{1,0:T(8,128)(2,1)S(1)} %get-tuple-element.30), channel_id=1, source_target_pairs={{0,12},{4,0},{8,4},{12,8},{1,13},{5,1},{9,5},{13,9},{2,14},{6,2},{... | collective-permute-start | bytes 1376264 | tf_op jit(solution)/shard_map/ppermute | solution.py:29
  25.5 9.5 %all-to-all-start.1 = ((bf16[4,128,256]{2,1,0:T(8,128)(2,1)}), bf16[4,128,256]{2,1,0:T(8,128)(2,1)S(1)}, u32[]{:S(2)}, u32[]{:S(2)}) async-start(bf16[4,128,256]{2,1,0:T(8,128)(2,1)} %project.1), calls=%async_computation.1 | async-start | bytes 524288 | tf_op jit(solution)/shard_map/all_to_all | solution.py:17
  29.5 18.4 %copy-start.9 = (bf16[112,2048]{1,0:T(8,128)(2,1)S(1)}, bf16[112,2048]{1,0:T(8,128)(2,1)}, u32[]{:S(2)}) copy-start(bf16[112,2048]{1,0:T(8,128)(2,1)} %copy-done.8) | copy-start | bytes 1376260
  35.8 27.5 %all-to-all-start.2 = ((bf16[4,128,256]{2,1,0:T(8,128)(2,1)}), bf16[4,128,256]{2,1,0:T(8,128)(2,1)S(1)}, u32[]{:S(2)}, u32[]{:S(2)}) async-start(bf16[4,128,256]{2,1,0:T(8,128)(2,1)} %sum_and_replicate.2), calls=%async_computation.2 | async-start | bytes 524288 | tf_op jit(solution)/shard_map/all_to_all | solution.py:17
  47.9 15.4 %collective-permute-start.3 = (bf16[112,2048]{1,0:T(8,128)(2,1)S(1)}, bf16[112,2048]{1,0:T(8,128)(2,1)S(1)}, u32[]{:S(2)}, u32[]{:S(2)}) collective-permute-start(bf16[112,2048]{1,0:T(8,128)(2,1)S(1)} %copy-done.9), channel_id=1, source_target_pairs={{0,8},{4,12},{8,0},{12,4},{1,9},{5,13},{9,1},{13,5},{2,10},{6,14},... | collective-permute-start | bytes 1376264 | tf_op jit(solution)/shard_map/ppermute | solution.py:29
  52.5 8.7 %collective-permute-start.4 = (bf16[448,256]{1,0:T(8,128)(2,1)}, bf16[448,256]{1,0:T(8,128)(2,1)S(1)}, u32[]{:S(2)}, u32[]{:S(2)}) collective-permute-start(bf16[448,256]{1,0:T(8,128)(2,1)} %get-tuple-element.35), channel_id=1, source_target_pairs={{0,128},{128,256},{256,384},{384,0},{1,129},{129,257},{257,385},{3... | collective-permute-start | bytes 688136 | tf_op jit(solution)/shard_map/ppermute | solution.py:29
  56.0 7.3 %collective-permute-start.5 = (bf16[448,256]{1,0:T(8,128)(2,1)}, bf16[448,256]{1,0:T(8,128)(2,1)S(1)}, u32[]{:S(2)}, u32[]{:S(2)}) collective-permute-start(bf16[448,256]{1,0:T(8,128)(2,1)} %get-tuple-element.36), channel_id=1, source_target_pairs={{0,384},{128,0},{256,128},{384,256},{1,385},{129,1},{257,129},{385... | collective-permute-start | bytes 688136 | tf_op jit(solution)/shard_map/ppermute | solution.py:29
  63.3 19.6 %copy-start.3 = (bf16[448,256]{1,0:T(8,128)(2,1)}, bf16[448,256]{1,0:T(8,128)(2,1)S(1)}, u32[]{:S(2)}) copy-start(bf16[448,256]{1,0:T(8,128)(2,1)S(1)} %collective-permute-done.5.rest_3_) | copy-start | bytes 688132
  64.1 18.8 %all-to-all-start.3 = ((bf16[4,136,256]{2,1,0:T(8,128)(2,1)}), bf16[4,136,256]{2,1,0:T(8,128)(2,1)S(1)}, u32[]{:S(2)}, u32[]{:S(2)}) async-start(bf16[4,136,256]{2,1,0:T(8,128)(2,1)} %carried_and_squares.1), calls=%async_computation.3 | async-start | bytes 557056 | tf_op jit(solution)/shard_map/all_to_all | solution.py:17
  71.2 11.0 %collective-permute-start.6 = (bf16[448,256]{1,0:T(8,128)(2,1)S(1)}, bf16[448,256]{1,0:T(8,128)(2,1)S(1)}, u32[]{:S(2)}, u32[]{:S(2)}) collective-permute-start(bf16[448,256]{1,0:T(8,128)(2,1)S(1)} %get-tuple-element.40), channel_id=1, source_target_pairs={{0,256},{128,384},{256,0},{384,128},{1,257},{129,385},{257,1},{385... | collective-permute-start | bytes 688136 | tf_op jit(solution)/shard_map/ppermute | solution.py:29
  82.2 0.7 copy-start.5
  99.3 8.7 %collective-permute-start.7 = (bf16[16,136,256]{2,1,0:T(8,128)(2,1)S(1)}, bf16[16,136,256]{2,1,0:T(8,128)(2,1)}, u32[]{:S(2)}, u32[]{:S(2)}) collective-permute-start(bf16[16,136,256]{2,1,0:T(8,128)(2,1)S(1)} %bitcast.21), channel_id=1, source_target_pairs={{0,16},{16,0},{1,17},{17,1},{2,18},{18,2},{3,19},{19,3},{4,20},{20... | collective-permute-start | bytes 3342344 | tf_op jit(solution)/shard_map/ppermute | solution.py:25
  121.1 15.6 %copy-start.4 = (bf16[448,256]{1,0:T(8,128)(2,1)S(1)}, bf16[448,256]{1,0:T(8,128)(2,1)}, u32[]{:S(2)}) copy-start(bf16[448,256]{1,0:T(8,128)(2,1)} %copy-done.3) | copy-start | bytes 688132
  121.1 15.6 %copy-start.6 = (bf16[448,256]{1,0:T(8,128)(2,1)S(1)}, bf16[448,256]{1,0:T(8,128)(2,1)}, u32[]{:S(2)}) copy-start(bf16[448,256]{1,0:T(8,128)(2,1)} %copy-done.5) | copy-start | bytes 688132
  121.9 9.6 %all-to-all-start.6 = ((bf16[4,56,512]{2,1,0:T(8,128)(2,1)}), bf16[4,56,512]{2,1,0:T(8,128)(2,1)S(1)}, u32[]{:S(2)}, u32[]{:S(2)}) async-start(bf16[4,56,512]{2,1,0:T(8,128)(2,1)} %activate.1), calls=%async_computation.6 | async-start | bytes 458752 | tf_op jit(solution)/shard_map/all_to_all | solution.py:17

commit v7 on v6

--- a/solution.py
+++ b/solution.py
@@ -173,6 +173,32 @@
     )(at, hidden, kept, *pieces)
 
 
+def sum_to_row(parts, d):
+    _, rows, lanes = parts.shape
+    per_x = rows // X
+
+    def kernel(parts_ref, out_ref):
+        for zl in range(ZL):
+            for core in range(CORES):
+                first = (core * ZL + zl) * ZH
+                total = parts_ref[first].astype(F32)
+                for zh in range(1, ZH):
+                    total = total + parts_ref[first + zh].astype(F32)
+                for row in range(rows):
+                    x, piece = row // per_x, row % per_x
+                    at = (((x * ZL + zl) * CORES + core) * per_x + piece) * lanes
+                    out_ref[:, at : at + lanes] = total[row : row + 1].astype(BF16)
+
+    return pl.pallas_call(
+        kernel,
+        out_shape=jax.ShapeDtypeStruct((1, d), BF16),
+        in_specs=[vmem()],
+        out_specs=vmem(),
+        compiler_params=pltpu.CompilerParams(vmem_limit_bytes=4 * 1024 * 1024),
+        name="sum_to_row",
+    )(parts)
+
+
 def sum_and_replicate(parts, count):
     pieces, rows, width = parts.shape
 
@@ -358,10 +384,7 @@
     near = sum_and_replicate(exchange(by_owner, ("x", "y")), 1)
     near = near.reshape(CORES * ZL * ZH, X * cols // 128, 128)
     final = exchange(near, ("core", "zl", "zh"))
-    final = final.reshape(CORES, ZL, ZH, X, cols).astype(F32)
-    mixed = jnp.sum(final, axis=2)
-    mixed = jnp.transpose(mixed, (2, 1, 0, 3)).reshape(1, d)
-    return mixed.astype(BF16)
+    return sum_to_row(final, d)
 
 
 def solution(mesh):

time: 180 us -> 180 us (level)
  no operation moved by 1% of the time
where the time goes in v7:
time: 180 us; the launch traced here: 179 us
  blocking collectives  73 us (41%)
  starting transfers between devices  70.9 us (39%)
  waiting for transfers between devices  17.7 us (10%)
  Pallas kernels  12.5 us (7%)
  local copies, waits for them, and re-layouts  4.89 us (3%)
    all_to_all x4, blocking collectives, exchange(): return lax.all_to_all(value, axes, 0, 0, tiled=True)  67.9 us
    all_to_all x5, starting transfers between devices, exchange(): return lax.all_to_all(value, axes, 0, 0, tiled=True)  36.4 us
    ppermute x6, starting transfers between devices, shift_along(): return lax.ppermute(value, axis, [(i, (i + shift) % 4) for i in range(4)])  24.9 us
    ppermute x2, starting transfers between devices, swap_cores(): return lax.ppermute(value, 'core', [(0, 1), (1, 0)])  9.56 us
    all_to_all x5, waiting for transfers between devices, exchange(): return lax.all_to_all(value, axes, 0, 0, tiled=True)  8.75 us
    ppermute x6, waiting for transfers between devices, shift_along(): return lax.ppermute(value, axis, [(i, (i + shift) % 4) for i in range(4)])  7.91 us
    all_gather x1, blocking collectives, shards(): hidden = lax.all_gather(hidden, 'core', axis=0, tiled=False)  5.15 us
  transfers between devices with their start and end apart: 13, of which 6 were waited for; matrix products, arithmetic and copies ran while one was open for 1% of the time, Pallas kernels for 3%

profile of v7, /device:TPU:1, one launch (start us, length us, event | category | flops | bytes accessed | tf_op | source)
XLA Modules:
  0.0 179.3 jit_solution(13221484508109533451)
XLA Ops:
  0.0 1.7 pack_rows.1
  1.7 9.0 %all-to-all-start = ((bf16[16,24,512]{2,1,0:T(8,128)(2,1)}), bf16[16,24,512]{2,1,0:T(8,128)(2,1)S(1)}, u32[]{:S(2)}, u32[]{:S(2)}) async-start(bf16[16,24,512]{2,1,0:T(8,128)(2,1)} %pack_rows.1), calls=%async_computation | async-start | bytes 786432 | tf_op jit(solution)/shard_map/all_to_all | solution.py:17
  10.7 3.3 %collective-permute-start = (bf16[512,256]{1,0:T(8,128)(2,1)S(1)}, bf16[512,256]{1,0:T(8,128)(2,1)S(1)}, u32[]{:S(2)}, u32[]{:S(2)}) collective-permute-start(bf16[512,256]{1,0:T(8,128)(2,1)S(1)} %copy-done.2), channel_id=1, source_target_pairs={{0,16},{16,0},{1,17},{17,1},{2,18},{18,2},{3,19},{19,3},{4,20},{20... | collective-permute-start | bytes 786440 | tf_op jit(solution)/shard_map/ppermute | solution.py:25
  14.1 0.0 copy-start.1
  14.1 1.2 copy-done.1
  15.3 1.2 cut_weights.1
  16.5 0.8 copy-done.8
  17.2 2.7 %collective-permute-start.1 = (bf16[112,2048]{1,0:T(8,128)(2,1)}, bf16[112,2048]{1,0:T(8,128)(2,1)S(1)}, u32[]{:S(2)}, u32[]{:S(2)}) collective-permute-start(bf16[112,2048]{1,0:T(8,128)(2,1)} %get-tuple-element.29), channel_id=1, source_target_pairs={{0,4},{4,8},{8,12},{12,0},{1,5},{5,9},{9,13},{13,1},{2,6},{6,10},{... | collective-permute-start | bytes 1376264 | tf_op jit(solution)/shard_map/ppermute | solution.py:29
  20.0 3.7 %collective-permute-start.2 = (bf16[112,2048]{1,0:T(8,128)(2,1)S(1)}, bf16[112,2048]{1,0:T(8,128)(2,1)S(1)}, u32[]{:S(2)}, u32[]{:S(2)}) collective-permute-start(bf16[112,2048]{1,0:T(8,128)(2,1)S(1)} %get-tuple-element.30), channel_id=1, source_target_pairs={{0,12},{4,0},{8,4},{12,8},{1,13},{5,1},{9,5},{13,9},{2,14},{6,2},{... | collective-permute-start | bytes 1376264 | tf_op jit(solution)/shard_map/ppermute | solution.py:29
  23.7 0.1 pad_add_fusion.2.at_ref
  23.8 0.0 collective-permute-done.other_ref
  23.8 1.7 project.1
  25.5 4.0 %all-to-all-start.1 = ((bf16[4,128,256]{2,1,0:T(8,128)(2,1)}), bf16[4,128,256]{2,1,0:T(8,128)(2,1)S(1)}, u32[]{:S(2)}, u32[]{:S(2)}) async-start(bf16[4,128,256]{2,1,0:T(8,128)(2,1)} %project.1), calls=%async_computation.1 | async-start | bytes 524288 | tf_op jit(solution)/shard_map/all_to_all | solution.py:17
  29.5 2.1 %dynamic-slice_bitcast_fusion = (bf16[448,256]{1,0:T(8,128)(2,1)}, bf16[448,256]{1,0:T(8,128)(2,1)S(1)}, bf16[448,256]{1,0:T(8,128)(2,1)}, bf16[448,256]{1,0:T(8,128)(2,1)S(1)}) fusion(bf16[4,448,256]{2,1,0:T(8,128)(2,1)} %bitcast.25, s32[]{:T(128)S(6)} %select_n.39, s32[]{:T(128)S(6)} %select_n.37, s32[]{:T(128)S(6)} %select_n.35, s32[]{:T(128)S(6)} %select_n.33), kind=kLoop, calls=%fused_computation | loop fusion | bytes 1835024 | tf_op jit(solution)/shard_map/jit(dynamic_index_in_dim)/squeeze | solution.py:347
  31.7 3.4 %all-to-all-done.1.parts_ref = bf16[4,128,256]{2,1,0:T(8,128)(2,1)S(1)} async-done(((bf16[4,128,256]{2,1,0:T(8,128)(2,1)}), bf16[4,128,256]{2,1,0:T(8,128)(2,1)S(1)}, u32[]{:S(2)}, u32[]{:S(2)}) %all-to-all-start.1) | async-done | bytes 262176 | tf_op jit(solution)/shard_map/all_to_all | solution.py:17
  35.1 0.7 sum_and_replicate.2
  35.8 12.1 %all-to-all-start.2 = ((bf16[4,128,256]{2,1,0:T(8,128)(2,1)}), bf16[4,128,256]{2,1,0:T(8,128)(2,1)S(1)}, u32[]{:S(2)}, u32[]{:S(2)}) async-start(bf16[4,128,256]{2,1,0:T(8,128)(2,1)} %sum_and_replicate.2), calls=%async_computation.2 | async-start | bytes 524288 | tf_op jit(solution)/shard_map/all_to_all | solution.py:17
  47.9 4.5 %collective-permute-start.3 = (bf16[112,2048]{1,0:T(8,128)(2,1)S(1)}, bf16[112,2048]{1,0:T(8,128)(2,1)S(1)}, u32[]{:S(2)}, u32[]{:S(2)}) collective-permute-start(bf16[112,2048]{1,0:T(8,128)(2,1)S(1)} %copy-done.9), channel_id=1, source_target_pairs={{0,8},{4,12},{8,0},{12,4},{1,9},{5,13},{9,1},{13,5},{2,10},{6,14},... | collective-permute-start | bytes 1376264 | tf_op jit(solution)/shard_map/ppermute | solution.py:29
  52.5 3.6 %collective-permute-start.4 = (bf16[448,256]{1,0:T(8,128)(2,1)}, bf16[448,256]{1,0:T(8,128)(2,1)S(1)}, u32[]{:S(2)}, u32[]{:S(2)}) collective-permute-start(bf16[448,256]{1,0:T(8,128)(2,1)} %get-tuple-element.35), channel_id=1, source_target_pairs={{0,128},{128,256},{256,384},{384,0},{1,129},{129,257},{257,385},{3... | collective-permute-start | bytes 688136 | tf_op jit(solution)/shard_map/ppermute | solution.py:29
  56.0 3.1 %collective-permute-start.5 = (bf16[448,256]{1,0:T(8,128)(2,1)}, bf16[448,256]{1,0:T(8,128)(2,1)S(1)}, u32[]{:S(2)}, u32[]{:S(2)}) collective-permute-start(bf16[448,256]{1,0:T(8,128)(2,1)} %get-tuple-element.36), channel_id=1, source_target_pairs={{0,384},{128,0},{256,128},{384,256},{1,385},{129,1},{257,129},{385... | collective-permute-start | bytes 688136 | tf_op jit(solution)/shard_map/ppermute | solution.py:29
  59.2 2.0 %collective-permute-done.4.rest_1_ = bf16[448,256]{1,0:T(8,128)(2,1)S(1)} collective-permute-done((bf16[448,256]{1,0:T(8,128)(2,1)}, bf16[448,256]{1,0:T(8,128)(2,1)S(1)}, u32[]{:S(2)}, u32[]{:S(2)}) %collective-permute-start.4) | collective-permute-done | bytes 229408 | tf_op jit(solution)/shard_map/ppermute | solution.py:29
  61.1 2.2 %collective-permute-done.5.rest_3_ = bf16[448,256]{1,0:T(8,128)(2,1)S(1)} collective-permute-done((bf16[448,256]{1,0:T(8,128)(2,1)}, bf16[448,256]{1,0:T(8,128)(2,1)S(1)}, u32[]{:S(2)}, u32[]{:S(2)}) %collective-permute-start.5) | collective-permute-done | bytes 229408 | tf_op jit(solution)/shard_map/ppermute | solution.py:29
  63.3 0.0 collective-permute-done.3.rest_2_
  63.3 0.0 all-to-all-done.2.parts_ref
  63.3 0.8 carried_and_squares.1
  64.1 7.1 %all-to-all-start.3 = ((bf16[4,136,256]{2,1,0:T(8,128)(2,1)}), bf16[4,136,256]{2,1,0:T(8,128)(2,1)S(1)}, u32[]{:S(2)}, u32[]{:S(2)}) async-start(bf16[4,136,256]{2,1,0:T(8,128)(2,1)} %carried_and_squares.1), calls=%async_computation.3 | async-start | bytes 557056 | tf_op jit(solution)/shard_map/all_to_all | solution.py:17
  71.2 7.2 %collective-permute-start.6 = (bf16[448,256]{1,0:T(8,128)(2,1)S(1)}, bf16[448,256]{1,0:T(8,128)(2,1)S(1)}, u32[]{:S(2)}, u32[]{:S(2)}) collective-permute-start(bf16[448,256]{1,0:T(8,128)(2,1)S(1)} %get-tuple-element.40), channel_id=1, source_target_pairs={{0,256},{128,384},{256,0},{384,128},{1,257},{129,385},{257,1},{385... | collective-permute-start | bytes 688136 | tf_op jit(solution)/shard_map/ppermute | solution.py:29
  78.4 3.8 %collective-permute-done.6.rest_2_ = bf16[448,256]{1,0:T(8,128)(2,1)S(1)} collective-permute-done((bf16[448,256]{1,0:T(8,128)(2,1)S(1)}, bf16[448,256]{1,0:T(8,128)(2,1)S(1)}, u32[]{:S(2)}, u32[]{:S(2)}) %collective-permute-start.6) | collective-permute-done | bytes 229408 | tf_op jit(solution)/shard_map/ppermute | solution.py:29
  82.2 0.7 copy-done.5
  82.8 0.0 all-to-all-done.3
  82.8 0.1 broadcast_in_dim.2
  82.9 16.4 %all_to_all.45 = bf16[4,4,136,256]{3,2,1,0:T(8,128)(2,1)S(1)} all-to-all(bf16[4,4,136,256]{3,2,1,0:T(8,128)(2,1)S(1)} %broadcast_in_dim.2), channel_id=1, replica_groups=mesh['x'=4,'zl'=4,'core'=2,'y'=4,'zh'=4] {'x'}, dimensions={0} | all-to-all | bytes 2228224 | tf_op jit(solution)/shard_map/all_to_all | solution.py:17
  99.3 6.2 %collective-permute-start.7 = (bf16[16,136,256]{2,1,0:T(8,128)(2,1)S(1)}, bf16[16,136,256]{2,1,0:T(8,128)(2,1)}, u32[]{:S(2)}, u32[]{:S(2)}) collective-permute-start(bf16[16,136,256]{2,1,0:T(8,128)(2,1)S(1)} %bitcast.20), channel_id=1, source_target_pairs={{0,16},{16,0},{1,17},{17,1},{2,18},{18,2},{3,19},{19,3},{4,20},{20... | collective-permute-start | bytes 3342344 | tf_op jit(solution)/shard_map/ppermute | solution.py:25
  105.5 0.1 pad_add_fusion.1.at_ref
  105.6 1.4 gate_up.1
  107.0 1.0 collective-permute-done.7.spread_ref
  108.0 2.1 %gate_up_both.1 = (bf16[4,120,512]{2,1,0:T(8,128)(2,1)S(1)}, bf16[128,512]{1,0:T(8,128)(2,1)S(1)}) custom-call(s32[3]{0:T(128)S(1)} %pad_add_fusion.1.at_ref, bf16[16,136,256]{2,1,0:T(8,128)(2,1)} %collective-permute-done.7.spread_ref, bf16[112,2048]{1,0:T(8,128)(2,1)S(1)} %get-tuple-element.42.rest_0_, ...), custom_call_target="tpu_custom_call" | custom-call | tf_op jit(solution)/shard_map/gate_up_both/pallas_call | solution.py:311
  110.1 11.0 %all_to_all.46.parts_ref = bf16[4,120,512]{2,1,0:T(8,128)(2,1)S(1)} all-to-all(bf16[4,120,512]{2,1,0:T(8,128)(2,1)S(1)} %get-tuple-element.48), channel_id=1, replica_groups=mesh['x'=4,'zl'=4,'core'=2,'y'=4,'zh'=4] {'y'}, dimensions={0} | all-to-all | bytes 983040 | tf_op jit(solution)/shard_map/all_to_all | solution.py:17
  121.1 0.8 activate.1
  121.9 4.2 %all-to-all-start.6 = ((bf16[4,56,512]{2,1,0:T(8,128)(2,1)}), bf16[4,56,512]{2,1,0:T(8,128)(2,1)S(1)}, u32[]{:S(2)}, u32[]{:S(2)}) async-start(bf16[4,56,512]{2,1,0:T(8,128)(2,1)} %activate.1), calls=%async_computation.6 | async-start | bytes 458752 | tf_op jit(solution)/shard_map/all_to_all | solution.py:17
  126.1 0.1 pad_add_fusion.at_ref
  126.2 5.3 %all-to-all-done.6 = bf16[4,56,512]{2,1,0:T(8,128)(2,1)S(1)} async-done(((bf16[4,56,512]{2,1,0:T(8,128)(2,1)}), bf16[4,56,512]{2,1,0:T(8,128)(2,1)S(1)}, u32[]{:S(2)}, u32[]{:S(2)}) %all-to-all-start.6) | async-done | bytes 229408 | tf_op jit(solution)/shard_map/all_to_all | solution.py:17
  131.5 5.2 %all-gather = bf16[8,56,512]{2,1,0:T(8,128)(2,1)S(1)} all-gather(bf16[4,56,512]{2,1,0:T(8,128)(2,1)S(1)} %all-to-all-done.6), channel_id=2, replica_groups=mesh['x'=4,'zl'=4,'core'=2,'y'=4,'zh'=4] {'core'}, dimensions={0}, use_global_device_ids=true | all-gather | bytes 688128 | tf_op jit(solution)/shard_map/all_gather | solution.py:377
  136.7 1.3 down.1
  138.0 18.6 %all_to_all.47.parts_ref = bf16[16,32,1024]{2,1,0:T(8,128)(2,1)S(1)} all-to-all(bf16[16,32,1024]{2,1,0:T(8,128)(2,1)S(1)} %down.1), channel_id=1, replica_groups=mesh['x'=4,'zl'=4,'core'=2,'y'=4,'zh'=4] {'x','y'}, dimensions={0} | all-to-all | bytes 2097152 | tf_op jit(solution)/shard_map/all_to_all | solution.py:17
  156.7 0.1 sum_and_replicate.3
  156.8 21.9 %all_to_all.48.parts_ref = bf16[32,8,128]{2,1,0:T(8,128)(2,1)S(1)} all-to-all(bf16[32,8,128]{2,1,0:T(8,128)(2,1)S(1)} %bitcast.26), channel_id=1, replica_groups=mesh['x'=4,'zl'=4,'core'=2,'y'=4,'zh'=4] {'core','zl','zh'}, dimensions={0} | all-to-all | bytes 131072 | tf_op jit(solution)/shard_map/all_to_all | solution.py:17
  178.7 0.6 sum_to_row.1
  (20 shorter events, 0.0 us)
Async XLA Ops:
  0.0 10.7 %copy-start.2 = (bf16[512,256]{1,0:T(8,128)(2,1)S(1)}, bf16[512,256]{1,0:T(8,128)(2,1)}, u32[]{:S(2)}) copy-start(bf16[512,256]{1,0:T(8,128)(2,1)} %own_ref.1) | copy-start | bytes 786436
  0.0 14.0 %copy-start = (bf16[56,8192]{1,0:T(8,128)(2,1)S(1)}, bf16[56,8192]{1,0:T(8,128)(2,1)}, u32[]{:S(2)}) copy-start(bf16[56,8192]{1,0:T(8,128)(2,1)} %gate_ref.1) | copy-start | bytes 2752516
  0.0 14.1 %copy-start.7 = (f32[8192]{0:T(1024)S(1)}, f32[8192]{0:T(1024)}, u32[]{:S(2)}) copy-start(f32[8192]{0:T(1024)} %param.10) | copy-start | bytes 98308
  1.7 22.1 %all-to-all-start = ((bf16[16,24,512]{2,1,0:T(8,128)(2,1)}), bf16[16,24,512]{2,1,0:T(8,128)(2,1)S(1)}, u32[]{:S(2)}, u32[]{:S(2)}) async-start(bf16[16,24,512]{2,1,0:T(8,128)(2,1)} %pack_rows.1), calls=%async_computation | async-start | bytes 786432 | tf_op jit(solution)/shard_map/all_to_all | solution.py:17
  10.7 13.1 %collective-permute-start = (bf16[512,256]{1,0:T(8,128)(2,1)S(1)}, bf16[512,256]{1,0:T(8,128)(2,1)S(1)}, u32[]{:S(2)}, u32[]{:S(2)}) collective-permute-start(bf16[512,256]{1,0:T(8,128)(2,1)S(1)} %copy-done.2), channel_id=1, source_target_pairs={{0,16},{16,0},{1,17},{17,1},{2,18},{18,2},{3,19},{19,3},{4,20},{20... | collective-permute-start | bytes 786440 | tf_op jit(solution)/shard_map/ppermute | solution.py:25
  14.1 1.2 copy-start.1
  16.5 0.8 copy-start.8
  17.2 18.6 %collective-permute-start.1 = (bf16[112,2048]{1,0:T(8,128)(2,1)}, bf16[112,2048]{1,0:T(8,128)(2,1)S(1)}, u32[]{:S(2)}, u32[]{:S(2)}) collective-permute-start(bf16[112,2048]{1,0:T(8,128)(2,1)} %get-tuple-element.29), channel_id=1, source_target_pairs={{0,4},{4,8},{8,12},{12,0},{1,5},{5,9},{9,13},{13,1},{2,6},{6,10},{... | collective-permute-start | bytes 1376264 | tf_op jit(solution)/shard_map/ppermute | solution.py:29
  20.0 15.9 %collective-permute-start.2 = (bf16[112,2048]{1,0:T(8,128)(2,1)S(1)}, bf16[112,2048]{1,0:T(8,128)(2,1)S(1)}, u32[]{:S(2)}, u32[]{:S(2)}) collective-permute-start(bf16[112,2048]{1,0:T(8,128)(2,1)S(1)} %get-tuple-element.30), channel_id=1, source_target_pairs={{0,12},{4,0},{8,4},{12,8},{1,13},{5,1},{9,5},{13,9},{2,14},{6,2},{... | collective-permute-start | bytes 1376264 | tf_op jit(solution)/shard_map/ppermute | solution.py:29
  25.5 9.6 %all-to-all-start.1 = ((bf16[4,128,256]{2,1,0:T(8,128)(2,1)}), bf16[4,128,256]{2,1,0:T(8,128)(2,1)S(1)}, u32[]{:S(2)}, u32[]{:S(2)}) async-start(bf16[4,128,256]{2,1,0:T(8,128)(2,1)} %project.1), calls=%async_computation.1 | async-start | bytes 524288 | tf_op jit(solution)/shard_map/all_to_all | solution.py:17
  29.5 18.4 %copy-start.9 = (bf16[112,2048]{1,0:T(8,128)(2,1)S(1)}, bf16[112,2048]{1,0:T(8,128)(2,1)}, u32[]{:S(2)}) copy-start(bf16[112,2048]{1,0:T(8,128)(2,1)} %copy-done.8) | copy-start | bytes 1376260
  35.8 27.5 %all-to-all-start.2 = ((bf16[4,128,256]{2,1,0:T(8,128)(2,1)}), bf16[4,128,256]{2,1,0:T(8,128)(2,1)S(1)}, u32[]{:S(2)}, u32[]{:S(2)}) async-start(bf16[4,128,256]{2,1,0:T(8,128)(2,1)} %sum_and_replicate.2), calls=%async_computation.2 | async-start | bytes 524288 | tf_op jit(solution)/shard_map/all_to_all | solution.py:17
  47.9 15.4 %collective-permute-start.3 = (bf16[112,2048]{1,0:T(8,128)(2,1)S(1)}, bf16[112,2048]{1,0:T(8,128)(2,1)S(1)}, u32[]{:S(2)}, u32[]{:S(2)}) collective-permute-start(bf16[112,2048]{1,0:T(8,128)(2,1)S(1)} %copy-done.9), channel_id=1, source_target_pairs={{0,8},{4,12},{8,0},{12,4},{1,9},{5,13},{9,1},{13,5},{2,10},{6,14},... | collective-permute-start | bytes 1376264 | tf_op jit(solution)/shard_map/ppermute | solution.py:29
  52.5 8.7 %collective-permute-start.4 = (bf16[448,256]{1,0:T(8,128)(2,1)}, bf16[448,256]{1,0:T(8,128)(2,1)S(1)}, u32[]{:S(2)}, u32[]{:S(2)}) collective-permute-start(bf16[448,256]{1,0:T(8,128)(2,1)} %get-tuple-element.35), channel_id=1, source_target_pairs={{0,128},{128,256},{256,384},{384,0},{1,129},{129,257},{257,385},{3... | collective-permute-start | bytes 688136 | tf_op jit(solution)/shard_map/ppermute | solution.py:29
  56.0 7.3 %collective-permute-start.5 = (bf16[448,256]{1,0:T(8,128)(2,1)}, bf16[448,256]{1,0:T(8,128)(2,1)S(1)}, u32[]{:S(2)}, u32[]{:S(2)}) collective-permute-start(bf16[448,256]{1,0:T(8,128)(2,1)} %get-tuple-element.36), channel_id=1, source_target_pairs={{0,384},{128,0},{256,128},{384,256},{1,385},{129,1},{257,129},{385... | collective-permute-start | bytes 688136 | tf_op jit(solution)/shard_map/ppermute | solution.py:29
  63.3 19.6 %copy-start.3 = (bf16[448,256]{1,0:T(8,128)(2,1)}, bf16[448,256]{1,0:T(8,128)(2,1)S(1)}, u32[]{:S(2)}) copy-start(bf16[448,256]{1,0:T(8,128)(2,1)S(1)} %collective-permute-done.5.rest_3_) | copy-start | bytes 688132
  64.1 18.8 %all-to-all-start.3 = ((bf16[4,136,256]{2,1,0:T(8,128)(2,1)}), bf16[4,136,256]{2,1,0:T(8,128)(2,1)S(1)}, u32[]{:S(2)}, u32[]{:S(2)}) async-start(bf16[4,136,256]{2,1,0:T(8,128)(2,1)} %carried_and_squares.1), calls=%async_computation.3 | async-start | bytes 557056 | tf_op jit(solution)/shard_map/all_to_all | solution.py:17
  71.2 11.0 %collective-permute-start.6 = (bf16[448,256]{1,0:T(8,128)(2,1)S(1)}, bf16[448,256]{1,0:T(8,128)(2,1)S(1)}, u32[]{:S(2)}, u32[]{:S(2)}) collective-permute-start(bf16[448,256]{1,0:T(8,128)(2,1)S(1)} %get-tuple-element.40), channel_id=1, source_target_pairs={{0,256},{128,384},{256,0},{384,128},{1,257},{129,385},{257,1},{385... | collective-permute-start | bytes 688136 | tf_op jit(solution)/shard_map/ppermute | solution.py:29
  82.2 0.7 copy-start.5
  99.3 8.7 %collective-permute-start.7 = (bf16[16,136,256]{2,1,0:T(8,128)(2,1)S(1)}, bf16[16,136,256]{2,1,0:T(8,128)(2,1)}, u32[]{:S(2)}, u32[]{:S(2)}) collective-permute-start(bf16[16,136,256]{2,1,0:T(8,128)(2,1)S(1)} %bitcast.20), channel_id=1, source_target_pairs={{0,16},{16,0},{1,17},{17,1},{2,18},{18,2},{3,19},{19,3},{4,20},{20... | collective-permute-start | bytes 3342344 | tf_op jit(solution)/shard_map/ppermute | solution.py:25
  121.1 15.6 %copy-start.4 = (bf16[448,256]{1,0:T(8,128)(2,1)S(1)}, bf16[448,256]{1,0:T(8,128)(2,1)}, u32[]{:S(2)}) copy-start(bf16[448,256]{1,0:T(8,128)(2,1)} %copy-done.3) | copy-start | bytes 688132
  121.1 15.6 %copy-start.6 = (bf16[448,256]{1,0:T(8,128)(2,1)S(1)}, bf16[448,256]{1,0:T(8,128)(2,1)}, u32[]{:S(2)}) copy-start(bf16[448,256]{1,0:T(8,128)(2,1)} %copy-done.5) | copy-start | bytes 688132
  121.9 9.6 %all-to-all-start.6 = ((bf16[4,56,512]{2,1,0:T(8,128)(2,1)}), bf16[4,56,512]{2,1,0:T(8,128)(2,1)S(1)}, u32[]{:S(2)}, u32[]{:S(2)}) async-start(bf16[4,56,512]{2,1,0:T(8,128)(2,1)} %activate.1), calls=%async_computation.6 | async-start | bytes 458752 | tf_op jit(solution)/shard_map/all_to_all | solution.py:17

commit v8 on v7

--- a/solution.py
+++ b/solution.py
@@ -173,6 +173,25 @@
     )(at, hidden, kept, *pieces)
 
 
+def sum_by_token(parts):
+    pieces, rows, width = parts.shape
+
+    def kernel(parts_ref, out_ref):
+        total = parts_ref[0].astype(F32)
+        for piece in range(1, pieces):
+            total = total + parts_ref[piece].astype(F32)
+        out_ref[...] = total.reshape(rows, width // 128, 128).astype(BF16)
+
+    return pl.pallas_call(
+        kernel,
+        out_shape=jax.ShapeDtypeStruct((rows, width // 128, 128), BF16),
+        in_specs=[vmem()],
+        out_specs=vmem(),
+        compiler_params=pltpu.CompilerParams(vmem_limit_bytes=4 * 1024 * 1024),
+        name="sum_by_token",
+    )(parts)
+
+
 def sum_to_row(parts, d):
     _, rows, lanes = parts.shape
     per_x = rows // X
@@ -381,8 +400,7 @@
         kept,
         jnp.stack([x_at, y_at, core_at, zh_at]),
     )
-    near = sum_and_replicate(exchange(by_owner, ("x", "y")), 1)
-    near = near.reshape(CORES * ZL * ZH, X * cols // 128, 128)
+    near = sum_by_token(exchange(by_owner, ("x", "y")))
     final = exchange(near, ("core", "zl", "zh"))
     return sum_to_row(final, d)
 

time: 180 us -> 180 us (level)
  no operation moved by 1% of the time
where the time goes in v8:
time: 180 us; the launch traced here: 179 us
  blocking collectives  73 us (41%)
  starting transfers between devices  70.9 us (39%)
  waiting for transfers between devices  17.7 us (10%)
  Pallas kernels  12.5 us (7%)
  local copies, waits for them, and re-layouts  4.87 us (3%)
    all_to_all x4, blocking collectives, exchange(): return lax.all_to_all(value, axes, 0, 0, tiled=True)  67.9 us
    all_to_all x5, starting transfers between devices, exchange(): return lax.all_to_all(value, axes, 0, 0, tiled=True)  36.4 us
    ppermute x6, starting transfers between devices, shift_along(): return lax.ppermute(value, axis, [(i, (i + shift) % 4) for i in range(4)])  24.9 us
    ppermute x2, starting transfers between devices, swap_cores(): return lax.ppermute(value, 'core', [(0, 1), (1, 0)])  9.56 us
    all_to_all x5, waiting for transfers between devices, exchange(): return lax.all_to_all(value, axes, 0, 0, tiled=True)  8.75 us
    ppermute x6, waiting for transfers between devices, shift_along(): return lax.ppermute(value, axis, [(i, (i + shift) % 4) for i in range(4)])  7.91 us
    all_gather x1, blocking collectives, shards(): hidden = lax.all_gather(hidden, 'core', axis=0, tiled=False)  5.15 us
  transfers between devices with their start and end apart: 13, of which 6 were waited for; matrix products, arithmetic and copies ran while one was open for 1% of the time, Pallas kernels for 3%

profile of v8, /device:TPU:1, one launch (start us, length us, event | category | flops | bytes accessed | tf_op | source)
XLA Modules:
  0.0 179.4 jit_solution(16815563510448275471)
XLA Ops:
  0.0 1.7 pack_rows.1
  1.7 9.0 %all-to-all-start = ((bf16[16,24,512]{2,1,0:T(8,128)(2,1)}), bf16[16,24,512]{2,1,0:T(8,128)(2,1)S(1)}, u32[]{:S(2)}, u32[]{:S(2)}) async-start(bf16[16,24,512]{2,1,0:T(8,128)(2,1)} %pack_rows.1), calls=%async_computation | async-start | bytes 786432 | tf_op jit(solution)/shard_map/all_to_all | solution.py:17
  10.7 3.3 %collective-permute-start = (bf16[512,256]{1,0:T(8,128)(2,1)S(1)}, bf16[512,256]{1,0:T(8,128)(2,1)S(1)}, u32[]{:S(2)}, u32[]{:S(2)}) collective-permute-start(bf16[512,256]{1,0:T(8,128)(2,1)S(1)} %copy-done.2), channel_id=1, source_target_pairs={{0,16},{16,0},{1,17},{17,1},{2,18},{18,2},{3,19},{19,3},{4,20},{20... | collective-permute-start | bytes 786440 | tf_op jit(solution)/shard_map/ppermute | solution.py:25
  14.1 0.0 copy-start.1
  14.1 1.2 copy-done.1
  15.3 1.2 cut_weights.1
  16.5 0.8 copy-done.8
  17.2 2.7 %collective-permute-start.1 = (bf16[112,2048]{1,0:T(8,128)(2,1)}, bf16[112,2048]{1,0:T(8,128)(2,1)S(1)}, u32[]{:S(2)}, u32[]{:S(2)}) collective-permute-start(bf16[112,2048]{1,0:T(8,128)(2,1)} %get-tuple-element.29), channel_id=1, source_target_pairs={{0,4},{4,8},{8,12},{12,0},{1,5},{5,9},{9,13},{13,1},{2,6},{6,10},{... | collective-permute-start | bytes 1376264 | tf_op jit(solution)/shard_map/ppermute | solution.py:29
  20.0 3.7 %collective-permute-start.2 = (bf16[112,2048]{1,0:T(8,128)(2,1)S(1)}, bf16[112,2048]{1,0:T(8,128)(2,1)S(1)}, u32[]{:S(2)}, u32[]{:S(2)}) collective-permute-start(bf16[112,2048]{1,0:T(8,128)(2,1)S(1)} %get-tuple-element.30), channel_id=1, source_target_pairs={{0,12},{4,0},{8,4},{12,8},{1,13},{5,1},{9,5},{13,9},{2,14},{6,2},{... | collective-permute-start | bytes 1376264 | tf_op jit(solution)/shard_map/ppermute | solution.py:29
  23.7 0.1 pad_add_fusion.2.at_ref
  23.8 0.0 all-to-all-done.got_ref
  23.8 1.7 project.1
  25.5 4.0 %all-to-all-start.1 = ((bf16[4,128,256]{2,1,0:T(8,128)(2,1)}), bf16[4,128,256]{2,1,0:T(8,128)(2,1)S(1)}, u32[]{:S(2)}, u32[]{:S(2)}) async-start(bf16[4,128,256]{2,1,0:T(8,128)(2,1)} %project.1), calls=%async_computation.1 | async-start | bytes 524288 | tf_op jit(solution)/shard_map/all_to_all | solution.py:17
  29.5 2.1 %dynamic-slice_bitcast_fusion = (bf16[448,256]{1,0:T(8,128)(2,1)}, bf16[448,256]{1,0:T(8,128)(2,1)S(1)}, bf16[448,256]{1,0:T(8,128)(2,1)}, bf16[448,256]{1,0:T(8,128)(2,1)S(1)}) fusion(bf16[4,448,256]{2,1,0:T(8,128)(2,1)} %bitcast.21, s32[]{:T(128)S(6)} %select_n.39, s32[]{:T(128)S(6)} %select_n.37, s32[]{:T(128)S(6)} %select_n.35, s32[]{:T(128)S(6)} %select_n.33), kind=kLoop, calls=%fused_computation | loop fusion | bytes 1835024 | tf_op jit(solution)/shard_map/jit(dynamic_index_in_dim)/squeeze | solution.py:366
  31.7 3.4 %all-to-all-done.1.parts_ref = bf16[4,128,256]{2,1,0:T(8,128)(2,1)S(1)} async-done(((bf16[4,128,256]{2,1,0:T(8,128)(2,1)}), bf16[4,128,256]{2,1,0:T(8,128)(2,1)S(1)}, u32[]{:S(2)}, u32[]{:S(2)}) %all-to-all-start.1) | async-done | bytes 262176 | tf_op jit(solution)/shard_map/all_to_all | solution.py:17
  35.1 0.7 sum_and_replicate.1
  35.8 12.1 %all-to-all-start.2 = ((bf16[4,128,256]{2,1,0:T(8,128)(2,1)}), bf16[4,128,256]{2,1,0:T(8,128)(2,1)S(1)}, u32[]{:S(2)}, u32[]{:S(2)}) async-start(bf16[4,128,256]{2,1,0:T(8,128)(2,1)} %sum_and_replicate.1), calls=%async_computation.2 | async-start | bytes 524288 | tf_op jit(solution)/shard_map/all_to_all | solution.py:17
  47.9 4.5 %collective-permute-start.3 = (bf16[112,2048]{1,0:T(8,128)(2,1)S(1)}, bf16[112,2048]{1,0:T(8,128)(2,1)S(1)}, u32[]{:S(2)}, u32[]{:S(2)}) collective-permute-start(bf16[112,2048]{1,0:T(8,128)(2,1)S(1)} %copy-done.9), channel_id=1, source_target_pairs={{0,8},{4,12},{8,0},{12,4},{1,9},{5,13},{9,1},{13,5},{2,10},{6,14},... | collective-permute-start | bytes 1376264 | tf_op jit(solution)/shard_map/ppermute | solution.py:29
  52.5 3.6 %collective-permute-start.4 = (bf16[448,256]{1,0:T(8,128)(2,1)}, bf16[448,256]{1,0:T(8,128)(2,1)S(1)}, u32[]{:S(2)}, u32[]{:S(2)}) collective-permute-start(bf16[448,256]{1,0:T(8,128)(2,1)} %get-tuple-element.35), channel_id=1, source_target_pairs={{0,128},{128,256},{256,384},{384,0},{1,129},{129,257},{257,385},{3... | collective-permute-start | bytes 688136 | tf_op jit(solution)/shard_map/ppermute | solution.py:29
  56.0 3.1 %collective-permute-start.5 = (bf16[448,256]{1,0:T(8,128)(2,1)}, bf16[448,256]{1,0:T(8,128)(2,1)S(1)}, u32[]{:S(2)}, u32[]{:S(2)}) collective-permute-start(bf16[448,256]{1,0:T(8,128)(2,1)} %get-tuple-element.36), channel_id=1, source_target_pairs={{0,384},{128,0},{256,128},{384,256},{1,385},{129,1},{257,129},{385... | collective-permute-start | bytes 688136 | tf_op jit(solution)/shard_map/ppermute | solution.py:29
  59.2 2.0 %collective-permute-done.4.rest_1_ = bf16[448,256]{1,0:T(8,128)(2,1)S(1)} collective-permute-done((bf16[448,256]{1,0:T(8,128)(2,1)}, bf16[448,256]{1,0:T(8,128)(2,1)S(1)}, u32[]{:S(2)}, u32[]{:S(2)}) %collective-permute-start.4) | collective-permute-done | bytes 229408 | tf_op jit(solution)/shard_map/ppermute | solution.py:29
  61.1 2.2 %collective-permute-done.5.rest_3_ = bf16[448,256]{1,0:T(8,128)(2,1)S(1)} collective-permute-done((bf16[448,256]{1,0:T(8,128)(2,1)}, bf16[448,256]{1,0:T(8,128)(2,1)S(1)}, u32[]{:S(2)}, u32[]{:S(2)}) %collective-permute-start.5) | collective-permute-done | bytes 229408 | tf_op jit(solution)/shard_map/ppermute | solution.py:29
  63.3 0.0 collective-permute-done.3.rest_2_
  63.3 0.0 all-to-all-done.2.parts_ref
  63.3 0.8 carried_and_squares.1
  64.1 7.1 %all-to-all-start.3 = ((bf16[4,136,256]{2,1,0:T(8,128)(2,1)}), bf16[4,136,256]{2,1,0:T(8,128)(2,1)S(1)}, u32[]{:S(2)}, u32[]{:S(2)}) async-start(bf16[4,136,256]{2,1,0:T(8,128)(2,1)} %carried_and_squares.1), calls=%async_computation.3 | async-start | bytes 557056 | tf_op jit(solution)/shard_map/all_to_all | solution.py:17
  71.2 7.2 %collective-permute-start.6 = (bf16[448,256]{1,0:T(8,128)(2,1)S(1)}, bf16[448,256]{1,0:T(8,128)(2,1)S(1)}, u32[]{:S(2)}, u32[]{:S(2)}) collective-permute-start(bf16[448,256]{1,0:T(8,128)(2,1)S(1)} %get-tuple-element.40), channel_id=1, source_target_pairs={{0,256},{128,384},{256,0},{384,128},{1,257},{129,385},{257,1},{385... | collective-permute-start | bytes 688136 | tf_op jit(solution)/shard_map/ppermute | solution.py:29
  78.4 3.8 %collective-permute-done.6.rest_2_ = bf16[448,256]{1,0:T(8,128)(2,1)S(1)} collective-permute-done((bf16[448,256]{1,0:T(8,128)(2,1)S(1)}, bf16[448,256]{1,0:T(8,128)(2,1)S(1)}, u32[]{:S(2)}, u32[]{:S(2)}) %collective-permute-start.6) | collective-permute-done | bytes 229408 | tf_op jit(solution)/shard_map/ppermute | solution.py:29
  82.2 0.7 copy-done.5
  82.8 0.0 all-to-all-done.3
  82.8 0.1 broadcast_in_dim.2
  82.9 16.4 %all_to_all.45 = bf16[4,4,136,256]{3,2,1,0:T(8,128)(2,1)S(1)} all-to-all(bf16[4,4,136,256]{3,2,1,0:T(8,128)(2,1)S(1)} %broadcast_in_dim.2), channel_id=1, replica_groups=mesh['x'=4,'zl'=4,'core'=2,'y'=4,'zh'=4] {'x'}, dimensions={0} | all-to-all | bytes 2228224 | tf_op jit(solution)/shard_map/all_to_all | solution.py:17
  99.3 6.2 %collective-permute-start.7 = (bf16[16,136,256]{2,1,0:T(8,128)(2,1)S(1)}, bf16[16,136,256]{2,1,0:T(8,128)(2,1)}, u32[]{:S(2)}, u32[]{:S(2)}) collective-permute-start(bf16[16,136,256]{2,1,0:T(8,128)(2,1)S(1)} %bitcast.17), channel_id=1, source_target_pairs={{0,16},{16,0},{1,17},{17,1},{2,18},{18,2},{3,19},{19,3},{4,20},{20... | collective-permute-start | bytes 3342344 | tf_op jit(solution)/shard_map/ppermute | solution.py:25
  105.5 0.1 pad_add_fusion.1.at_ref
  105.6 1.4 gate_up.1
  107.0 1.0 collective-permute-done.7.spread_ref
  108.0 2.1 %gate_up_both.1 = (bf16[4,120,512]{2,1,0:T(8,128)(2,1)S(1)}, bf16[128,512]{1,0:T(8,128)(2,1)S(1)}) custom-call(s32[3]{0:T(128)S(1)} %pad_add_fusion.1.at_ref, bf16[16,136,256]{2,1,0:T(8,128)(2,1)} %collective-permute-done.7.spread_ref, bf16[112,2048]{1,0:T(8,128)(2,1)S(1)} %get-tuple-element.42.rest_0_, ...), custom_call_target="tpu_custom_call" | custom-call | tf_op jit(solution)/shard_map/gate_up_both/pallas_call | solution.py:330
  110.1 11.0 %all_to_all.46.parts_ref = bf16[4,120,512]{2,1,0:T(8,128)(2,1)S(1)} all-to-all(bf16[4,120,512]{2,1,0:T(8,128)(2,1)S(1)} %get-tuple-element.48), channel_id=1, replica_groups=mesh['x'=4,'zl'=4,'core'=2,'y'=4,'zh'=4] {'y'}, dimensions={0} | all-to-all | bytes 983040 | tf_op jit(solution)/shard_map/all_to_all | solution.py:17
  121.1 0.8 activate.1
  121.9 4.2 %all-to-all-start.6 = ((bf16[4,56,512]{2,1,0:T(8,128)(2,1)}), bf16[4,56,512]{2,1,0:T(8,128)(2,1)S(1)}, u32[]{:S(2)}, u32[]{:S(2)}) async-start(bf16[4,56,512]{2,1,0:T(8,128)(2,1)} %activate.1), calls=%async_computation.6 | async-start | bytes 458752 | tf_op jit(solution)/shard_map/all_to_all | solution.py:17
  126.2 0.1 pad_add_fusion.at_ref
  126.2 5.3 %all-to-all-done.6 = bf16[4,56,512]{2,1,0:T(8,128)(2,1)S(1)} async-done(((bf16[4,56,512]{2,1,0:T(8,128)(2,1)}), bf16[4,56,512]{2,1,0:T(8,128)(2,1)S(1)}, u32[]{:S(2)}, u32[]{:S(2)}) %all-to-all-start.6) | async-done | bytes 229408 | tf_op jit(solution)/shard_map/all_to_all | solution.py:17
  131.5 5.2 %all-gather = bf16[8,56,512]{2,1,0:T(8,128)(2,1)S(1)} all-gather(bf16[4,56,512]{2,1,0:T(8,128)(2,1)S(1)} %all-to-all-done.6), channel_id=2, replica_groups=mesh['x'=4,'zl'=4,'core'=2,'y'=4,'zh'=4] {'core'}, dimensions={0}, use_global_device_ids=true | all-gather | bytes 688128 | tf_op jit(solution)/shard_map/all_gather | solution.py:396
  136.7 1.3 down.1
  138.0 18.6 %all_to_all.47.parts_ref = bf16[16,32,1024]{2,1,0:T(8,128)(2,1)S(1)} all-to-all(bf16[16,32,1024]{2,1,0:T(8,128)(2,1)S(1)} %down.1), channel_id=1, replica_groups=mesh['x'=4,'zl'=4,'core'=2,'y'=4,'zh'=4] {'x','y'}, dimensions={0} | all-to-all | bytes 2097152 | tf_op jit(solution)/shard_map/all_to_all | solution.py:17
  156.7 0.2 sum_by_token.1
  156.8 21.9 %all_to_all.48.parts_ref = bf16[32,8,128]{2,1,0:T(8,128)(2,1)S(1)} all-to-all(bf16[32,8,128]{2,1,0:T(8,128)(2,1)S(1)} %sum_by_token.1), channel_id=1, replica_groups=mesh['x'=4,'zl'=4,'core'=2,'y'=4,'zh'=4] {'core','zl','zh'}, dimensions={0} | all-to-all | bytes 131072 | tf_op jit(solution)/shard_map/all_to_all | solution.py:17
  178.7 0.6 sum_to_row.1
  (19 shorter events, 0.0 us)
Async XLA Ops:
  0.0 10.7 %copy-start.2 = (bf16[512,256]{1,0:T(8,128)(2,1)S(1)}, bf16[512,256]{1,0:T(8,128)(2,1)}, u32[]{:S(2)}) copy-start(bf16[512,256]{1,0:T(8,128)(2,1)} %own_ref.1) | copy-start | bytes 786436
  0.0 14.0 %copy-start = (bf16[56,8192]{1,0:T(8,128)(2,1)S(1)}, bf16[56,8192]{1,0:T(8,128)(2,1)}, u32[]{:S(2)}) copy-start(bf16[56,8192]{1,0:T(8,128)(2,1)} %gate_ref.1) | copy-start | bytes 2752516
  0.0 14.1 %copy-start.7 = (f32[8192]{0:T(1024)S(1)}, f32[8192]{0:T(1024)}, u32[]{:S(2)}) copy-start(f32[8192]{0:T(1024)} %param.10) | copy-start | bytes 98308
  1.7 22.1 %all-to-all-start = ((bf16[16,24,512]{2,1,0:T(8,128)(2,1)}), bf16[16,24,512]{2,1,0:T(8,128)(2,1)S(1)}, u32[]{:S(2)}, u32[]{:S(2)}) async-start(bf16[16,24,512]{2,1,0:T(8,128)(2,1)} %pack_rows.1), calls=%async_computation | async-start | bytes 786432 | tf_op jit(solution)/shard_map/all_to_all | solution.py:17
  10.7 13.1 %collective-permute-start = (bf16[512,256]{1,0:T(8,128)(2,1)S(1)}, bf16[512,256]{1,0:T(8,128)(2,1)S(1)}, u32[]{:S(2)}, u32[]{:S(2)}) collective-permute-start(bf16[512,256]{1,0:T(8,128)(2,1)S(1)} %copy-done.2), channel_id=1, source_target_pairs={{0,16},{16,0},{1,17},{17,1},{2,18},{18,2},{3,19},{19,3},{4,20},{20... | collective-permute-start | bytes 786440 | tf_op jit(solution)/shard_map/ppermute | solution.py:25
  14.1 1.2 copy-start.1
  16.5 0.8 copy-start.8
  17.2 18.6 %collective-permute-start.1 = (bf16[112,2048]{1,0:T(8,128)(2,1)}, bf16[112,2048]{1,0:T(8,128)(2,1)S(1)}, u32[]{:S(2)}, u32[]{:S(2)}) collective-permute-start(bf16[112,2048]{1,0:T(8,128)(2,1)} %get-tuple-element.29), channel_id=1, source_target_pairs={{0,4},{4,8},{8,12},{12,0},{1,5},{5,9},{9,13},{13,1},{2,6},{6,10},{... | collective-permute-start | bytes 1376264 | tf_op jit(solution)/shard_map/ppermute | solution.py:29
  20.0 15.9 %collective-permute-start.2 = (bf16[112,2048]{1,0:T(8,128)(2,1)S(1)}, bf16[112,2048]{1,0:T(8,128)(2,1)S(1)}, u32[]{:S(2)}, u32[]{:S(2)}) collective-permute-start(bf16[112,2048]{1,0:T(8,128)(2,1)S(1)} %get-tuple-element.30), channel_id=1, source_target_pairs={{0,12},{4,0},{8,4},{12,8},{1,13},{5,1},{9,5},{13,9},{2,14},{6,2},{... | collective-permute-start | bytes 1376264 | tf_op jit(solution)/shard_map/ppermute | solution.py:29
  25.5 9.6 %all-to-all-start.1 = ((bf16[4,128,256]{2,1,0:T(8,128)(2,1)}), bf16[4,128,256]{2,1,0:T(8,128)(2,1)S(1)}, u32[]{:S(2)}, u32[]{:S(2)}) async-start(bf16[4,128,256]{2,1,0:T(8,128)(2,1)} %project.1), calls=%async_computation.1 | async-start | bytes 524288 | tf_op jit(solution)/shard_map/all_to_all | solution.py:17
  29.5 18.4 %copy-start.9 = (bf16[112,2048]{1,0:T(8,128)(2,1)S(1)}, bf16[112,2048]{1,0:T(8,128)(2,1)}, u32[]{:S(2)}) copy-start(bf16[112,2048]{1,0:T(8,128)(2,1)} %copy-done.8) | copy-start | bytes 1376260
  35.8 27.5 %all-to-all-start.2 = ((bf16[4,128,256]{2,1,0:T(8,128)(2,1)}), bf16[4,128,256]{2,1,0:T(8,128)(2,1)S(1)}, u32[]{:S(2)}, u32[]{:S(2)}) async-start(bf16[4,128,256]{2,1,0:T(8,128)(2,1)} %sum_and_replicate.1), calls=%async_computation.2 | async-start | bytes 524288 | tf_op jit(solution)/shard_map/all_to_all | solution.py:17
  47.9 15.4 %collective-permute-start.3 = (bf16[112,2048]{1,0:T(8,128)(2,1)S(1)}, bf16[112,2048]{1,0:T(8,128)(2,1)S(1)}, u32[]{:S(2)}, u32[]{:S(2)}) collective-permute-start(bf16[112,2048]{1,0:T(8,128)(2,1)S(1)} %copy-done.9), channel_id=1, source_target_pairs={{0,8},{4,12},{8,0},{12,4},{1,9},{5,13},{9,1},{13,5},{2,10},{6,14},... | collective-permute-start | bytes 1376264 | tf_op jit(solution)/shard_map/ppermute | solution.py:29
  52.5 8.7 %collective-permute-start.4 = (bf16[448,256]{1,0:T(8,128)(2,1)}, bf16[448,256]{1,0:T(8,128)(2,1)S(1)}, u32[]{:S(2)}, u32[]{:S(2)}) collective-permute-start(bf16[448,256]{1,0:T(8,128)(2,1)} %get-tuple-element.35), channel_id=1, source_target_pairs={{0,128},{128,256},{256,384},{384,0},{1,129},{129,257},{257,385},{3... | collective-permute-start | bytes 688136 | tf_op jit(solution)/shard_map/ppermute | solution.py:29
  56.0 7.3 %collective-permute-start.5 = (bf16[448,256]{1,0:T(8,128)(2,1)}, bf16[448,256]{1,0:T(8,128)(2,1)S(1)}, u32[]{:S(2)}, u32[]{:S(2)}) collective-permute-start(bf16[448,256]{1,0:T(8,128)(2,1)} %get-tuple-element.36), channel_id=1, source_target_pairs={{0,384},{128,0},{256,128},{384,256},{1,385},{129,1},{257,129},{385... | collective-permute-start | bytes 688136 | tf_op jit(solution)/shard_map/ppermute | solution.py:29
  63.3 19.6 %copy-start.3 = (bf16[448,256]{1,0:T(8,128)(2,1)}, bf16[448,256]{1,0:T(8,128)(2,1)S(1)}, u32[]{:S(2)}) copy-start(bf16[448,256]{1,0:T(8,128)(2,1)S(1)} %collective-permute-done.5.rest_3_) | copy-start | bytes 688132
  64.1 18.8 %all-to-all-start.3 = ((bf16[4,136,256]{2,1,0:T(8,128)(2,1)}), bf16[4,136,256]{2,1,0:T(8,128)(2,1)S(1)}, u32[]{:S(2)}, u32[]{:S(2)}) async-start(bf16[4,136,256]{2,1,0:T(8,128)(2,1)} %carried_and_squares.1), calls=%async_computation.3 | async-start | bytes 557056 | tf_op jit(solution)/shard_map/all_to_all | solution.py:17
  71.2 11.0 %collective-permute-start.6 = (bf16[448,256]{1,0:T(8,128)(2,1)S(1)}, bf16[448,256]{1,0:T(8,128)(2,1)S(1)}, u32[]{:S(2)}, u32[]{:S(2)}) collective-permute-start(bf16[448,256]{1,0:T(8,128)(2,1)S(1)} %get-tuple-element.40), channel_id=1, source_target_pairs={{0,256},{128,384},{256,0},{384,128},{1,257},{129,385},{257,1},{385... | collective-permute-start | bytes 688136 | tf_op jit(solution)/shard_map/ppermute | solution.py:29
  82.2 0.7 copy-start.5
  99.3 8.7 %collective-permute-start.7 = (bf16[16,136,256]{2,1,0:T(8,128)(2,1)S(1)}, bf16[16,136,256]{2,1,0:T(8,128)(2,1)}, u32[]{:S(2)}, u32[]{:S(2)}) collective-permute-start(bf16[16,136,256]{2,1,0:T(8,128)(2,1)S(1)} %bitcast.17), channel_id=1, source_target_pairs={{0,16},{16,0},{1,17},{17,1},{2,18},{18,2},{3,19},{19,3},{4,20},{20... | collective-permute-start | bytes 3342344 | tf_op jit(solution)/shard_map/ppermute | solution.py:25
  121.1 15.6 %copy-start.4 = (bf16[448,256]{1,0:T(8,128)(2,1)S(1)}, bf16[448,256]{1,0:T(8,128)(2,1)}, u32[]{:S(2)}) copy-start(bf16[448,256]{1,0:T(8,128)(2,1)} %copy-done.3) | copy-start | bytes 688132
  121.1 15.6 %copy-start.6 = (bf16[448,256]{1,0:T(8,128)(2,1)S(1)}, bf16[448,256]{1,0:T(8,128)(2,1)}, u32[]{:S(2)}) copy-start(bf16[448,256]{1,0:T(8,128)(2,1)} %copy-done.5) | copy-start | bytes 688132
  121.9 9.6 %all-to-all-start.6 = ((bf16[4,56,512]{2,1,0:T(8,128)(2,1)}), bf16[4,56,512]{2,1,0:T(8,128)(2,1)S(1)}, u32[]{:S(2)}, u32[]{:S(2)}) async-start(bf16[4,56,512]{2,1,0:T(8,128)(2,1)} %activate.1), calls=%async_computation.6 | async-start | bytes 458752 | tf_op jit(solution)/shard_map/all_to_all | solution.py:17
